TPU v7x, 32 devices: a whole 2x2x4 slice. The times are simulated.
32 devices in a mesh: row: 4 (over z), mix: 8 (over y, x, core).
Axes of the slice: x: 2, y: 2, z: 4, core: 2. Of those that a mesh axis runs over, the one named last changes fastest.
Arguments:
- velocity: bfloat16 [64, 3, 8, 32, 128], P(None, None, 'mix', 'row'), may hold values from -6 to 6
- field_b: bfloat16 [64, 3, 8, 32, 128], P(None, None, 'mix', 'row'), may hold values from -6 to 6
- test_signs: int32 [384, 256], replicated, may hold values from 0 to 1
- row_signs: int32 [8, 32, 128], P('mix', 'row'), may hold values from 0 to 1
- sample_index: int32 [8, 4, 256], P('mix', 'row'), may hold values from 0 to 1023
Outputs:
- basis_rows: float32 [8, 4, 256, 256], P('mix', 'row')
- factor: float32 [256, 256], replicated
Inputs may be any that keep to these rules, and one draw needn't show every extreme that they name: test_signs entries are bits; the test matrix is 2 test_signs - 1. row_signs entries are bits; the sign is 2 row_signs - 1. `sample_index`: a point of the device's own block, p = x_local 128 + y; repeats may occur.
All inputs are finite; a program needn't handle non-finite values.
Results may differ from a plain program's by a relative error of at most 0.0021.
Values may be sent and summed in bfloat16 or wider, within the bound.
No kernel may reach another device: no remote copies, remote signals or barrier semaphores. Data moves between devices by JAX's collectives and lax.ppermute only.
A program may use at most 64 MiB of HBM per device.

v0:
```python
import math

import jax
import jax.numpy as jnp
from jax import lax
from jax.sharding import PartitionSpec as P


def swapped(block, axis, distance):
    count = lax.axis_size(axis)
    route = []
    for low in range(count):
        high = low | 1 << distance
        if high != low and high < count:
            route += [(low, high), (high, low)]
    return lax.ppermute(block, axis, route)


def padded(shard, sides, width):
    for axis, dim in sides:
        size, length = (lax.axis_size(axis), shard.shape[dim])
        up = [(i, (i + 1) % size) for i in range(size - 1)]
        down = [(j, i) for i, j in up]
        last = lax.slice_in_dim(shard, length - width, length, axis=dim)
        first = lax.slice_in_dim(shard, 0, width, axis=dim)
        before = lax.ppermute(last, axis, up)
        after = lax.ppermute(first, axis, down)
        shard = jnp.concatenate([before, shard, after], axis=dim)
    return shard


def curl_plane(stencil_slab):
    center = stencil_slab[:, :, 1]

    def along_x(component):
        return (center[:, component, 2:, 1:-1] - center[:, component, :-2, 1:-1]) * 0.5

    def along_y(component):
        return (center[:, component, 1:-1, 2:] - center[:, component, 1:-1, :-2]) * 0.5

    def along_z(component):
        return (
            stencil_slab[:, component, 2, 1:-1, 1:-1] - stencil_slab[:, component, 0, 1:-1, 1:-1]
        ) * 0.5

    current_x = along_y(2) - along_z(1)
    current_y = along_z(0) - along_x(2)
    current_z = along_x(1) - along_y(0)
    return jnp.stack([current_x, current_y, current_z], axis=1).astype(jnp.bfloat16)


def pair_mixing(signed, planes):
    my_index = lax.axis_index("mix")
    values = signed
    for level in range(planes.bit_length() - 1):
        partner = swapped(values, "mix", level)
        upper_bit = my_index // (1 << level) % 2
        values = jnp.where(upper_bit == 1, partner - values, values + partner)
    return values / math.sqrt(planes)


def upper_factor(gram_matrix):
    return jnp.linalg.cholesky(gram_matrix).T


def on_device(velocity, field_b, test_signs, row_signs, sample_index):
    snaps = field_b.shape[0]
    sketch_width = test_signs.shape[1]
    planes = lax.axis_size("mix")
    row_blocks = lax.axis_size("row")
    with_rims = padded(field_b, (("row", 3), ("mix", 2)), 1)
    stencil_slab = jnp.pad(with_rims.astype(jnp.float32), ((0, 0), (0, 0), (0, 0), (0, 0), (1, 1)))
    current = curl_plane(stencil_slab)
    snapshot = jnp.concatenate([velocity[:, :, 0], current], axis=1).reshape(6 * snaps, -1)
    test_matrix = (2 * test_signs - 1).astype(jnp.bfloat16)
    sketch = lax.dot_general(
        snapshot, test_matrix, (((0,), (0,)), ((), ())), preferred_element_type=jnp.float32
    ) * (1.0 / math.sqrt(6 * snaps))
    point_signs = (2 * row_signs - 1).astype(jnp.float32).reshape(-1)
    signed = sketch * point_signs[:, None]
    mixed_rows = pair_mixing(signed, planes)
    picked = jnp.take(mixed_rows, sample_index.reshape(-1), axis=0)
    picked_total = planes * row_blocks * picked.shape[0]
    local_gram = (
        jnp.dot(
            picked.T, picked, precision=lax.Precision.HIGHEST, preferred_element_type=jnp.float32
        )
        / picked_total
    )
    block_factor = upper_factor(lax.psum(local_gram, "mix"))
    every_factor = lax.all_gather(block_factor[None], "row", axis=0, tiled=True)
    stacked_gram = jnp.einsum(
        "bij,bil->jl", every_factor, every_factor, precision=lax.Precision.HIGHEST
    )
    factor = upper_factor(stacked_gram)
    solved = jax.scipy.linalg.solve_triangular(factor.T, picked.T, lower=True)
    basis_rows = solved.T.reshape(sample_index.shape + (sketch_width,))
    return (basis_rows, factor)


def solution(mesh):
    return jax.shard_map(
        on_device,
        mesh=mesh,
        in_specs=(
            P(None, None, "mix", "row", None),
            P(None, None, "mix", "row", None),
            P(),
            P("mix", "row", None),
            P("mix", "row", None),
        ),
        out_specs=(P("mix", "row", None, None), P()),
        check_vma=False,
    )
```

profile of v0, /device:TPU:0, one launch (start us, length us, event | category | flops | bytes accessed | tf_op | source)
XLA Modules:
  0.0 284.6 jit_solution(11077461579640509562)
XLA Ops:
  7.2 1.4 fusion.46
  8.6 4.9 %collective-permute-start = (bf16[64,3,1,1,128]{4,0,3,2,1:T(8,128)(2,1)S(1)}, bf16[64,3,1,1,128]{4,0,3,2,1:T(8,128)(2,1)S(1)}, u32[]{:S(2)}, u32[]{:S(2)}) collective-permute-start(bf16[64,3,1,1,128]{4,0,3,2,1:T(8,128)(2,1)S(1)} %copy.62), channel_id=1, source_target_pairs={{0,8},{8,16},{16,24},{1,9},{9,17},{17,25},{2,10},{10,18},{18,26},{... | collective-permute-start | bytes 147464 | tf_op jit(solution)/shard_map/ppermute | solution.py:26
  13.6 1.3 collective-permute-start.1
  16.4 3.2 %collective-permute-done.1 = bf16[64,3,1,1,128]{4,0,3,2,1:T(8,128)(2,1)S(1)} collective-permute-done((bf16[64,3,1,1,128]{4,0,3,2,1:T(8,128)(2,1)S(1)}, bf16[64,3,1,1,128]{4,0,3,2,1:T(8,128)(2,1)S(1)}, u32[]{:S(2)}, u32[]{:S(2)}) %collective-permute-start.1) | collective-permute-done | bytes 49184 | tf_op jit(solution)/shard_map/ppermute | solution.py:27
  20.9 3.1 %collective-permute-start.2 = (bf16[64,3,1,10,128]{4,0,3,2,1:T(8,128)(2,1)S(1)}, bf16[64,3,1,10,128]{4,0,3,2,1:T(8,128)(2,1)S(1)}, u32[]{:S(2)}, u32[]{:S(2)}) collective-permute-start(bf16[64,3,1,10,128]{4,0,3,2,1:T(8,128)(2,1)S(1)} %constant_dynamic-update-slice_fusion), channel_id=1, source_target_pairs={{0,1},{1,2},{2,3},{3,4},{4,5},{5,6},{6,7},{8,9},{9,10},{10,11},{11... | collective-permute-start | bytes 1474568 | tf_op jit(solution)/shard_map/ppermute | solution.py:26
  28.0 6.6 %collective-permute-start.4 = (f32[1024,256]{1,0:T(8,128)S(1)}, f32[1024,256]{1,0:T(8,128)S(1)}, u32[]{:S(2)}, u32[]{:S(2)}) collective-permute-start(f32[1024,256]{1,0:T(8,128)S(1)} %convolution_multiply_fusion), channel_id=1, source_target_pairs={{0,1},{1,0},{2,3},{3,2},{4,5},{5,4},{6,7},{7,6},{8,9},{9,8},{10,11... | collective-permute-start | bytes 3145736 | tf_op jit(solution)/shard_map/ppermute | solution.py:16
  34.6 2.3 collective-permute-done.4
  37.0 2.8 collective-permute-start.5
  39.9 23.7 %collective-permute-done.5 = f32[1024,256]{1,0:T(8,128)S(1)} collective-permute-done((f32[1024,256]{1,0:T(8,128)S(1)}, f32[1024,256]{1,0:T(8,128)S(1)}, u32[]{:S(2)}, u32[]{:S(2)}) %collective-permute-start.5) | collective-permute-done | bytes 1048608 | tf_op jit(solution)/shard_map/ppermute | solution.py:16
  63.7 3.7 %collective-permute-start.6 = (f32[1024,256]{1,0:T(8,128)S(1)}, f32[1024,256]{1,0:T(8,128)S(1)}, u32[]{:S(2)}, u32[]{:S(2)}) collective-permute-start(f32[1024,256]{1,0:T(8,128)S(1)} %add_select_fusion), channel_id=1, source_target_pairs={{0,4},{4,0},{1,5},{5,1},{2,6},{6,2},{3,7},{7,3},{8,12},{12,8},{9,1... | collective-permute-start | bytes 3145736 | tf_op jit(solution)/shard_map/ppermute | solution.py:16
  67.5 22.6 %collective-permute-done.6 = f32[1024,256]{1,0:T(8,128)S(1)} collective-permute-done((f32[1024,256]{1,0:T(8,128)S(1)}, f32[1024,256]{1,0:T(8,128)S(1)}, u32[]{:S(2)}, u32[]{:S(2)}) %collective-permute-start.6) | collective-permute-done | bytes 1048608 | tf_op jit(solution)/shard_map/ppermute | solution.py:16
  92.7 53.0 %all-reduce.4.cloned.1.call-done = f32[256,256]{0,1:T(8,128)} async-done(((f32[256,256]{0,1:T(8,128)}), f32[256,256]{0,1:T(8,128)}) %all-reduce.4.cloned.1.call-update) | async-done | bytes 262160 | tf_op jit(solution)/shard_map/psum | solution.py:90
  147.8 11.7 %cholesky.130 = f32[128,128]{1,0:T(8,128)S(1)} custom-call(f32[128,128]{1,0:T(8,128)S(1)} %cholesky.194), custom_call_target="Cholesky" | custom-call | tf_op jit(solution)/shard_map/jit(cholesky)/cholesky | solution.py:63
  159.6 9.8 %custom-call.14 = f32[1,128,128]{1,2,0:T(8,128)S(1)} custom-call(f32[1,128,128]{2,1,0:T(8,128)S(1)} %get-tuple-element.41), custom_call_target="InvertDiagBlocksLowerTriangular" | custom-call | tf_op jit(solution)/shard_map/jit(cholesky)/cholesky | solution.py:63
  169.9 11.7 %cholesky.147 = f32[128,128]{1,0:T(8,128)S(1)} custom-call(f32[128,128]{1,0:T(8,128)S(1)} %convolution_subtract_fusion.2), custom_call_target="Cholesky" | custom-call | tf_op jit(solution)/shard_map/jit(cholesky)/cholesky | solution.py:63
  184.4 27.4 %all-gather.3.cloned.1.call-done = f32[1024,256]{0,1:T(8,128)} async-done(((f32[256,256]{0,1:T(8,128)}), f32[1024,256]{0,1:T(8,128)}) %all-gather.3.cloned.1.call-update) | async-done | bytes 1048592 | tf_op jit(solution)/shard_map/all_gather | solution.py:91
  211.8 2.6 convolution_bitcast_fusion
  214.6 11.9 %cholesky.164 = f32[128,128]{1,0:T(8,128)S(1)} custom-call(f32[128,128]{1,0:T(8,128)S(1)} %cholesky.197), custom_call_target="Cholesky" | custom-call | tf_op jit(solution)/shard_map/jit(cholesky)/cholesky | solution.py:63
  226.6 9.8 %custom-call.15 = f32[1,128,128]{1,2,0:T(8,128)S(1)} custom-call(f32[1,128,128]{2,1,0:T(8,128)S(1)} %get-tuple-element.37), custom_call_target="InvertDiagBlocksLowerTriangular" | custom-call | tf_op jit(solution)/shard_map/jit(cholesky)/cholesky | solution.py:63
  236.8 11.7 %cholesky.181 = f32[128,128]{1,0:T(8,128)S(1)} custom-call(f32[128,128]{1,0:T(8,128)S(1)} %convolution_subtract_fusion.1), custom_call_target="Cholesky" | custom-call | tf_op jit(solution)/shard_map/jit(cholesky)/cholesky | solution.py:63
  251.3 4.2 %while.1 = (s32[]{:T(128)}, f32[256,256]{1,0:T(8,128)S(1)}, s32[2,2]{1,0:T(2,128)S(1)}, f32[2,128,128]{2,1,0:T(8,128)S(1)}, s32[]{:T(128)}) while((s32[]{:T(128)}, f32[256,256]{1,0:T(8,128)S(1)}, s32[2,2]{1,0:T(2,128)S(1)}, f32[2,128,128]{2,1,0:T(8,128)S(1)}, s32[]{:T(128)}) %tuple.38), condition=%wide.while_cond, body=%wide.while_body.sunk | while | flops 2 | bytes 131189 | solution.py:96
  252.1 1.4 bitcast_dynamic-update-slice_fusion.2
  254.1 1.4 bitcast_dynamic-update-slice_fusion.2
  255.5 19.7 %custom-call.12 = f32[2,128,128]{1,2,0:T(8,128)S(1)} custom-call(f32[2,128,128]{2,1,0:T(8,128)S(1)} %get-tuple-element.10), custom_call_target="InvertDiagBlocksLowerTriangular" | custom-call | tf_op jit(solution)/shard_map/jit(_solve_triangular)/triangular_solve | solution.py:96
  (72 shorter events, 19.7 us)
Async XLA Ops:
  7.2 138.5 %all-reduce.4.cloned.1.call-start = ((), (), s32[]{:S(2)}) async-start(), calls=%async_computation | async-start | bytes 524288 | tf_op jit(solution)/shard_map/psum | solution.py:90
  8.6 6.7 %collective-permute-start = (bf16[64,3,1,1,128]{4,0,3,2,1:T(8,128)(2,1)S(1)}, bf16[64,3,1,1,128]{4,0,3,2,1:T(8,128)(2,1)S(1)}, u32[]{:S(2)}, u32[]{:S(2)}) collective-permute-start(bf16[64,3,1,1,128]{4,0,3,2,1:T(8,128)(2,1)S(1)} %copy.62), channel_id=1, source_target_pairs={{0,8},{8,16},{16,24},{1,9},{9,17},{17,25},{2,10},{10,18},{18,26},{... | collective-permute-start | bytes 147464 | tf_op jit(solution)/shard_map/ppermute | solution.py:26
  13.6 6.0 %collective-permute-start.1 = (bf16[64,3,1,1,128]{4,0,3,2,1:T(8,128)(2,1)S(1)}, bf16[64,3,1,1,128]{4,0,3,2,1:T(8,128)(2,1)S(1)}, u32[]{:S(2)}, u32[]{:S(2)}) collective-permute-start(bf16[64,3,1,1,128]{4,0,3,2,1:T(8,128)(2,1)S(1)} %copy.63), channel_id=1, source_target_pairs={{8,0},{16,8},{24,16},{9,1},{17,9},{25,17},{10,2},{18,10},{26,18},{... | collective-permute-start | bytes 147464 | tf_op jit(solution)/shard_map/ppermute | solution.py:27
  19.6 5.1 %collective-permute-start.3 = (bf16[64,3,1,10,128]{4,0,3,2,1:T(8,128)(2,1)S(1)}, bf16[64,3,1,10,128]{4,0,3,2,1:T(8,128)(2,1)S(1)}, u32[]{:S(2)}, u32[]{:S(2)}) collective-permute-start(bf16[64,3,1,10,128]{4,0,3,2,1:T(8,128)(2,1)S(1)} %constant_dynamic-update-slice_fusion), channel_id=1, source_target_pairs={{1,0},{2,1},{3,2},{4,3},{5,4},{6,5},{7,6},{9,8},{10,9},{11,10},{12... | collective-permute-start | bytes 1474568 | tf_op jit(solution)/shard_map/ppermute | solution.py:27
  20.9 4.5 %collective-permute-start.2 = (bf16[64,3,1,10,128]{4,0,3,2,1:T(8,128)(2,1)S(1)}, bf16[64,3,1,10,128]{4,0,3,2,1:T(8,128)(2,1)S(1)}, u32[]{:S(2)}, u32[]{:S(2)}) collective-permute-start(bf16[64,3,1,10,128]{4,0,3,2,1:T(8,128)(2,1)S(1)} %constant_dynamic-update-slice_fusion), channel_id=1, source_target_pairs={{0,1},{1,2},{2,3},{3,4},{4,5},{5,6},{6,7},{8,9},{9,10},{10,11},{11... | collective-permute-start | bytes 1474568 | tf_op jit(solution)/shard_map/ppermute | solution.py:26
  26.0 1.0 copy-start
  26.5 1.0 copy-start.2
  28.0 8.9 %collective-permute-start.4 = (f32[1024,256]{1,0:T(8,128)S(1)}, f32[1024,256]{1,0:T(8,128)S(1)}, u32[]{:S(2)}, u32[]{:S(2)}) collective-permute-start(f32[1024,256]{1,0:T(8,128)S(1)} %convolution_multiply_fusion), channel_id=1, source_target_pairs={{0,1},{1,0},{2,3},{3,2},{4,5},{5,4},{6,7},{7,6},{8,9},{9,8},{10,11... | collective-permute-start | bytes 3145736 | tf_op jit(solution)/shard_map/ppermute | solution.py:16
  37.0 30.4 %copy-start.1 = (s32[1,1,256]{2,1,0:T(1,128)S(1)}, s32[1,1,256]{2,1,0:T(1,128)}, u32[]{:S(2)}) copy-start(s32[1,1,256]{2,1,0:T(1,128)} %param.10) | copy-start | bytes 3076
  37.0 26.5 %collective-permute-start.5 = (f32[1024,256]{1,0:T(8,128)S(1)}, f32[1024,256]{1,0:T(8,128)S(1)}, u32[]{:S(2)}, u32[]{:S(2)}) collective-permute-start(f32[1024,256]{1,0:T(8,128)S(1)} %add_select_fusion.1), channel_id=1, source_target_pairs={{0,2},{2,0},{1,3},{3,1},{4,6},{6,4},{5,7},{7,5},{8,10},{10,8},{9,1... | collective-permute-start | bytes 3145736 | tf_op jit(solution)/shard_map/ppermute | solution.py:16
  63.7 26.4 %collective-permute-start.6 = (f32[1024,256]{1,0:T(8,128)S(1)}, f32[1024,256]{1,0:T(8,128)S(1)}, u32[]{:S(2)}, u32[]{:S(2)}) collective-permute-start(f32[1024,256]{1,0:T(8,128)S(1)} %add_select_fusion), channel_id=1, source_target_pairs={{0,4},{4,0},{1,5},{5,1},{2,6},{6,2},{3,7},{7,3},{8,12},{12,8},{9,1... | collective-permute-start | bytes 3145736 | tf_op jit(solution)/shard_map/ppermute | solution.py:16
  92.5 119.3 %all-gather.3.cloned.1.call-start = ((), (), s32[]{:S(2)}) async-start(), calls=%async_computation.1 | async-start | bytes 1310720 | tf_op jit(solution)/shard_map/all_gather | solution.py:91
Sparse Core Ops, SparseCore 0:
  92.6 53.0 all-reduce.3
  184.4 27.2 all-gather.2
where the time goes:
time: 285 us
  waiting for transfers between devices  133 us (47%)
  other arithmetic  92.6 us (32%)
  starting transfers between devices  24 us (8%)
  between operations  17 us (6%)
  local copies, waits for them, and re-layouts  11.4 us (4%)
  matrix products  5.98 us (2%)
    another operation x13, other arithmetic, upper_factor(): return jnp.linalg.cholesky(gram_matrix).T  68.8 us
    psum x1, waiting for transfers between devices, on_device(): block_factor = upper_factor(lax.psum(local_gram, 'mix'))  53 us
    ppermute x3, waiting for transfers between devices, swapped(): return lax.ppermute(block, axis, route)  48.6 us
    all_gather x1, waiting for transfers between devices, on_device(): every_factor = lax.all_gather(block_factor[None], 'row', axis=0, tiled=True)  27.4 us
    another operation x2, other arithmetic, on_device(): solved = jax.scipy.linalg.solve_triangular(factor.T, picked.T, lower=True)  19.7 us
    ppermute x3, starting transfers between devices, swapped(): return lax.ppermute(block, axis, route)  13.2 us
    ppermute x2, starting transfers between devices, padded(): before = lax.ppermute(last, axis, up)  7.99 us
  transfers between devices with their start and end apart: 9, of which 8 were waited for; matrix products, arithmetic and copies ran while one was open for 1% of the time, Pallas kernels for 0%

commit v1 on v0

v1 whole, which is shorter than its diff:
```python
import math

import jax
import jax.numpy as jnp
from jax import lax
from jax.sharding import PartitionSpec as P

MESH_AXES = ("row", "mix")


def xor_route(count, bits):
    return [(i, i ^ bits) for i in range(count) if i ^ bits < count]


def turn_route(count, steps):
    return [(i, (i + steps) % count) for i in range(count)]


def neighbours(first, last, axis):
    size = lax.axis_size(axis)
    up = [(i, i + 1) for i in range(size - 1)]
    down = [(i + 1, i) for i in range(size - 1)]
    return lax.ppermute(last, axis, up), lax.ppermute(first, axis, down)


def curl(field_b):
    plane = field_b[:, :, 0]
    below, above = neighbours(plane[:, :2], plane[:, :2], "mix")
    left, right = neighbours(plane[:, 1:, :1], plane[:, 1:, -1:], "row")
    with_rims = jnp.concatenate([left, plane[:, 1:], right], axis=2).astype(jnp.float32)
    center = plane.astype(jnp.float32)
    over_z = (above.astype(jnp.float32) - below.astype(jnp.float32)) * 0.5
    over_x = (with_rims[:, :, 2:] - with_rims[:, :, :-2]) * 0.5
    wide = jnp.pad(center, ((0, 0), (0, 0), (0, 0), (1, 1)))
    over_y = (wide[..., 2:] - wide[..., :-2]) * 0.5
    current_x = over_y[:, 2] - over_z[:, 1]
    current_y = over_z[:, 0] - over_x[:, 1]
    current_z = over_x[:, 0] - over_y[:, 0]
    return jnp.stack([current_x, current_y, current_z], axis=1).astype(jnp.bfloat16)


def parity_sign(a, b):
    both = jnp.bitwise_and(a, b)
    return 1.0 - 2.0 * (lax.population_count(both) % 2).astype(jnp.float32)


def sampled_mixing(velocity, current, test_matrix, signs, sample_index):
    planes = lax.axis_size("mix")
    mine = lax.axis_index("mix")
    core = mine % 2
    hops = range(2, planes, 2)
    wanted = [sample_index] + [lax.ppermute(sample_index, "mix", xor_route(planes, k)) for k in hops]
    wanted = jnp.stack(wanted)
    snaps = velocity.shape[0]
    points = signs.shape[0]

    def flat(part):
        return part.reshape(3 * snaps, points) * signs

    by_part = test_matrix.reshape(snaps, 6, -1)
    for_velocity = by_part[:, :3].reshape(3 * snaps, -1)
    for_current = by_part[:, 3:].reshape(3 * snaps, -1)
    own_sign = (1 - 2 * core).astype(jnp.bfloat16)
    chosen = (wanted[:, None, :] == jnp.arange(points, dtype=jnp.int32)[None, :, None]).astype(jnp.bfloat16)

    def part_sum(part, matrix):
        own = flat(part)
        other = lax.ppermute(own, "mix", xor_route(planes, 1))
        both = jnp.concatenate([own, other])
        gathered = jnp.einsum("sp,tpk->tsk", both, chosen, preferred_element_type=jnp.float32).astype(jnp.bfloat16)
        twice = jnp.concatenate([own_sign * matrix, matrix])
        return jnp.einsum("sj,tsk->tjk", twice, gathered, preferred_element_type=jnp.float32)

    parts = part_sum(velocity, for_velocity) + part_sum(current, for_current)
    total = parity_sign(mine, mine - core) * parts[0]
    for slot, k in enumerate(hops):
        arrived = lax.ppermute(parts[slot + 1], "mix", xor_route(planes, k))
        total = total + parity_sign(mine, (mine ^ k) - core) * arrived
    return total * (1.0 / math.sqrt(6 * snaps) / math.sqrt(planes))


def whole_mixing(velocity, current, test_matrix, signs, sample_index):
    planes = lax.axis_size("mix")
    mine = lax.axis_index("mix")
    snaps = velocity.shape[0]
    snapshot = jnp.concatenate([velocity, current], axis=1).reshape(6 * snaps, -1) * signs
    values = lax.dot_general(
        snapshot, test_matrix, (((0,), (0,)), ((), ())), preferred_element_type=jnp.float32
    ) * (1.0 / math.sqrt(6 * snaps))
    for level in range(planes.bit_length() - 1):
        partner = lax.ppermute(values, "mix", xor_route(planes, 1 << level))
        upper_bit = mine // (1 << level) % 2
        values = jnp.where(upper_bit == 1, partner - values, values + partner)
    return jnp.take(values / math.sqrt(planes), sample_index, axis=0).T


def sum_over_mesh(gram):
    planes, blocks = lax.axis_size("mix"), lax.axis_size("row")
    if planes > 8 or blocks > 4:
        return lax.psum(gram, MESH_AXES)
    n = gram.shape[0]
    core = lax.axis_index("mix") % 2
    low, high = gram[: n // 2], gram[n // 2 :]
    half = jnp.where(core == 0, low, high)
    half = half + lax.ppermute(jnp.where(core == 0, high, low), "mix", xor_route(planes, 1))
    half = half + sum(lax.ppermute(half, "mix", xor_route(planes, k)) for k in range(2, planes, 2))
    half = half + sum(lax.ppermute(half, "row", turn_route(blocks, k)) for k in range(1, blocks))
    other = lax.ppermute(half, "mix", xor_route(planes, 1))
    return jnp.concatenate([jnp.where(core == 0, half, other), jnp.where(core == 0, other, half)])


def on_device(velocity, field_b, test_signs, row_signs, sample_index):
    snaps = field_b.shape[0]
    sketch_width = test_signs.shape[1]
    planes, blocks = lax.axis_size("mix"), lax.axis_size("row")
    samples = sample_index.shape[-1]
    points = row_signs.size
    test_matrix = (2 * test_signs - 1).astype(jnp.bfloat16)
    signs = (2 * row_signs - 1).astype(jnp.bfloat16).reshape(-1)
    current = curl(field_b)
    sampled_bytes = (planes // 2 - 1) * samples * sketch_width
    whole_bytes = (planes.bit_length() - 1) * points * sketch_width
    mixing = sampled_mixing if sampled_bytes < whole_bytes else whole_mixing
    picked = mixing(velocity[:, :, 0], current, test_matrix, signs, sample_index.reshape(-1))
    gram = jnp.einsum(
        "ik,jk->ij", picked, picked, precision=lax.Precision.HIGHEST, preferred_element_type=jnp.float32
    ) * (1.0 / (planes * blocks * samples))
    lower = jnp.linalg.cholesky(sum_over_mesh(gram))
    solved = jax.scipy.linalg.solve_triangular(lower, picked, lower=True)
    return solved.T.reshape(sample_index.shape + (sketch_width,)), lower.T


def solution(mesh):
    return jax.shard_map(
        on_device,
        mesh=mesh,
        in_specs=(
            P(None, None, "mix", "row", None),
            P(None, None, "mix", "row", None),
            P(),
            P("mix", "row", None),
            P("mix", "row", None),
        ),
        out_specs=(P("mix", "row", None, None), P()),
        check_vma=False,
    )
```

time: 285 us -> 139 us (0.49)
  waiting for transfers between devices: 133 us -> 34.4 us
  other arithmetic: 92.6 us -> 56 us
  between operations: 17 us -> 2.4 us
  starting transfers between devices: 24 us -> 30.3 us
    psum x1 -> x0, waiting for transfers between devices: 53 us -> none  [on_device(): block_factor = upper_factor(lax.psum(local_gram, 'mix'))]
    another operation x16 -> x12, other arithmetic: 88.9 us -> 54.5 us  [the longest x7 34.6 us: on_device(): lower = jnp.linalg.cholesky(sum_over_mesh(gram))]
    all_gather x1 -> x0, waiting for transfers between devices: 27.4 us -> none  [on_device(): every_factor = lax.all_gather(block_factor[None], 'row', axis=0, tiled=True)]
    ppermute x7 -> x20, waiting for transfers between devices: 52.9 us -> 34.4 us  [the longest x3 11.3 us: sampled_mixing(): arrived = lax.ppermute(parts[slot + 1], 'mix', xor_route(planes, k))]
    ppermute x7 -> x20, starting transfers between devices: 23.8 us -> 30.3 us  [the longest x4 8.44 us: neighbours(): return (lax.ppermute(last, axis, up), lax.ppermute(first, axis, down))]
  transfers between devices with their start and end apart: 9 -> 20, of which waited for: 8 -> 11; matrix products, arithmetic and copies ran while one was open for 1% -> 4% of each run, Pallas kernels for 0% -> 0%
where the time goes in v1:
time: 139 us
  other arithmetic  56 us (40%)
  waiting for transfers between devices  34.4 us (25%)
  starting transfers between devices  30.3 us (22%)
  local copies, waits for them, and re-layouts  10 us (7%)
  matrix products  5.42 us (4%)
  between operations  2.4 us (2%)
    another operation x7, other arithmetic, on_device(): lower = jnp.linalg.cholesky(sum_over_mesh(gram))  34.6 us
    another operation x2, other arithmetic, on_device(): solved = jax.scipy.linalg.solve_triangular(lower, picked, lower=True)  19.7 us
    ppermute x3, waiting for transfers between devices, sampled_mixing(): arrived = lax.ppermute(parts[slot + 1], 'mix', xor_route(planes, k))  11.3 us
    ppermute x3, waiting for transfers between devices, sum_over_mesh(): lax.ppermute(half, 'row', turn_route(blocks, k))  9.9 us
    ppermute x4, starting transfers between devices, neighbours(): return (lax.ppermute(last, axis, up), lax.ppermute(first, axis, down))  8.44 us
    ppermute x3, waiting for transfers between devices, sum_over_mesh(): lax.ppermute(half, 'mix', xor_route(planes, k))  5.77 us
    ppermute x2, starting transfers between devices, part_sum(): other = lax.ppermute(own, 'mix', xor_route(planes, 1))  4.96 us
    ppermute x3, starting transfers between devices, sum_over_mesh(): lax.ppermute(half, 'row', turn_route(blocks, k))  4.66 us
  transfers between devices with their start and end apart: 20, of which 11 were waited for; matrix products, arithmetic and copies ran while one was open for 4% of the time, Pallas kernels for 0%

profile of v1, /device:TPU:0, one launch (start us, length us, event | category | flops | bytes accessed | tf_op | source)
XLA Modules:
  0.0 138.7 jit_solution(16655356998082850027)
XLA Ops:
  0.6 4.0 %collective-permute-start.2 = (s32[256]{0:T(256)}, s32[256]{0:T(256)S(1)}, u32[]{:S(2)}, u32[]{:S(2)}) collective-permute-start(s32[256]{0:T(256)} %bitcast.99), channel_id=1, source_target_pairs={{0,6},{1,7},{2,4},{3,5},{4,2},{5,3},{6,0},{7,1},{8,14},{9,15},{10,... | collective-permute-start | bytes 3080 | tf_op jit(solution)/shard_map/ppermute | solution.py:52
  7.7 4.5 %collective-permute-start.6 = (bf16[64,2,1,128]{3,2,1,0:T(2,128)(2,1)S(1)}, bf16[64,2,1,128]{3,2,1,0:T(2,128)(2,1)S(1)}, u32[]{:S(2)}, u32[]{:S(2)}) collective-permute-start(bf16[64,2,1,128]{3,2,1,0:T(2,128)(2,1)S(1)} %get-tuple-element.32), channel_id=1, source_target_pairs={{0,8},{8,16},{16,24},{1,9},{9,17},{17,25},{2,10},{10,18},{18,26},{... | collective-permute-start | bytes 98312 | tf_op jit(solution)/shard_map/ppermute | solution.py:23
  17.8 3.9 %collective-permute-done.4 = bf16[64,2,8,128]{3,2,1,0:T(8,128)(2,1)S(1)} collective-permute-done((bf16[64,2,8,128]{3,2,1,0:T(8,128)(2,1)S(1)}, bf16[64,2,8,128]{3,2,1,0:T(8,128)(2,1)S(1)}, u32[]{:S(2)}, u32[]{:S(2)}) %collective-permute-start.4) | collective-permute-done | bytes 262176 | tf_op jit(solution)/shard_map/ppermute | solution.py:23
  22.8 4.9 %collective-permute-start.3 = (bf16[192,1024]{1,0:T(8,128)(2,1)S(1)}, bf16[192,1024]{1,0:T(8,128)(2,1)S(1)}, u32[]{:S(2)}, u32[]{:S(2)}) collective-permute-start(bf16[192,1024]{1,0:T(8,128)(2,1)S(1)} %get-tuple-element.45), channel_id=1, source_target_pairs={{0,1},{1,0},{2,3},{3,2},{4,5},{5,4},{6,7},{7,6},{8,9},{9,8},{10,11... | collective-permute-start | bytes 1179656 | tf_op jit(solution)/shard_map/ppermute | solution.py:68
  29.0 1.7 %fusion.21 = f32[4,256,256]{2,1,0:T(8,128)S(1)} fusion(s32[4,256]{1,0:T(4,128)S(1)} %pad_add_fusion, bf16[192,1024]{1,0:T(8,128)(2,1)S(1)} %collective-permute-done.3, bf16[192,1024]{1,0:T(8,128)(2,1)S(1)} %get-tuple-element.45, bf16[192,256]{1,0:T(8,128)(2,1)S(1)} %reshape.47, bf16[192,256]{1,0:T(8,128)(2,1)S(1)} %get-tuple-element.49), kind=kOutput, calls=%fused_computation.14 | convolution fusion | flops 1011089408 | bytes 2035712 | tf_op jit(solution)/shard_map/sj,tsk->tjk/dot_general | solution.py:72
  30.7 1.7 %fusion.13 = f32[4,256,256]{1,2,0:T(8,128)S(1)} fusion(f32[4,256,256]{2,1,0:T(8,128)S(1)} %fusion.21, s32[4,256]{1,0:T(4,128)S(1)} %pad_add_fusion, bf16[192,1024]{1,0:T(8,128)(2,1)S(1)} %collective-permute-done.8, bf16[192,1024]{1,0:T(8,128)(2,1)S(1)} %get-tuple-element.44, bf16[192,256]{1,0:T(8,128)(2,1)S(1)} %reshape.48, ...), kind=kOutput, calls=%fused_computation.11 | convolution fusion | flops 1011351552 | bytes 3084288 | tf_op jit(solution)/shard_map/sj,tsk->tjk/dot_general | solution.py:72
  33.5 2.8 %collective-permute-start.10 = (f32[256,256]{0,1:T(8,128)S(1)}, f32[256,256]{0,1:T(8,128)S(1)}, u32[]{:S(2)}, u32[]{:S(2)}) collective-permute-start(f32[256,256]{0,1:T(8,128)S(1)} %get-tuple-element.26), channel_id=1, source_target_pairs={{0,4},{1,5},{2,6},{3,7},{4,0},{5,1},{6,2},{7,3},{8,12},{9,13},{10,... | collective-permute-start | bytes 786440 | tf_op jit(solution)/shard_map/ppermute | solution.py:77
  36.4 6.3 %collective-permute-done.11 = f32[256,256]{0,1:T(8,128)S(1)} collective-permute-done((f32[256,256]{0,1:T(8,128)S(1)}, f32[256,256]{0,1:T(8,128)S(1)}, u32[]{:S(2)}, u32[]{:S(2)}) %collective-permute-start.11) | collective-permute-done | bytes 262176 | tf_op jit(solution)/shard_map/ppermute | solution.py:77
  42.6 5.0 %collective-permute-done.10 = f32[256,256]{0,1:T(8,128)S(1)} collective-permute-done((f32[256,256]{0,1:T(8,128)S(1)}, f32[256,256]{0,1:T(8,128)S(1)}, u32[]{:S(2)}, u32[]{:S(2)}) %collective-permute-start.10) | collective-permute-done | bytes 262176 | tf_op jit(solution)/shard_map/ppermute | solution.py:77
  48.5 1.3 collective-permute-done.12
  49.8 2.4 %collective-permute-start.15 = (f32[128,256]{0,1:T(8,128)S(1)}, f32[128,256]{0,1:T(8,128)S(1)}, u32[]{:S(2)}, u32[]{:S(2)}) collective-permute-start(f32[128,256]{0,1:T(8,128)S(1)} %select_add_fusion), channel_id=1, source_target_pairs={{0,6},{1,7},{2,4},{3,5},{4,2},{5,3},{6,0},{7,1},{8,14},{9,15},{10,... | collective-permute-start | bytes 393224 | tf_op jit(solution)/shard_map/ppermute | solution.py:106
  53.4 3.7 %collective-permute-done.15 = f32[128,256]{0,1:T(8,128)S(1)} collective-permute-done((f32[128,256]{0,1:T(8,128)S(1)}, f32[128,256]{0,1:T(8,128)S(1)}, u32[]{:S(2)}, u32[]{:S(2)}) %collective-permute-start.15) | collective-permute-done | bytes 131104 | tf_op jit(solution)/shard_map/ppermute | solution.py:106
  57.1 2.0 %collective-permute-done.13 = f32[128,256]{0,1:T(8,128)S(1)} collective-permute-done((f32[128,256]{0,1:T(8,128)S(1)}, f32[128,256]{0,1:T(8,128)S(1)}, u32[]{:S(2)}, u32[]{:S(2)}) %collective-permute-start.13) | collective-permute-done | bytes 131104 | tf_op jit(solution)/shard_map/ppermute | solution.py:106
  59.2 1.5 %collective-permute-start.18 = (f32[128,256]{0,1:T(8,128)S(1)}, f32[128,256]{0,1:T(8,128)S(1)}, u32[]{:S(2)}, u32[]{:S(2)}) collective-permute-start(f32[128,256]{0,1:T(8,128)S(1)} %add_add_fusion.1), channel_id=1, source_target_pairs={{0,24},{8,0},{16,8},{24,16},{1,25},{9,1},{17,9},{25,17},{2,26},{10... | collective-permute-start | bytes 393224 | tf_op jit(solution)/shard_map/ppermute | solution.py:107
  61.3 2.6 %collective-permute-start.17 = (f32[128,256]{0,1:T(8,128)S(1)}, f32[128,256]{0,1:T(8,128)S(1)}, u32[]{:S(2)}, u32[]{:S(2)}) collective-permute-start(f32[128,256]{0,1:T(8,128)S(1)} %add_add_fusion.1), channel_id=1, source_target_pairs={{0,16},{8,24},{16,0},{24,8},{1,17},{9,25},{17,1},{25,9},{2,18},{10... | collective-permute-start | bytes 393224 | tf_op jit(solution)/shard_map/ppermute | solution.py:107
  64.6 5.9 %collective-permute-done.16 = f32[128,256]{0,1:T(8,128)S(1)} collective-permute-done((f32[128,256]{0,1:T(8,128)S(1)}, f32[128,256]{0,1:T(8,128)S(1)}, u32[]{:S(2)}, u32[]{:S(2)}) %collective-permute-start.16) | collective-permute-done | bytes 131104 | tf_op jit(solution)/shard_map/ppermute | solution.py:107
  70.6 3.2 %collective-permute-done.17 = f32[128,256]{0,1:T(8,128)S(1)} collective-permute-done((f32[128,256]{0,1:T(8,128)S(1)}, f32[128,256]{0,1:T(8,128)S(1)}, u32[]{:S(2)}, u32[]{:S(2)}) %collective-permute-start.17) | collective-permute-done | bytes 131104 | tf_op jit(solution)/shard_map/ppermute | solution.py:107
  75.5 11.7 %cholesky.50 = f32[128,128]{1,0:T(8,128)S(1)} custom-call(f32[128,128]{1,0:T(8,128)S(1)} %cholesky.118), custom_call_target="Cholesky" | custom-call | tf_op jit(solution)/shard_map/jit(cholesky)/cholesky | solution.py:128
  87.2 9.8 %custom-call.15 = f32[1,128,128]{1,2,0:T(8,128)S(1)} custom-call(f32[1,128,128]{2,1,0:T(8,128)S(1)} %get-tuple-element.43), custom_call_target="InvertDiagBlocksLowerTriangular" | custom-call | tf_op jit(solution)/shard_map/jit(cholesky)/cholesky | solution.py:128
  97.5 11.7 %cholesky.105 = f32[128,128]{1,0:T(8,128)S(1)} custom-call(f32[128,128]{1,0:T(8,128)S(1)} %convolution_subtract_fusion), custom_call_target="Cholesky" | custom-call | tf_op jit(solution)/shard_map/jit(cholesky)/cholesky | solution.py:128
  112.0 4.2 %while.1 = (s32[]{:T(128)}, f32[256,256]{1,0:T(8,128)S(1)}, s32[2,2]{1,0:T(2,128)S(1)}, f32[2,128,128]{2,1,0:T(8,128)S(1)}, s32[]{:T(128)}) while((s32[]{:T(128)}, f32[256,256]{1,0:T(8,128)S(1)}, s32[2,2]{1,0:T(2,128)S(1)}, f32[2,128,128]{2,1,0:T(8,128)S(1)}, s32[]{:T(128)}) %tuple.39), condition=%wide.while_cond, body=%wide.while_body.sunk | while | flops 2 | bytes 131189 | solution.py:129
  112.8 1.4 %bitcast_dynamic-update-slice_fusion.2 = f32[2,128,128]{2,1,0:T(8,128)S(1)} fusion(f32[2,128,128]{2,1,0:T(8,128)S(1)} %get-tuple-element.87, s32[]{:T(128)S(6)} %copy.25, f32[256,256]{1,0:T(8,128)S(1)} %get-tuple-element.90, s32[]{:T(128)} %bitcast.92, s32[]{:T(128)} %bitcast.93), kind=kLoop, calls=%fused_computation.clone.1 | loop fusion | bytes 131084 | tf_op jit(solution)/shard_map/jit(_solve_triangular)/triangular_solve
  114.8 1.4 %bitcast_dynamic-update-slice_fusion.2 = f32[2,128,128]{2,1,0:T(8,128)S(1)} fusion(f32[2,128,128]{2,1,0:T(8,128)S(1)} %get-tuple-element.87, s32[]{:T(128)S(6)} %copy.25, f32[256,256]{1,0:T(8,128)S(1)} %get-tuple-element.90, s32[]{:T(128)} %bitcast.92, s32[]{:T(128)} %bitcast.93), kind=kLoop, calls=%fused_computation.clone.1 | loop fusion | bytes 131084 | tf_op jit(solution)/shard_map/jit(_solve_triangular)/triangular_solve
  116.3 19.7 %custom-call.16 = f32[2,128,128]{1,2,0:T(8,128)S(1)} custom-call(f32[2,128,128]{2,1,0:T(8,128)S(1)} %get-tuple-element.9), custom_call_target="InvertDiagBlocksLowerTriangular" | custom-call | tf_op jit(solution)/shard_map/jit(_solve_triangular)/triangular_solve | solution.py:129
  (86 shorter events, 23.0 us)
Async XLA Ops:
  0.6 12.7 %copy-start = (bf16[64,3,1,8,128]{4,3,2,1,0:T(8,128)(2,1)S(1)}, bf16[64,3,1,8,128]{4,3,2,1,0:T(8,128)(2,1)}, u32[]{:S(2)}) copy-start(bf16[64,3,1,8,128]{4,3,2,1,0:T(8,128)(2,1)} %param.6) | copy-start | bytes 1179652
  0.6 27.5 %collective-permute-start.2 = (s32[256]{0:T(256)}, s32[256]{0:T(256)S(1)}, u32[]{:S(2)}, u32[]{:S(2)}) collective-permute-start(s32[256]{0:T(256)} %bitcast.99), channel_id=1, source_target_pairs={{0,6},{1,7},{2,4},{3,5},{4,2},{5,3},{6,0},{7,1},{8,14},{9,15},{10,... | collective-permute-start | bytes 3080 | tf_op jit(solution)/shard_map/ppermute | solution.py:52
  4.6 23.5 %collective-permute-start.1 = (s32[256]{0:T(256)}, s32[256]{0:T(256)S(1)}, u32[]{:S(2)}, u32[]{:S(2)}) collective-permute-start(s32[256]{0:T(256)} %bitcast.100), channel_id=1, source_target_pairs={{0,4},{1,5},{2,6},{3,7},{4,0},{5,1},{6,2},{7,3},{8,12},{9,13},{10,... | collective-permute-start | bytes 3080 | tf_op jit(solution)/shard_map/ppermute | solution.py:52
  5.1 23.0 %collective-permute-start = (s32[256]{0:T(256)}, s32[256]{0:T(256)S(1)}, u32[]{:S(2)}, u32[]{:S(2)}) collective-permute-start(s32[256]{0:T(256)} %bitcast.101), channel_id=1, source_target_pairs={{0,2},{1,3},{2,0},{3,1},{4,6},{5,7},{6,4},{7,5},{8,10},{9,11},{10,... | collective-permute-start | bytes 3080 | tf_op jit(solution)/shard_map/ppermute | solution.py:52
  6.4 8.4 %collective-permute-start.7 = (bf16[64,2,1,128]{3,2,1,0:T(2,128)(2,1)S(1)}, bf16[64,2,1,128]{3,2,1,0:T(2,128)(2,1)S(1)}, u32[]{:S(2)}, u32[]{:S(2)}) collective-permute-start(bf16[64,2,1,128]{3,2,1,0:T(2,128)(2,1)S(1)} %get-tuple-element.33), channel_id=1, source_target_pairs={{8,0},{16,8},{24,16},{9,1},{17,9},{25,17},{10,2},{18,10},{26,18},{... | collective-permute-start | bytes 98312 | tf_op jit(solution)/shard_map/ppermute | solution.py:23
  7.7 8.4 %collective-permute-start.6 = (bf16[64,2,1,128]{3,2,1,0:T(2,128)(2,1)S(1)}, bf16[64,2,1,128]{3,2,1,0:T(2,128)(2,1)S(1)}, u32[]{:S(2)}, u32[]{:S(2)}) collective-permute-start(bf16[64,2,1,128]{3,2,1,0:T(2,128)(2,1)S(1)} %get-tuple-element.32), channel_id=1, source_target_pairs={{0,8},{8,16},{16,24},{1,9},{9,17},{17,25},{2,10},{10,18},{18,26},{... | collective-permute-start | bytes 98312 | tf_op jit(solution)/shard_map/ppermute | solution.py:23
  13.6 1.0 copy-start.3
  14.8 3.0 %collective-permute-start.5 = (bf16[64,2,8,128]{3,2,1,0:T(8,128)(2,1)S(1)}, bf16[64,2,8,128]{3,2,1,0:T(8,128)(2,1)S(1)}, u32[]{:S(2)}, u32[]{:S(2)}) collective-permute-start(bf16[64,2,8,128]{3,2,1,0:T(8,128)(2,1)S(1)} %get-tuple-element.30), channel_id=1, source_target_pairs={{0,1},{1,2},{2,3},{3,4},{4,5},{5,6},{6,7},{8,9},{9,10},{10,11},{11... | collective-permute-start | bytes 786440 | tf_op jit(solution)/shard_map/ppermute | solution.py:23
  16.1 5.5 %collective-permute-start.4 = (bf16[64,2,8,128]{3,2,1,0:T(8,128)(2,1)S(1)}, bf16[64,2,8,128]{3,2,1,0:T(8,128)(2,1)S(1)}, u32[]{:S(2)}, u32[]{:S(2)}) collective-permute-start(bf16[64,2,8,128]{3,2,1,0:T(8,128)(2,1)S(1)} %get-tuple-element.30), channel_id=1, source_target_pairs={{1,0},{2,1},{3,2},{4,3},{5,4},{6,5},{7,6},{9,8},{10,9},{11,10},{12... | collective-permute-start | bytes 786440 | tf_op jit(solution)/shard_map/ppermute | solution.py:23
  21.7 1.0 copy-start.2
  21.9 6.2 %copy-start.4 = (s32[1,1,256]{2,1,0:T(1,128)S(1)}, s32[1,1,256]{2,1,0:T(1,128)}, u32[]{:S(2)}) copy-start(s32[1,1,256]{2,1,0:T(1,128)} %param.9) | copy-start | bytes 3076
  22.8 6.2 %collective-permute-start.3 = (bf16[192,1024]{1,0:T(8,128)(2,1)S(1)}, bf16[192,1024]{1,0:T(8,128)(2,1)S(1)}, u32[]{:S(2)}, u32[]{:S(2)}) collective-permute-start(bf16[192,1024]{1,0:T(8,128)(2,1)S(1)} %get-tuple-element.45), channel_id=1, source_target_pairs={{0,1},{1,0},{2,3},{3,2},{4,5},{5,4},{6,7},{7,6},{8,9},{9,8},{10,11... | collective-permute-start | bytes 1179656 | tf_op jit(solution)/shard_map/ppermute | solution.py:68
  28.0 2.7 %collective-permute-start.8 = (bf16[192,1024]{1,0:T(8,128)(2,1)S(1)}, bf16[192,1024]{1,0:T(8,128)(2,1)S(1)}, u32[]{:S(2)}, u32[]{:S(2)}) collective-permute-start(bf16[192,1024]{1,0:T(8,128)(2,1)S(1)} %get-tuple-element.44), channel_id=1, source_target_pairs={{0,1},{1,0},{2,3},{3,2},{4,5},{5,4},{6,7},{7,6},{8,9},{9,8},{10,11... | collective-permute-start | bytes 1179656 | tf_op jit(solution)/shard_map/ppermute | solution.py:68
  32.5 10.1 %collective-permute-start.11 = (f32[256,256]{0,1:T(8,128)S(1)}, f32[256,256]{0,1:T(8,128)S(1)}, u32[]{:S(2)}, u32[]{:S(2)}) collective-permute-start(f32[256,256]{0,1:T(8,128)S(1)} %get-tuple-element.25), channel_id=1, source_target_pairs={{0,6},{1,7},{2,4},{3,5},{4,2},{5,3},{6,0},{7,1},{8,14},{9,15},{10,... | collective-permute-start | bytes 786440 | tf_op jit(solution)/shard_map/ppermute | solution.py:77
  33.5 14.1 %collective-permute-start.10 = (f32[256,256]{0,1:T(8,128)S(1)}, f32[256,256]{0,1:T(8,128)S(1)}, u32[]{:S(2)}, u32[]{:S(2)}) collective-permute-start(f32[256,256]{0,1:T(8,128)S(1)} %get-tuple-element.26), channel_id=1, source_target_pairs={{0,4},{1,5},{2,6},{3,7},{4,0},{5,1},{6,2},{7,3},{8,12},{9,13},{10,... | collective-permute-start | bytes 786440 | tf_op jit(solution)/shard_map/ppermute | solution.py:77
  36.4 11.3 %collective-permute-start.9 = (f32[256,256]{0,1:T(8,128)S(1)}, f32[256,256]{0,1:T(8,128)S(1)}, u32[]{:S(2)}, u32[]{:S(2)}) collective-permute-start(f32[256,256]{0,1:T(8,128)S(1)} %get-tuple-element.24), channel_id=1, source_target_pairs={{0,2},{1,3},{2,0},{3,1},{4,6},{5,7},{6,4},{7,5},{8,10},{9,11},{10,... | collective-permute-start | bytes 786440 | tf_op jit(solution)/shard_map/ppermute | solution.py:77
  48.4 1.4 %collective-permute-start.12 = (f32[128,256]{0,1:T(8,128)S(1)}, f32[128,256]{0,1:T(8,128)S(1)}, u32[]{:S(2)}, u32[]{:S(2)}) collective-permute-start(f32[128,256]{0,1:T(8,128)S(1)} %slice_select_fusion), channel_id=1, source_target_pairs={{0,1},{1,0},{2,3},{3,2},{4,5},{5,4},{6,7},{7,6},{8,9},{9,8},{10,11... | collective-permute-start | bytes 393224 | tf_op jit(solution)/shard_map/ppermute | solution.py:105
  49.8 7.3 %collective-permute-start.15 = (f32[128,256]{0,1:T(8,128)S(1)}, f32[128,256]{0,1:T(8,128)S(1)}, u32[]{:S(2)}, u32[]{:S(2)}) collective-permute-start(f32[128,256]{0,1:T(8,128)S(1)} %select_add_fusion), channel_id=1, source_target_pairs={{0,6},{1,7},{2,4},{3,5},{4,2},{5,3},{6,0},{7,1},{8,14},{9,15},{10,... | collective-permute-start | bytes 393224 | tf_op jit(solution)/shard_map/ppermute | solution.py:106
  52.2 6.9 %collective-permute-start.13 = (f32[128,256]{0,1:T(8,128)S(1)}, f32[128,256]{0,1:T(8,128)S(1)}, u32[]{:S(2)}, u32[]{:S(2)}) collective-permute-start(f32[128,256]{0,1:T(8,128)S(1)} %select_add_fusion), channel_id=1, source_target_pairs={{0,2},{1,3},{2,0},{3,1},{4,6},{5,7},{6,4},{7,5},{8,10},{9,11},{10,... | collective-permute-start | bytes 393224 | tf_op jit(solution)/shard_map/ppermute | solution.py:106
  52.8 6.4 %collective-permute-start.14 = (f32[128,256]{0,1:T(8,128)S(1)}, f32[128,256]{0,1:T(8,128)S(1)}, u32[]{:S(2)}, u32[]{:S(2)}) collective-permute-start(f32[128,256]{0,1:T(8,128)S(1)} %select_add_fusion), channel_id=1, source_target_pairs={{0,4},{1,5},{2,6},{3,7},{4,0},{5,1},{6,2},{7,3},{8,12},{9,13},{10,... | collective-permute-start | bytes 393224 | tf_op jit(solution)/shard_map/ppermute | solution.py:106
  59.2 5.4 %collective-permute-start.18 = (f32[128,256]{0,1:T(8,128)S(1)}, f32[128,256]{0,1:T(8,128)S(1)}, u32[]{:S(2)}, u32[]{:S(2)}) collective-permute-start(f32[128,256]{0,1:T(8,128)S(1)} %add_add_fusion.1), channel_id=1, source_target_pairs={{0,24},{8,0},{16,8},{24,16},{1,25},{9,1},{17,9},{25,17},{2,26},{10... | collective-permute-start | bytes 393224 | tf_op jit(solution)/shard_map/ppermute | solution.py:107
  60.6 9.9 %collective-permute-start.16 = (f32[128,256]{0,1:T(8,128)S(1)}, f32[128,256]{0,1:T(8,128)S(1)}, u32[]{:S(2)}, u32[]{:S(2)}) collective-permute-start(f32[128,256]{0,1:T(8,128)S(1)} %add_add_fusion.1), channel_id=1, source_target_pairs={{0,8},{8,16},{16,24},{24,0},{1,9},{9,17},{17,25},{25,1},{2,10},{10... | collective-permute-start | bytes 393224 | tf_op jit(solution)/shard_map/ppermute | solution.py:107
  61.3 12.5 %collective-permute-start.17 = (f32[128,256]{0,1:T(8,128)S(1)}, f32[128,256]{0,1:T(8,128)S(1)}, u32[]{:S(2)}, u32[]{:S(2)}) collective-permute-start(f32[128,256]{0,1:T(8,128)S(1)} %add_add_fusion.1), channel_id=1, source_target_pairs={{0,16},{8,24},{16,0},{24,8},{1,17},{9,25},{17,1},{25,9},{2,18},{10... | collective-permute-start | bytes 393224 | tf_op jit(solution)/shard_map/ppermute | solution.py:107
  73.8 1.4 %collective-permute-start.19 = (f32[128,256]{0,1:T(8,128)S(1)}, f32[128,256]{0,1:T(8,128)S(1)}, u32[]{:S(2)}, u32[]{:S(2)}) collective-permute-start(f32[128,256]{0,1:T(8,128)S(1)} %add_add_fusion), channel_id=1, source_target_pairs={{0,1},{1,0},{2,3},{3,2},{4,5},{5,4},{6,7},{7,6},{8,9},{9,8},{10,11... | collective-permute-start | bytes 393224 | tf_op jit(solution)/shard_map/ppermute | solution.py:108
  (1 other events, 1.0 us)

commit v2 on v1

--- a/solution.py
+++ b/solution.py
@@ -3,9 +3,13 @@
 import jax
 import jax.numpy as jnp
 from jax import lax
+from jax.experimental import pallas as pl
+from jax.experimental.pallas import tpu as pltpu
 from jax.sharding import PartitionSpec as P
 
 MESH_AXES = ("row", "mix")
+ROWS = 8
+VMEM = pl.BlockSpec(memory_space=pltpu.VMEM)
 
 
 def xor_route(count, bits):
@@ -107,6 +111,92 @@
     half = half + sum(lax.ppermute(half, "row", turn_route(blocks, k)) for k in range(1, blocks))
     other = lax.ppermute(half, "mix", xor_route(planes, 1))
     return jnp.concatenate([jnp.where(core == 0, half, other), jnp.where(core == 0, other, half)])
+
+
+def product(a, b, dims):
+    return lax.dot_general(
+        a, b, (dims, ((), ())), precision=lax.Precision.HIGHEST, preferred_element_type=jnp.float32
+    )
+
+
+def eliminate(a_ref, z_ref):
+    n = a_ref.shape[0]
+    row = lax.broadcasted_iota(jnp.int32, (ROWS, n), 0)
+    lane = lax.broadcasted_iota(jnp.int32, (ROWS, n), 1)
+
+    def spread(x):
+        return jnp.broadcast_to(x, (ROWS, n))
+
+    def rows_of(ref, start):
+        return ref[start : start + ROWS, :]
+
+    for start in range(0, n, ROWS):
+        z_ref[start : start + ROWS, :] = jnp.where(lane == row + start, 1.0, 0.0)
+    for start in range(0, n, ROWS):
+        block, block_z = rows_of(a_ref, start), rows_of(z_ref, start)
+        columns = [spread(block[:, start + c : start + c + 1]) for c in range(ROWS)]
+        pivots = {(k, c): spread(columns[c][k : k + 1, :]) for c in range(ROWS) for k in range(c + 1)}
+        top = [spread(block[k : k + 1, :]) for k in range(ROWS)]
+        top_z = [spread(block_z[k : k + 1, :]) for k in range(ROWS)]
+        inverse = []
+        for k in range(ROWS):
+            inverse.append(1.0 / pivots[k, k])
+            for i in range(k + 1, ROWS):
+                times = pivots[k, i] * inverse[k]
+                for c in range(i, ROWS):
+                    pivots[i, c] = pivots[i, c] - times * pivots[k, c]
+                top[i] = top[i] - times * top[k]
+                top_z[i] = top_z[i] - times * top_z[k]
+        for below in range(start + ROWS, n, ROWS):
+            rest, rest_z = rows_of(a_ref, below), rows_of(z_ref, below)
+            columns = [spread(rest[:, start + c : start + c + 1]) for c in range(ROWS)]
+            for k in range(ROWS):
+                times = columns[k] * inverse[k]
+                for c in range(k + 1, ROWS):
+                    columns[c] = columns[c] - times * pivots[k, c]
+                rest = rest - times * top[k]
+                rest_z = rest_z - times * top_z[k]
+            a_ref[below : below + ROWS, :] = rest
+            z_ref[below : below + ROWS, :] = rest_z
+        done, done_z = jnp.zeros_like(block), jnp.zeros_like(block)
+        for k in range(ROWS):
+            scale = lax.rsqrt(pivots[k, k])
+            done = jnp.where(row == k, top[k] * scale, done)
+            done_z = jnp.where(row == k, top_z[k] * scale, done_z)
+        a_ref[start : start + ROWS, :] = jnp.where(lane >= row + start, done, 0.0)
+        z_ref[start : start + ROWS, :] = done_z
+
+
+def finish_kernel(gram_ref, picked_ref, basis_ref, factor_ref, a_ref, first_ref, second_ref):
+    half = a_ref.shape[0]
+    nn, nt = ((1,), (0,)), ((1,), (1,))
+    a_ref[...] = gram_ref[:half, :half]
+    eliminate(a_ref, first_ref)
+    first = first_ref[...]
+    across = product(first, gram_ref[:half, half:], nn)
+    down = product(gram_ref[half:, :half], first, nt)
+    factor_ref[:half, :half] = a_ref[...]
+    factor_ref[:half, half:] = across
+    factor_ref[half:, :half] = jnp.zeros_like(across)
+    a_ref[...] = gram_ref[half:, half:] - product(down, across, nn)
+    solved = product(picked_ref[:, :half], first, nt)
+    basis_ref[:, :half] = solved
+    left_over = picked_ref[:, half:] - product(solved, across, nn)
+    eliminate(a_ref, second_ref)
+    basis_ref[:, half:] = product(left_over, second_ref[...], nt)
+    factor_ref[half:, half:] = a_ref[...]
+
+
+def finish(gram, picked):
+    n = gram.shape[0]
+    return pl.pallas_call(
+        finish_kernel,
+        out_shape=(jax.ShapeDtypeStruct(picked.shape, jnp.float32), jax.ShapeDtypeStruct(gram.shape, jnp.float32)),
+        in_specs=[VMEM] * 2,
+        out_specs=[VMEM] * 2,
+        scratch_shapes=[pltpu.VMEM((n // 2, n // 2), jnp.float32)] * 3,
+        name="finish",
+    )(gram, picked)
 
 
 def on_device(velocity, field_b, test_signs, row_signs, sample_index):
@@ -125,9 +215,8 @@
     gram = jnp.einsum(
         "ik,jk->ij", picked, picked, precision=lax.Precision.HIGHEST, preferred_element_type=jnp.float32
     ) * (1.0 / (planes * blocks * samples))
-    lower = jnp.linalg.cholesky(sum_over_mesh(gram))
-    solved = jax.scipy.linalg.solve_triangular(lower, picked, lower=True)
-    return solved.T.reshape(sample_index.shape + (sketch_width,)), lower.T
+    basis_rows, factor = finish(sum_over_mesh(gram), picked.T)
+    return basis_rows.reshape(sample_index.shape + (sketch_width,)), factor
 
 
 def solution(mesh):

time: 139 us -> 87.5 us (0.63)
  other arithmetic: 56 us -> 2.28 us
  Pallas kernels: 0 us -> 11.3 us
  local copies, waits for them, and re-layouts: 10 us -> 4.11 us
  matrix products: 5.42 us -> 3.94 us
  between operations: 2.4 us -> 0.98 us
    another operation x10 -> x1, other arithmetic: 54.4 us -> 0.1 us  [the longest x7 34.6 us: on_device(): lower = jnp.linalg.cholesky(sum_over_mesh(gram))]
    pallas_call x0 -> x1, Pallas kernels: none -> 11.3 us  [finish(): pl.pallas_call(finish_kernel, out_shape=(jax.ShapeDtypeStruct(picked.shap...]
    another operation x9 -> x0, local copies, waits for them, and re-layouts: 4.1 us -> none
    unnamed x12, local copies, waits for them, and re-layouts: 3.19 us -> 1.52 us
    another operation x5 -> x0, matrix products: 1.48 us -> none  [the longest x3 1.01 us: on_device(): solved = jax.scipy.linalg.solve_triangular(lower, picked, lower=True)]
  transfers between devices with their start and end apart: 20 -> 20, of which waited for: 11 -> 11; matrix products, arithmetic and copies ran while one was open for 4% -> 6% of each run, Pallas kernels for 0% -> 0%
where the time goes in v2:
time: 87.5 us; the launch traced here: 87.3 us
  waiting for transfers between devices  34.4 us (39%)
  starting transfers between devices  30.3 us (35%)
  Pallas kernels  11.3 us (13%)
  local copies, waits for them, and re-layouts  4.11 us (5%)
  matrix products  3.94 us (5%)
  other arithmetic  2.28 us (3%)
  between operations  0.98 us (1%)
    ppermute x3, waiting for transfers between devices, sampled_mixing(): arrived = lax.ppermute(parts[slot + 1], 'mix', xor_route(planes, k))  11.3 us
    pallas_call x1, Pallas kernels, finish(): pl.pallas_call(finish_kernel, out_shape=(jax.ShapeDtypeStruct(picked.shap...  11.3 us
    ppermute x3, waiting for transfers between devices, sum_over_mesh(): lax.ppermute(half, 'row', turn_route(blocks, k))  9.89 us
    ppermute x4, starting transfers between devices, neighbours(): return (lax.ppermute(last, axis, up), lax.ppermute(first, axis, down))  8.44 us
    ppermute x3, waiting for transfers between devices, sum_over_mesh(): lax.ppermute(half, 'mix', xor_route(planes, k))  5.77 us
    ppermute x2, starting transfers between devices, part_sum(): other = lax.ppermute(own, 'mix', xor_route(planes, 1))  4.96 us
    ppermute x3, starting transfers between devices, sum_over_mesh(): lax.ppermute(half, 'row', turn_route(blocks, k))  4.67 us
    ppermute x3, starting transfers between devices, sampled_mixing(): lax.ppermute(sample_index, 'mix', xor_route(planes, k))  4.6 us
  transfers between devices with their start and end apart: 20, of which 11 were waited for; matrix products, arithmetic and copies ran while one was open for 6% of the time, Pallas kernels for 0%

profile of v2, /device:TPU:0, one launch (start us, length us, event | category | flops | bytes accessed | tf_op | source)
XLA Modules:
  0.0 87.3 jit_solution(8004832646893095964)
XLA Ops:
  0.6 4.0 %collective-permute-start.2 = (s32[256]{0:T(256)}, s32[256]{0:T(256)S(1)}, u32[]{:S(2)}, u32[]{:S(2)}) collective-permute-start(s32[256]{0:T(256)} %bitcast.66), channel_id=1, source_target_pairs={{0,6},{1,7},{2,4},{3,5},{4,2},{5,3},{6,0},{7,1},{8,14},{9,15},{10,... | collective-permute-start | bytes 3080 | tf_op jit(solution)/shard_map/ppermute | solution.py:56
  5.2 1.1 %fusion.53 = (bf16[64,2,1,128]{3,2,1,0:T(2,128)(2,1)S(1)}, bf16[64,2,1,128]{3,2,1,0:T(2,128)(2,1)S(1)}) fusion(bf16[64,3,8,128]{3,2,1,0:T(8,128)(2,1)} %bitcast.61), kind=kLoop, calls=%fused_computation.67 | loop fusion | bytes 131072 | tf_op jit(solution)/shard_map/slice | solution.py:33
  6.4 1.3 %collective-permute-start.7 = (bf16[64,2,1,128]{3,2,1,0:T(2,128)(2,1)S(1)}, bf16[64,2,1,128]{3,2,1,0:T(2,128)(2,1)S(1)}, u32[]{:S(2)}, u32[]{:S(2)}) collective-permute-start(bf16[64,2,1,128]{3,2,1,0:T(2,128)(2,1)S(1)} %get-tuple-element.15), channel_id=1, source_target_pairs={{8,0},{16,8},{24,16},{9,1},{17,9},{25,17},{10,2},{18,10},{26,18},{... | collective-permute-start | bytes 98312 | tf_op jit(solution)/shard_map/ppermute | solution.py:27
  7.7 4.5 %collective-permute-start.6 = (bf16[64,2,1,128]{3,2,1,0:T(2,128)(2,1)S(1)}, bf16[64,2,1,128]{3,2,1,0:T(2,128)(2,1)S(1)}, u32[]{:S(2)}, u32[]{:S(2)}) collective-permute-start(bf16[64,2,1,128]{3,2,1,0:T(2,128)(2,1)S(1)} %get-tuple-element.14), channel_id=1, source_target_pairs={{0,8},{8,16},{16,24},{1,9},{9,17},{17,25},{2,10},{10,18},{18,26},{... | collective-permute-start | bytes 98312 | tf_op jit(solution)/shard_map/ppermute | solution.py:27
  12.2 1.1 %fusion.52 = (bf16[64,2,8,128]{3,2,1,0:T(8,128)(2,1)S(1)}, bf16[64,2,8,128]{3,2,1,0:T(8,128)(2,1)S(1)}) fusion(bf16[64,3,8,128]{3,2,1,0:T(8,128)(2,1)} %bitcast.62), kind=kLoop, calls=%fused_computation.66 | loop fusion | bytes 1048576 | tf_op jit(solution)/shard_map/slice | solution.py:32
  14.8 1.3 %collective-permute-start.5 = (bf16[64,2,8,128]{3,2,1,0:T(8,128)(2,1)S(1)}, bf16[64,2,8,128]{3,2,1,0:T(8,128)(2,1)S(1)}, u32[]{:S(2)}, u32[]{:S(2)}) collective-permute-start(bf16[64,2,8,128]{3,2,1,0:T(8,128)(2,1)S(1)} %get-tuple-element.12), channel_id=1, source_target_pairs={{0,1},{1,2},{2,3},{3,4},{4,5},{5,6},{6,7},{8,9},{9,10},{10,11},{11... | collective-permute-start | bytes 786440 | tf_op jit(solution)/shard_map/ppermute | solution.py:27
  16.1 1.3 %collective-permute-start.4 = (bf16[64,2,8,128]{3,2,1,0:T(8,128)(2,1)S(1)}, bf16[64,2,8,128]{3,2,1,0:T(8,128)(2,1)S(1)}, u32[]{:S(2)}, u32[]{:S(2)}) collective-permute-start(bf16[64,2,8,128]{3,2,1,0:T(8,128)(2,1)S(1)} %get-tuple-element.12), channel_id=1, source_target_pairs={{1,0},{2,1},{3,2},{4,3},{5,4},{6,5},{7,6},{9,8},{10,9},{11,10},{12... | collective-permute-start | bytes 786440 | tf_op jit(solution)/shard_map/ppermute | solution.py:27
  17.8 3.9 %collective-permute-done.4 = bf16[64,2,8,128]{3,2,1,0:T(8,128)(2,1)S(1)} collective-permute-done((bf16[64,2,8,128]{3,2,1,0:T(8,128)(2,1)S(1)}, bf16[64,2,8,128]{3,2,1,0:T(8,128)(2,1)S(1)}, u32[]{:S(2)}, u32[]{:S(2)}) %collective-permute-start.4) | collective-permute-done | bytes 262176 | tf_op jit(solution)/shard_map/ppermute | solution.py:27
  22.8 4.9 %collective-permute-start.3 = (bf16[192,1024]{1,0:T(8,128)(2,1)S(1)}, bf16[192,1024]{1,0:T(8,128)(2,1)S(1)}, u32[]{:S(2)}, u32[]{:S(2)}) collective-permute-start(bf16[192,1024]{1,0:T(8,128)(2,1)S(1)} %get-tuple-element.21), channel_id=1, source_target_pairs={{0,1},{1,0},{2,3},{3,2},{4,5},{5,4},{6,7},{7,6},{8,9},{9,8},{10,11... | collective-permute-start | bytes 1179656 | tf_op jit(solution)/shard_map/ppermute | solution.py:72
  29.0 1.7 %fusion.21 = f32[4,256,256]{2,1,0:T(8,128)S(1)} fusion(s32[4,256]{1,0:T(4,128)S(1)} %pad_add_fusion, bf16[192,1024]{1,0:T(8,128)(2,1)S(1)} %collective-permute-done.3, bf16[192,1024]{1,0:T(8,128)(2,1)S(1)} %get-tuple-element.21, bf16[192,256]{1,0:T(8,128)(2,1)S(1)} %reshape.28, bf16[192,256]{1,0:T(8,128)(2,1)S(1)} %get-tuple-element.23), kind=kOutput, calls=%fused_computation.12 | convolution fusion | flops 1011089408 | bytes 2035712 | tf_op jit(solution)/shard_map/sj,tsk->tjk/dot_general | solution.py:76
  30.7 1.7 %fusion.13 = f32[4,256,256]{1,2,0:T(8,128)S(1)} fusion(f32[4,256,256]{2,1,0:T(8,128)S(1)} %fusion.21, s32[4,256]{1,0:T(4,128)S(1)} %pad_add_fusion, bf16[192,1024]{1,0:T(8,128)(2,1)S(1)} %collective-permute-done.8, bf16[192,1024]{1,0:T(8,128)(2,1)S(1)} %get-tuple-element.20, bf16[192,256]{1,0:T(8,128)(2,1)S(1)} %reshape.29, ...), kind=kOutput, calls=%fused_computation.9 | convolution fusion | flops 1011351552 | bytes 3084288 | tf_op jit(solution)/shard_map/sj,tsk->tjk/dot_general | solution.py:76
  33.5 2.8 %collective-permute-start.10 = (f32[256,256]{0,1:T(8,128)S(1)}, f32[256,256]{0,1:T(8,128)S(1)}, u32[]{:S(2)}, u32[]{:S(2)}) collective-permute-start(f32[256,256]{0,1:T(8,128)S(1)} %get-tuple-element.8), channel_id=1, source_target_pairs={{0,4},{1,5},{2,6},{3,7},{4,0},{5,1},{6,2},{7,3},{8,12},{9,13},{10,... | collective-permute-start | bytes 786440 | tf_op jit(solution)/shard_map/ppermute | solution.py:81
  36.4 6.3 %collective-permute-done.11 = f32[256,256]{0,1:T(8,128)S(1)} collective-permute-done((f32[256,256]{0,1:T(8,128)S(1)}, f32[256,256]{0,1:T(8,128)S(1)}, u32[]{:S(2)}, u32[]{:S(2)}) %collective-permute-start.11) | collective-permute-done | bytes 262176 | tf_op jit(solution)/shard_map/ppermute | solution.py:81
  42.6 5.0 %collective-permute-done.10 = f32[256,256]{0,1:T(8,128)S(1)} collective-permute-done((f32[256,256]{0,1:T(8,128)S(1)}, f32[256,256]{0,1:T(8,128)S(1)}, u32[]{:S(2)}, u32[]{:S(2)}) %collective-permute-start.10) | collective-permute-done | bytes 262176 | tf_op jit(solution)/shard_map/ppermute | solution.py:81
  48.5 1.3 %collective-permute-done.12 = f32[128,256]{1,0:T(8,128)S(1)} collective-permute-done((f32[128,256]{1,0:T(8,128)S(1)}, f32[128,256]{1,0:T(8,128)S(1)}, u32[]{:S(2)}, u32[]{:S(2)}) %collective-permute-start.12) | collective-permute-done | bytes 131104 | tf_op jit(solution)/shard_map/ppermute | solution.py:109
  49.8 2.4 %collective-permute-start.15 = (f32[128,256]{1,0:T(8,128)S(1)}, f32[128,256]{1,0:T(8,128)S(1)}, u32[]{:S(2)}, u32[]{:S(2)}) collective-permute-start(f32[128,256]{1,0:T(8,128)S(1)} %select_add_fusion), channel_id=1, source_target_pairs={{0,6},{1,7},{2,4},{3,5},{4,2},{5,3},{6,0},{7,1},{8,14},{9,15},{10,... | collective-permute-start | bytes 393224 | tf_op jit(solution)/shard_map/ppermute | solution.py:110
  53.4 3.7 %collective-permute-done.15 = f32[128,256]{1,0:T(8,128)S(1)} collective-permute-done((f32[128,256]{1,0:T(8,128)S(1)}, f32[128,256]{1,0:T(8,128)S(1)}, u32[]{:S(2)}, u32[]{:S(2)}) %collective-permute-start.15) | collective-permute-done | bytes 131104 | tf_op jit(solution)/shard_map/ppermute | solution.py:110
  57.1 2.0 %collective-permute-done.13 = f32[128,256]{1,0:T(8,128)S(1)} collective-permute-done((f32[128,256]{1,0:T(8,128)S(1)}, f32[128,256]{1,0:T(8,128)S(1)}, u32[]{:S(2)}, u32[]{:S(2)}) %collective-permute-start.13) | collective-permute-done | bytes 131104 | tf_op jit(solution)/shard_map/ppermute | solution.py:110
  59.2 1.5 %collective-permute-start.18 = (f32[128,256]{1,0:T(8,128)S(1)}, f32[128,256]{1,0:T(8,128)S(1)}, u32[]{:S(2)}, u32[]{:S(2)}) collective-permute-start(f32[128,256]{1,0:T(8,128)S(1)} %add_add_fusion.1), channel_id=1, source_target_pairs={{0,24},{8,0},{16,8},{24,16},{1,25},{9,1},{17,9},{25,17},{2,26},{10... | collective-permute-start | bytes 393224 | tf_op jit(solution)/shard_map/ppermute | solution.py:111
  61.3 2.6 %collective-permute-start.17 = (f32[128,256]{1,0:T(8,128)S(1)}, f32[128,256]{1,0:T(8,128)S(1)}, u32[]{:S(2)}, u32[]{:S(2)}) collective-permute-start(f32[128,256]{1,0:T(8,128)S(1)} %add_add_fusion.1), channel_id=1, source_target_pairs={{0,16},{8,24},{16,0},{24,8},{1,17},{9,25},{17,1},{25,9},{2,18},{10... | collective-permute-start | bytes 393224 | tf_op jit(solution)/shard_map/ppermute | solution.py:111
  64.6 6.0 %collective-permute-done.16 = f32[128,256]{1,0:T(8,128)S(1)} collective-permute-done((f32[128,256]{1,0:T(8,128)S(1)}, f32[128,256]{1,0:T(8,128)S(1)}, u32[]{:S(2)}, u32[]{:S(2)}) %collective-permute-start.16) | collective-permute-done | bytes 131104 | tf_op jit(solution)/shard_map/ppermute | solution.py:111
  70.6 3.2 %collective-permute-done.17 = f32[128,256]{1,0:T(8,128)S(1)} collective-permute-done((f32[128,256]{1,0:T(8,128)S(1)}, f32[128,256]{1,0:T(8,128)S(1)}, u32[]{:S(2)}, u32[]{:S(2)}) %collective-permute-start.17) | collective-permute-done | bytes 131104 | tf_op jit(solution)/shard_map/ppermute | solution.py:111
  73.9 1.3 %collective-permute-done.19 = f32[128,256]{1,0:T(8,128)S(1)} collective-permute-done((f32[128,256]{1,0:T(8,128)S(1)}, f32[128,256]{1,0:T(8,128)S(1)}, u32[]{:S(2)}, u32[]{:S(2)}) %collective-permute-start.19) | collective-permute-done | bytes 131104 | tf_op jit(solution)/shard_map/ppermute | solution.py:112
  76.0 11.3 %finish.1 = (f32[256,256]{1,0:T(8,128)}, f32[256,256]{1,0:T(8,128)}) custom-call(f32[256,256]{1,0:T(8,128)} %pad_maximum_fusion.1.gram_ref, f32[256,256]{1,0:T(8,128)} %bitcast.60), custom_call_target="tpu_custom_call" | custom-call | tf_op jit(solution)/shard_map/finish/pallas_call | solution.py:192
  (58 shorter events, 10.3 us)
Async XLA Ops:
  0.6 12.7 %copy-start.1 = (bf16[64,3,1,8,128]{4,3,2,1,0:T(8,128)(2,1)S(1)}, bf16[64,3,1,8,128]{4,3,2,1,0:T(8,128)(2,1)}, u32[]{:S(2)}) copy-start(bf16[64,3,1,8,128]{4,3,2,1,0:T(8,128)(2,1)} %param.6) | copy-start | bytes 1179652
  0.6 27.5 %collective-permute-start.2 = (s32[256]{0:T(256)}, s32[256]{0:T(256)S(1)}, u32[]{:S(2)}, u32[]{:S(2)}) collective-permute-start(s32[256]{0:T(256)} %bitcast.66), channel_id=1, source_target_pairs={{0,6},{1,7},{2,4},{3,5},{4,2},{5,3},{6,0},{7,1},{8,14},{9,15},{10,... | collective-permute-start | bytes 3080 | tf_op jit(solution)/shard_map/ppermute | solution.py:56
  4.6 23.5 %collective-permute-start.1 = (s32[256]{0:T(256)}, s32[256]{0:T(256)S(1)}, u32[]{:S(2)}, u32[]{:S(2)}) collective-permute-start(s32[256]{0:T(256)} %bitcast.67), channel_id=1, source_target_pairs={{0,4},{1,5},{2,6},{3,7},{4,0},{5,1},{6,2},{7,3},{8,12},{9,13},{10,... | collective-permute-start | bytes 3080 | tf_op jit(solution)/shard_map/ppermute | solution.py:56
  5.1 23.0 %collective-permute-start = (s32[256]{0:T(256)}, s32[256]{0:T(256)S(1)}, u32[]{:S(2)}, u32[]{:S(2)}) collective-permute-start(s32[256]{0:T(256)} %bitcast.68), channel_id=1, source_target_pairs={{0,2},{1,3},{2,0},{3,1},{4,6},{5,7},{6,4},{7,5},{8,10},{9,11},{10,... | collective-permute-start | bytes 3080 | tf_op jit(solution)/shard_map/ppermute | solution.py:56
  6.4 8.4 %collective-permute-start.7 = (bf16[64,2,1,128]{3,2,1,0:T(2,128)(2,1)S(1)}, bf16[64,2,1,128]{3,2,1,0:T(2,128)(2,1)S(1)}, u32[]{:S(2)}, u32[]{:S(2)}) collective-permute-start(bf16[64,2,1,128]{3,2,1,0:T(2,128)(2,1)S(1)} %get-tuple-element.15), channel_id=1, source_target_pairs={{8,0},{16,8},{24,16},{9,1},{17,9},{25,17},{10,2},{18,10},{26,18},{... | collective-permute-start | bytes 98312 | tf_op jit(solution)/shard_map/ppermute | solution.py:27
  7.7 8.4 %collective-permute-start.6 = (bf16[64,2,1,128]{3,2,1,0:T(2,128)(2,1)S(1)}, bf16[64,2,1,128]{3,2,1,0:T(2,128)(2,1)S(1)}, u32[]{:S(2)}, u32[]{:S(2)}) collective-permute-start(bf16[64,2,1,128]{3,2,1,0:T(2,128)(2,1)S(1)} %get-tuple-element.14), channel_id=1, source_target_pairs={{0,8},{8,16},{16,24},{1,9},{9,17},{17,25},{2,10},{10,18},{18,26},{... | collective-permute-start | bytes 98312 | tf_op jit(solution)/shard_map/ppermute | solution.py:27
  13.6 1.0 %copy-start.4 = (s32[1,8,128]{2,1,0:T(8,128)S(1)}, s32[1,8,128]{2,1,0:T(8,128)}, u32[]{:S(2)}) copy-start(s32[1,8,128]{2,1,0:T(8,128)} %param.8) | copy-start | bytes 12292
  14.8 3.0 %collective-permute-start.5 = (bf16[64,2,8,128]{3,2,1,0:T(8,128)(2,1)S(1)}, bf16[64,2,8,128]{3,2,1,0:T(8,128)(2,1)S(1)}, u32[]{:S(2)}, u32[]{:S(2)}) collective-permute-start(bf16[64,2,8,128]{3,2,1,0:T(8,128)(2,1)S(1)} %get-tuple-element.12), channel_id=1, source_target_pairs={{0,1},{1,2},{2,3},{3,4},{4,5},{5,6},{6,7},{8,9},{9,10},{10,11},{11... | collective-permute-start | bytes 786440 | tf_op jit(solution)/shard_map/ppermute | solution.py:27
  16.1 5.5 %collective-permute-start.4 = (bf16[64,2,8,128]{3,2,1,0:T(8,128)(2,1)S(1)}, bf16[64,2,8,128]{3,2,1,0:T(8,128)(2,1)S(1)}, u32[]{:S(2)}, u32[]{:S(2)}) collective-permute-start(bf16[64,2,8,128]{3,2,1,0:T(8,128)(2,1)S(1)} %get-tuple-element.12), channel_id=1, source_target_pairs={{1,0},{2,1},{3,2},{4,3},{5,4},{6,5},{7,6},{9,8},{10,9},{11,10},{12... | collective-permute-start | bytes 786440 | tf_op jit(solution)/shard_map/ppermute | solution.py:27
  21.9 6.2 %copy-start.5 = (s32[1,1,256]{2,1,0:T(1,128)S(1)}, s32[1,1,256]{2,1,0:T(1,128)}, u32[]{:S(2)}) copy-start(s32[1,1,256]{2,1,0:T(1,128)} %param.9) | copy-start | bytes 3076
  22.8 6.2 %collective-permute-start.3 = (bf16[192,1024]{1,0:T(8,128)(2,1)S(1)}, bf16[192,1024]{1,0:T(8,128)(2,1)S(1)}, u32[]{:S(2)}, u32[]{:S(2)}) collective-permute-start(bf16[192,1024]{1,0:T(8,128)(2,1)S(1)} %get-tuple-element.21), channel_id=1, source_target_pairs={{0,1},{1,0},{2,3},{3,2},{4,5},{5,4},{6,7},{7,6},{8,9},{9,8},{10,11... | collective-permute-start | bytes 1179656 | tf_op jit(solution)/shard_map/ppermute | solution.py:72
  28.0 2.7 %collective-permute-start.8 = (bf16[192,1024]{1,0:T(8,128)(2,1)S(1)}, bf16[192,1024]{1,0:T(8,128)(2,1)S(1)}, u32[]{:S(2)}, u32[]{:S(2)}) collective-permute-start(bf16[192,1024]{1,0:T(8,128)(2,1)S(1)} %get-tuple-element.20), channel_id=1, source_target_pairs={{0,1},{1,0},{2,3},{3,2},{4,5},{5,4},{6,7},{7,6},{8,9},{9,8},{10,11... | collective-permute-start | bytes 1179656 | tf_op jit(solution)/shard_map/ppermute | solution.py:72
  32.5 10.1 %collective-permute-start.11 = (f32[256,256]{0,1:T(8,128)S(1)}, f32[256,256]{0,1:T(8,128)S(1)}, u32[]{:S(2)}, u32[]{:S(2)}) collective-permute-start(f32[256,256]{0,1:T(8,128)S(1)} %get-tuple-element.7), channel_id=1, source_target_pairs={{0,6},{1,7},{2,4},{3,5},{4,2},{5,3},{6,0},{7,1},{8,14},{9,15},{10,... | collective-permute-start | bytes 786440 | tf_op jit(solution)/shard_map/ppermute | solution.py:81
  33.5 14.1 %collective-permute-start.10 = (f32[256,256]{0,1:T(8,128)S(1)}, f32[256,256]{0,1:T(8,128)S(1)}, u32[]{:S(2)}, u32[]{:S(2)}) collective-permute-start(f32[256,256]{0,1:T(8,128)S(1)} %get-tuple-element.8), channel_id=1, source_target_pairs={{0,4},{1,5},{2,6},{3,7},{4,0},{5,1},{6,2},{7,3},{8,12},{9,13},{10,... | collective-permute-start | bytes 786440 | tf_op jit(solution)/shard_map/ppermute | solution.py:81
  36.4 11.3 %collective-permute-start.9 = (f32[256,256]{0,1:T(8,128)S(1)}, f32[256,256]{0,1:T(8,128)S(1)}, u32[]{:S(2)}, u32[]{:S(2)}) collective-permute-start(f32[256,256]{0,1:T(8,128)S(1)} %get-tuple-element.6), channel_id=1, source_target_pairs={{0,2},{1,3},{2,0},{3,1},{4,6},{5,7},{6,4},{7,5},{8,10},{9,11},{10,... | collective-permute-start | bytes 786440 | tf_op jit(solution)/shard_map/ppermute | solution.py:81
  47.8 27.5 %copy-start = (f32[256,256]{0,1:T(8,128)}, f32[256,256]{0,1:T(8,128)S(1)}, u32[]{:S(2)}) copy-start(f32[256,256]{0,1:T(8,128)S(1)} %fusion.39) | copy-start | bytes 786436
  48.4 1.4 %collective-permute-start.12 = (f32[128,256]{1,0:T(8,128)S(1)}, f32[128,256]{1,0:T(8,128)S(1)}, u32[]{:S(2)}, u32[]{:S(2)}) collective-permute-start(f32[128,256]{1,0:T(8,128)S(1)} %slice_select_fusion), channel_id=1, source_target_pairs={{0,1},{1,0},{2,3},{3,2},{4,5},{5,4},{6,7},{7,6},{8,9},{9,8},{10,11... | collective-permute-start | bytes 393224 | tf_op jit(solution)/shard_map/ppermute | solution.py:109
  49.8 7.3 %collective-permute-start.15 = (f32[128,256]{1,0:T(8,128)S(1)}, f32[128,256]{1,0:T(8,128)S(1)}, u32[]{:S(2)}, u32[]{:S(2)}) collective-permute-start(f32[128,256]{1,0:T(8,128)S(1)} %select_add_fusion), channel_id=1, source_target_pairs={{0,6},{1,7},{2,4},{3,5},{4,2},{5,3},{6,0},{7,1},{8,14},{9,15},{10,... | collective-permute-start | bytes 393224 | tf_op jit(solution)/shard_map/ppermute | solution.py:110
  52.2 6.9 %collective-permute-start.13 = (f32[128,256]{1,0:T(8,128)S(1)}, f32[128,256]{1,0:T(8,128)S(1)}, u32[]{:S(2)}, u32[]{:S(2)}) collective-permute-start(f32[128,256]{1,0:T(8,128)S(1)} %select_add_fusion), channel_id=1, source_target_pairs={{0,2},{1,3},{2,0},{3,1},{4,6},{5,7},{6,4},{7,5},{8,10},{9,11},{10,... | collective-permute-start | bytes 393224 | tf_op jit(solution)/shard_map/ppermute | solution.py:110
  52.8 6.4 %collective-permute-start.14 = (f32[128,256]{1,0:T(8,128)S(1)}, f32[128,256]{1,0:T(8,128)S(1)}, u32[]{:S(2)}, u32[]{:S(2)}) collective-permute-start(f32[128,256]{1,0:T(8,128)S(1)} %select_add_fusion), channel_id=1, source_target_pairs={{0,4},{1,5},{2,6},{3,7},{4,0},{5,1},{6,2},{7,3},{8,12},{9,13},{10,... | collective-permute-start | bytes 393224 | tf_op jit(solution)/shard_map/ppermute | solution.py:110
  59.2 5.4 %collective-permute-start.18 = (f32[128,256]{1,0:T(8,128)S(1)}, f32[128,256]{1,0:T(8,128)S(1)}, u32[]{:S(2)}, u32[]{:S(2)}) collective-permute-start(f32[128,256]{1,0:T(8,128)S(1)} %add_add_fusion.1), channel_id=1, source_target_pairs={{0,24},{8,0},{16,8},{24,16},{1,25},{9,1},{17,9},{25,17},{2,26},{10... | collective-permute-start | bytes 393224 | tf_op jit(solution)/shard_map/ppermute | solution.py:111
  60.7 9.9 %collective-permute-start.16 = (f32[128,256]{1,0:T(8,128)S(1)}, f32[128,256]{1,0:T(8,128)S(1)}, u32[]{:S(2)}, u32[]{:S(2)}) collective-permute-start(f32[128,256]{1,0:T(8,128)S(1)} %add_add_fusion.1), channel_id=1, source_target_pairs={{0,8},{8,16},{16,24},{24,0},{1,9},{9,17},{17,25},{25,1},{2,10},{10... | collective-permute-start | bytes 393224 | tf_op jit(solution)/shard_map/ppermute | solution.py:111
  61.3 12.5 %collective-permute-start.17 = (f32[128,256]{1,0:T(8,128)S(1)}, f32[128,256]{1,0:T(8,128)S(1)}, u32[]{:S(2)}, u32[]{:S(2)}) collective-permute-start(f32[128,256]{1,0:T(8,128)S(1)} %add_add_fusion.1), channel_id=1, source_target_pairs={{0,16},{8,24},{16,0},{24,8},{1,17},{9,25},{17,1},{25,9},{2,18},{10... | collective-permute-start | bytes 393224 | tf_op jit(solution)/shard_map/ppermute | solution.py:111
  73.8 1.4 %collective-permute-start.19 = (f32[128,256]{1,0:T(8,128)S(1)}, f32[128,256]{1,0:T(8,128)S(1)}, u32[]{:S(2)}, u32[]{:S(2)}) collective-permute-start(f32[128,256]{1,0:T(8,128)S(1)} %add_add_fusion), channel_id=1, source_target_pairs={{0,1},{1,0},{2,3},{3,2},{4,5},{5,4},{6,7},{7,6},{8,9},{9,8},{10,11... | collective-permute-start | bytes 393224 | tf_op jit(solution)/shard_map/ppermute | solution.py:112
  (2 other events, 2.0 us)

commit v3 on v1

v3 whole, which is shorter than its diff:
```python
import math

import jax
import jax.numpy as jnp
from jax import lax
from jax.experimental import pallas as pl
from jax.experimental.pallas import tpu as pltpu
from jax.sharding import PartitionSpec as P

MESH_AXES = ("row", "mix")
ROWS = 8
LANES = 128
NN, NT, TN = ((1,), (0,)), ((1,), (1,)), ((0,), (0,))
SMEM = pl.BlockSpec(memory_space=pltpu.SMEM)
VMEM = pl.BlockSpec(memory_space=pltpu.VMEM)


def xor_route(count, bits):
    return [(i, i ^ bits) for i in range(count) if i ^ bits < count]


def pair_route(count, first):
    lows = range(first, count - 1, 2)
    return [(i, i + 1) for i in lows] + [(i + 1, i) for i in lows]


def local(kernel, inputs, shapes, scratch=(), megabytes=8, scalars=1):
    return pl.pallas_call(
        kernel,
        out_shape=[jax.ShapeDtypeStruct(shape, dtype) for shape, dtype in shapes],
        in_specs=[SMEM] * scalars + [VMEM] * (len(inputs) - scalars),
        out_specs=[VMEM] * len(shapes),
        scratch_shapes=[pltpu.VMEM(shape, jnp.float32) for shape in scratch],
        compiler_params=pltpu.CompilerParams(vmem_limit_bytes=megabytes << 20),
        name=kernel.__name__,
    )(*inputs)


def lanes_of(ref, x, width):
    return ref[:, x * width : (x + 1) * width]


def to_lanes(source_ref, held_ref, sems, wide_ref, out_ref, signs_ref=None):
    snaps, parts, depth, width = source_ref.shape
    pieces = sems.shape[0]
    step = snaps // pieces
    copies = [
        pltpu.make_async_copy(
            source_ref.at[i * step : (i + 1) * step], held_ref.at[i * step : (i + 1) * step], sems.at[i]
        )
        for i in range(pieces)
    ]
    for copy in copies:
        copy.start()
    tall = step * parts * depth
    for i, copy in enumerate(copies):
        copy.wait()
        values = held_ref[i * step : (i + 1) * step].astype(jnp.float32).reshape(tall, width)
        wide_ref[i * tall : (i + 1) * tall, :] = values
        for c in range(parts):
            for x in range(depth):
                piece = wide_ref[pl.ds(i * tall + c * depth + x, step, stride=parts * depth), :]
                if signs_ref is not None:
                    piece = piece * (2 * signs_ref[x : x + 1, :] - 1).astype(jnp.float32)
                low = c * snaps + i * step
                out_ref[low : low + step, x * width : (x + 1) * width] = piece.astype(out_ref.dtype)


def field_kernel(flags_ref, field_ref, lanes_ref, flat_ref, rim_a_ref, rim_b_ref, held_ref, wide_ref, sems):
    snaps, _, depth, width = field_ref.shape
    to_lanes(field_ref, held_ref, sems, wide_ref, lanes_ref)
    flat_ref[...] = lanes_ref[: 2 * snaps, :]
    odd = flags_ref[1] == 1
    first = lanes_ref[snaps:, :width].astype(jnp.float32)
    last = lanes_ref[snaps:, (depth - 1) * width :].astype(jnp.float32)
    rim_a_ref[...] = jnp.where(odd, first, last).astype(rim_a_ref.dtype)
    rim_b_ref[...] = jnp.where(odd, last, first).astype(rim_b_ref.dtype)


def velocity_kernel(
    flags_ref,
    velocity_ref,
    test_ref,
    signs_ref,
    pair_ref,
    matrix_ref,
    held_ref,
    wide_ref,
    sems,
    bits_ref,
    bits_sem,
    held_signs_ref,
    signs_sem,
):
    snaps, parts = velocity_ref.shape[:2]
    copy_signs = pltpu.make_async_copy(signs_ref, held_signs_ref, signs_sem)
    copy_signs.start()
    copy = pltpu.make_async_copy(test_ref, bits_ref, bits_sem)
    copy.start()
    copy_signs.wait()
    to_lanes(velocity_ref, held_ref, sems, wide_ref, pair_ref, held_signs_ref)
    copy.wait()
    columns = bits_ref.shape[0]
    width = wide_ref.shape[1]
    for low in range(0, bits_ref.shape[1], width):
        wide_ref[:columns, :] = (2 * bits_ref[:, low : low + width] - 1).astype(jnp.float32)
        for c in range(2 * parts):
            piece = wide_ref[pl.ds(c, snaps, stride=2 * parts), :]
            matrix_ref[c * snaps : (c + 1) * snaps, low : low + width] = piece.astype(matrix_ref.dtype)


def relay(kernel, flags, inputs, in_vmem, shapes, scratch=()):
    snaps, parts, depth, width = inputs[0].shape
    held = [pltpu.VMEM(inputs[0].shape, inputs[0].dtype), pltpu.VMEM((snaps * parts * depth, width), jnp.float32)]
    return pl.pallas_call(
        kernel,
        out_shape=[jax.ShapeDtypeStruct(shape, dtype) for shape, dtype in shapes],
        in_specs=[SMEM] + [pl.BlockSpec(memory_space=pl.ANY)] * len(inputs) + [VMEM] * len(in_vmem),
        out_specs=[VMEM] * len(shapes),
        scratch_shapes=held + [pltpu.SemaphoreType.DMA((4,))] + list(scratch),
        compiler_params=pltpu.CompilerParams(vmem_limit_bytes=8 << 20),
        name=kernel.__name__,
    )(flags, *[pltpu.with_memory_space_constraint(array, pltpu.HBM) for array in inputs], *in_vmem)


def curl_kernel(flags_ref, field_ref, plane_a_ref, plane_b_ref, rim_a_ref, rim_b_ref, signs_ref, current_ref):
    snaps = rim_a_ref.shape[0] // 2
    width = rim_a_ref.shape[1]
    depth = field_ref.shape[1] // width
    upward = 0.5 - flags_ref[0].astype(jnp.float32)
    odd_block = flags_ref[1] == 1
    lane = lax.broadcasted_iota(jnp.int32, (snaps, width), 1)

    def field(c, x):
        return lanes_of(field_ref.at[c * snaps : (c + 1) * snaps], x, width).astype(jnp.float32)

    def over_x(c, x):
        rim_a = rim_a_ref[(c - 1) * snaps : c * snaps, :].astype(jnp.float32)
        rim_b = rim_b_ref[(c - 1) * snaps : c * snaps, :].astype(jnp.float32)
        low = field(c, x - 1) if x else jnp.where(odd_block, rim_a, rim_b)
        high = field(c, x + 1) if x < depth - 1 else jnp.where(odd_block, rim_b, rim_a)
        return (high - low) * 0.5

    def over_y(c, x):
        values = field(c, x)
        low = jnp.where(lane == 0, 0.0, pltpu.roll(values, 1, 1))
        high = jnp.where(lane == width - 1, 0.0, pltpu.roll(values, width - 1, 1))
        return (high - low) * 0.5

    def over_z(c, x):
        a = lanes_of(plane_a_ref.at[c * snaps : (c + 1) * snaps], x, width).astype(jnp.float32)
        b = lanes_of(plane_b_ref.at[c * snaps : (c + 1) * snaps], x, width).astype(jnp.float32)
        return (a - b) * upward

    for x in range(depth):
        sign = (2 * signs_ref[x : x + 1, :] - 1).astype(jnp.float32)
        current = (
            over_y(2, x) - over_z(1, x),
            over_z(0, x) - over_x(2, x),
            over_x(1, x) - over_y(0, x),
        )
        for c, values in enumerate(current):
            current_ref[c * snaps : (c + 1) * snaps, x * width : (x + 1) * width] = (values * sign).astype(
                current_ref.dtype
            )


def parts_kernel(flags_ref, wanted_ref, pair_ref, other_ref, current_ref, other_current_ref, matrix_ref, *refs):
    part_refs, held_ref = refs[:-1], refs[-1]
    rows, points = current_ref.shape
    width = held_ref.shape[1]
    halves = matrix_ref.shape[1] // width
    own_sign = (1 - 2 * flags_ref[0]).astype(jnp.float32)

    def sketch(values_ref, matrix):
        return lax.dot_general(values_ref, matrix, (TN, ((), ())), preferred_element_type=jnp.float32)

    plain = matrix_ref[...]
    turned = (plain.astype(jnp.float32) * own_sign).astype(plain.dtype)
    total = sketch(pair_ref[-rows:, :], turned[:rows]) + sketch(other_ref[-rows:, :], plain[:rows])
    total = total + sketch(current_ref[...], turned[rows:]) + sketch(other_current_ref[...], plain[rows:])
    for half in range(halves):
        held_ref[pl.ds(half, points, stride=halves), :] = total[:, half * width : (half + 1) * width]
    samples = part_refs[0].shape[0] // halves
    batch = 16
    for slot, part_ref in enumerate(part_refs):
        for first in range(0, samples, batch):
            at = [pl.multiple_of(wanted_ref[slot * samples + first + i], halves) for i in range(batch)]
            values = [held_ref[pl.ds(start, halves), :] for start in at]
            for i in range(batch):
                part_ref[(first + i) * halves : (first + i + 1) * halves, :] = values[i]


def gram_kernel(signs_ref, *refs):
    parts, (picked_ref, packed_ref, held_ref) = refs[:-3], refs[-3:]
    total = signs_ref[0] * parts[0][...]
    for slot in range(1, len(parts)):
        total = total + signs_ref[slot] * parts[slot][...]
    held_ref[...] = total
    samples, wide = picked_ref.shape
    width = held_ref.shape[1]
    halves = wide // width
    picked = [held_ref[pl.ds(half, samples, stride=halves), :] for half in range(halves)]
    picked = jnp.concatenate(picked, axis=1)
    picked_ref[...] = picked
    pack(product(picked.T, picked, NN) * signs_ref[len(parts)], packed_ref)


def product(a, b, dims):
    return lax.dot_general(
        a, b, (dims, ((), ())), precision=lax.Precision.HIGHEST, preferred_element_type=jnp.float32
    )


def eliminate(a_ref, z_ref):
    n = a_ref.shape[0]
    row = lax.broadcasted_iota(jnp.int32, (ROWS, n), 0)
    lane = lax.broadcasted_iota(jnp.int32, (ROWS, n), 1)

    def spread(x):
        return jnp.broadcast_to(x, (ROWS, n))

    def rows_of(ref, start):
        return ref[start : start + ROWS, :]

    for start in range(0, n, ROWS):
        z_ref[start : start + ROWS, :] = jnp.where(lane == row + start, 1.0, 0.0)
    for start in range(0, n, ROWS):
        block, block_z = rows_of(a_ref, start), rows_of(z_ref, start)
        columns = [spread(block[:, start + c : start + c + 1]) for c in range(ROWS)]
        pivots = {(k, c): spread(columns[c][k : k + 1, :]) for c in range(ROWS) for k in range(c + 1)}
        top = [spread(block[k : k + 1, :]) for k in range(ROWS)]
        top_z = [spread(block_z[k : k + 1, :]) for k in range(ROWS)]
        inverse = []
        for k in range(ROWS):
            inverse.append(1.0 / pivots[k, k])
            for i in range(k + 1, ROWS):
                times = pivots[k, i] * inverse[k]
                for c in range(i, ROWS):
                    pivots[i, c] = pivots[i, c] - times * pivots[k, c]
                top[i] = top[i] - times * top[k]
                top_z[i] = top_z[i] - times * top_z[k]
        for below in range(start + ROWS, n, ROWS):
            rest, rest_z = rows_of(a_ref, below), rows_of(z_ref, below)
            columns = [spread(rest[:, start + c : start + c + 1]) for c in range(ROWS)]
            for k in range(ROWS):
                times = columns[k] * inverse[k]
                for c in range(k + 1, ROWS):
                    columns[c] = columns[c] - times * pivots[k, c]
                rest = rest - times * top[k]
                rest_z = rest_z - times * top_z[k]
            a_ref[below : below + ROWS, :] = rest
            z_ref[below : below + ROWS, :] = rest_z
        done, done_z = jnp.zeros_like(block), jnp.zeros_like(block)
        for k in range(ROWS):
            scale = lax.rsqrt(pivots[k, k])
            done = jnp.where(row == k, top[k] * scale, done)
            done_z = jnp.where(row == k, top_z[k] * scale, done_z)
        a_ref[start : start + ROWS, :] = jnp.where(lane >= row + start, done, 0.0)
        z_ref[start : start + ROWS, :] = done_z


def pack(gram, packed_ref):
    n = gram.shape[0]
    q, h = n // 4, n // 2
    lane = lax.broadcasted_iota(jnp.int32, (q, h), 1)
    packed_ref[:q, :] = gram[:q, :]
    packed_ref[q:h, :h] = jnp.where(lane < q, gram[h : h + q, h:], gram[q:h, :h])
    packed_ref[q:h, h:] = gram[q:h, h:]
    packed_ref[h:, :h] = gram[h + q : h + q + q // 2, h:]
    packed_ref[h:, h:] = gram[h + q + q // 2 :, h:]


def unpack(packed):
    n = packed.shape[1]
    q, h = n // 4, n // 2
    row = lax.broadcasted_iota(jnp.int32, (h, h), 0)
    lane = lax.broadcasted_iota(jnp.int32, (h, h), 1)
    top = packed[:h, :h]
    first = jnp.where((row >= q) & (lane < q), top.T, top)
    bottom = jnp.concatenate([packed[q:h, :h], packed[h:, :h], packed[h:, h:]])
    last = jnp.where((row < q) & (lane >= q), bottom.T, bottom)
    return first, packed[:h, h:], last


def parity_sign(a, b):
    both = jnp.bitwise_and(a, b)
    return 1.0 - 2.0 * (lax.population_count(both) % 2).astype(jnp.float32)


def doubled(rows, bit):
    return jnp.concatenate([rows, lax.ppermute(rows, "mix", xor_route(lax.axis_size("mix"), bit))])


def sampled_mixing(flags, pair, other, current, matrix, wanted):
    planes = lax.axis_size("mix")
    mine = lax.axis_index("mix")
    targets, samples = wanted.shape
    halves = matrix.shape[1] // LANES
    part = ((samples * halves, LANES), jnp.float32)
    other_current = lax.ppermute(current, "mix", xor_route(planes, 1))
    inputs = (flags, wanted.reshape(-1) * halves, pair, other, current, other_current, matrix)
    scratch = ((current.shape[1] * halves, LANES),)
    parts = local(parts_kernel, inputs, [part] * targets, scratch, megabytes=12, scalars=2)
    hops = range(2, planes, 2)
    arrived = [parts[0]] + [lax.ppermute(part, "mix", xor_route(planes, k)) for part, k in zip(parts[1:], hops)]
    return arrived, [parity_sign(mine, (mine ^ k) - mine % 2) for k in range(0, planes, 2)]


def whole_mixing(pair, current, matrix, wanted):
    planes = lax.axis_size("mix")
    mine = lax.axis_index("mix")
    snapshot = jnp.concatenate([pair[-current.shape[0] :], current])
    values = lax.dot_general(snapshot, matrix, (((0,), (0,)), ((), ())), preferred_element_type=jnp.float32)
    for level in range(planes.bit_length() - 1):
        partner = lax.ppermute(values, "mix", xor_route(planes, 1 << level))
        upper_bit = mine // (1 << level) % 2
        values = jnp.where(upper_bit == 1, partner - values, values + partner)
    return [jnp.take(values, wanted[0], axis=0).reshape(-1, LANES)], [jnp.float32(1.0)]


def sum_over_mesh(packed):
    planes, blocks = lax.axis_size("mix"), lax.axis_size("row")
    half_rows = packed.shape[0] // 2
    low, high = packed[:half_rows], packed[half_rows:]
    if planes > 8 or blocks != 4:
        low, high = lax.psum((low, high), MESH_AXES)
        return low, high, jnp.int32(0)
    core = lax.axis_index("mix") % 2
    half = jnp.where(core == 0, low, high)
    half = half + lax.ppermute(jnp.where(core == 0, high, low), "mix", xor_route(planes, 1))
    half = half + sum(lax.ppermute(half, "mix", xor_route(planes, k)) for k in range(2, planes, 2))
    half = half + sum(lax.ppermute(half, "row", xor_route(blocks, k)) for k in range(1, blocks))
    return half, lax.ppermute(half, "mix", xor_route(planes, 1)), core


def finish_kernel(core_ref, half_ref, other_ref, picked_ref, basis_ref, factor_ref, a_ref, first_ref, second_ref):
    side = a_ref.shape[0]
    half, other = half_ref[...], other_ref[...]
    swap = core_ref[0] != 0
    packed = jnp.concatenate([jnp.where(swap, other, half), jnp.where(swap, half, other)])
    corner, right, last = unpack(packed)
    a_ref[...] = corner
    eliminate(a_ref, first_ref)
    first = first_ref[...]
    across = product(first, right, NN)
    down = product(right.T, first, NT)
    factor_ref[:side, :side] = a_ref[...]
    factor_ref[:side, side:] = across
    factor_ref[side:, :side] = jnp.zeros_like(across)
    a_ref[...] = last - product(down, across, NN)
    solved = product(picked_ref[:, :side], first, NT)
    basis_ref[:, :side] = solved
    left_over = picked_ref[:, side:] - product(solved, across, NN)
    eliminate(a_ref, second_ref)
    basis_ref[:, side:] = product(left_over, second_ref[...], NT)
    factor_ref[side:, side:] = a_ref[...]


def finish(half, other, core, picked):
    n = picked.shape[1]
    shapes = [(picked.shape, jnp.float32), ((n, n), jnp.float32)]
    scratch = ((n // 2, n // 2),) * 3
    return local(finish_kernel, (core.reshape(1), half, other, picked), shapes, scratch)


def on_device(velocity, field_b, test_signs, row_signs, sample_index):
    snaps, parts, _, depth, width = field_b.shape
    sketch_width = test_signs.shape[1]
    planes, blocks = lax.axis_size("mix"), lax.axis_size("row")
    samples = sample_index.shape[-1]
    points = depth * width
    flags = jnp.stack([lax.axis_index("mix") % 2, lax.axis_index("row") % 2]).astype(jnp.int32)
    signs = row_signs[0]
    lanes = ((parts * snaps, points), jnp.bfloat16)
    flat = ((2 * snaps, points), jnp.bfloat16)
    rim = ((2 * snaps, width), jnp.bfloat16)
    sampled_bytes = (planes // 2 - 1) * samples * sketch_width
    whole_bytes = (planes.bit_length() - 1) * points * sketch_width
    sampled = sampled_bytes < whole_bytes
    wanted = sample_index.reshape(1, -1)
    if sampled:
        wanted = doubled(wanted, 2)
    field, flat, rim_a, rim_b = relay(field_kernel, flags, [field_b[:, :, 0]], [], [lanes, flat, rim, rim])
    plane_b = lax.ppermute(flat, "mix", pair_route(planes, 1))
    rim_a = lax.ppermute(rim_a, "row", pair_route(blocks, 0))
    rim_b = lax.ppermute(rim_b, "row", pair_route(blocks, 1))
    matrix = ((2 * parts * snaps, sketch_width), jnp.bfloat16)
    scratch = [pltpu.VMEM(test_signs.shape, jnp.int32), pltpu.SemaphoreType.DMA]
    scratch += [pltpu.VMEM(signs.shape, jnp.int32), pltpu.SemaphoreType.DMA]
    inputs = [velocity[:, :, 0], test_signs, signs]
    pair, matrix = relay(velocity_kernel, flags, inputs, [], [lanes, matrix], scratch)
    plane_a = lax.ppermute(flat, "mix", pair_route(planes, 0))
    pair, wanted = lax.optimization_barrier((pair, wanted))
    other = lax.ppermute(pair, "mix", pair_route(planes, 0))
    if sampled:
        for level in range(2, planes.bit_length() - 1):
            wanted = doubled(wanted, 1 << level)
    (current,) = local(curl_kernel, (flags, field, plane_a, plane_b, rim_a, rim_b, signs), [lanes])
    if sampled:
        added, part_signs = sampled_mixing(flags, pair, other, current, matrix, wanted)
    else:
        added, part_signs = whole_mixing(pair, current, matrix, wanted)
    scale = 1.0 / math.sqrt(6 * snaps * planes)
    factors = jnp.stack([sign * scale for sign in part_signs] + [jnp.float32(1.0 / (planes * blocks * samples))])
    picked, packed = local(
        gram_kernel,
        (factors, *added),
        [((samples, sketch_width), jnp.float32), ((sketch_width * 5 // 8, sketch_width), jnp.float32)],
        (added[0].shape,),
    )
    basis_rows, factor = finish(*sum_over_mesh(packed), picked)
    return basis_rows.reshape(sample_index.shape + (sketch_width,)), factor


def solution(mesh):
    return jax.shard_map(
        on_device,
        mesh=mesh,
        in_specs=(
            P(None, None, "mix", "row", None),
            P(None, None, "mix", "row", None),
            P(),
            P("mix", "row", None),
            P("mix", "row", None),
        ),
        out_specs=(P("mix", "row", None, None), P()),
        check_vma=False,
    )
```

time: 139 us -> 69 us (0.50)
  other arithmetic: 56 us -> 0.16 us
  Pallas kernels: 0 us -> 18.4 us
  local copies, waits for them, and re-layouts: 10 us -> 0.1 us
  waiting for transfers between devices: 34.4 us -> 25.8 us
  starting transfers between devices: 30.3 us -> 23.5 us
  matrix products: 5.42 us -> 0 us
  between operations: 2.4 us -> 0.81 us
    another operation x12 -> x1, other arithmetic: 54.5 us -> 0.08 us  [on_device(): jnp.stack([lax.axis_index('mix') % 2, lax.axis_index('row') % 2])]
    pallas_call x0 -> x6, Pallas kernels: none -> 18.4 us  [the longest x4 14.1 us: local(): pl.pallas_call(kernel, out_shape=[jax.ShapeDtypeStruct(shape, dtype) for...]
    ppermute x16 -> x15, waiting for transfers between devices: 27.3 us -> 19.7 us  [the longest x3 10.4 us: sampled_mixing(): lax.ppermute(part, 'mix', xor_route(planes, k))]
    ppermute x16 -> x15, starting transfers between devices: 26.6 us -> 19.9 us  [the longest x3 5.77 us: sum_over_mesh(): lax.ppermute(half, 'row', xor_route(blocks, k))]
    another operation x9 -> x1, local copies, waits for them, and re-layouts: 4.1 us -> 0.08 us  [on_device(): jnp.stack([sign * scale for sign in part_signs] + [jnp.float32(1.0 / (pla...]
    dot_general x3 -> x0, matrix products: 3.94 us -> none  [the longest x2 3.34 us: part_sum(): jnp.einsum('sj,tsk->tjk', twice, gathered, preferred_element_type=jnp.flo...]
    unnamed x12 -> x5, local copies, waits for them, and re-layouts: 3.19 us -> 0.02 us
    slice x3 -> x0, local copies, waits for them, and re-layouts: 2.3 us -> none  [the longest x1 1.13 us: curl(): left, right = neighbours(plane[:, 1:, :1], plane[:, 1:, -1:], 'row')]
  transfers between devices with their start and end apart: 20 -> 19, of which waited for: 11 -> 11; matrix products, arithmetic and copies ran while one was open for 4% -> 0% of each run, Pallas kernels for 0% -> 5%
where the time goes in v3:
time: 69 us; the launch traced here: 68.8 us
  waiting for transfers between devices  25.8 us (37%)
  starting transfers between devices  23.5 us (34%)
  Pallas kernels  18.4 us (27%)
  between operations  0.81 us (1%)
    pallas_call x4, Pallas kernels, local(): pl.pallas_call(kernel, out_shape=[jax.ShapeDtypeStruct(shape, dtype) for...  14.1 us
    ppermute x3, waiting for transfers between devices, sampled_mixing(): lax.ppermute(part, 'mix', xor_route(planes, k))  10.4 us
    ppermute x3, starting transfers between devices, sum_over_mesh(): lax.ppermute(half, 'row', xor_route(blocks, k))  5.77 us
    ppermute x2, starting transfers between devices, doubled(): lax.ppermute(rows, 'mix', xor_route(lax.axis_size('mix'), bit))  5.47 us
    ppermute x3, waiting for transfers between devices, sum_over_mesh(): lax.ppermute(half, 'row', xor_route(blocks, k))  5.21 us
    ppermute x3, waiting for transfers between devices, sum_over_mesh(): lax.ppermute(half, 'mix', xor_route(planes, k))  4.87 us
    pallas_call x2, Pallas kernels, relay(): pl.pallas_call(kernel, out_shape=[jax.ShapeDtypeStruct(shape, dtype) for...  4.23 us
    ppermute x3, starting transfers between devices, sampled_mixing(): lax.ppermute(part, 'mix', xor_route(planes, k))  3.8 us
  transfers between devices with their start and end apart: 19, of which 11 were waited for; matrix products, arithmetic and copies ran while one was open for 0% of the time, Pallas kernels for 5%

profile of v3, /device:TPU:0, one launch (start us, length us, event | category | flops | bytes accessed | tf_op | source)
XLA Modules:
  0.0 68.8 jit_solution(18035283764906298459)
XLA Ops:
  0.7 1.7 %field_kernel.1 = (bf16[192,1024]{1,0:T(8,128)(2,1)S(1)}, bf16[128,1024]{1,0:T(8,128)(2,1)S(1)}, bf16[128,128]{1,0:T(8,128)(2,1)S(1)}, bf16[128,128]{1,0:T(8,128)(2,1)S(1)}) custom-call(s32[2]{0:T(128)S(1)} %pad_add_fusion.1.flags_ref, bf16[64,3,8,128]{3,2,1,0:T(8,128)(2,1)} %bitcast.17), custom_call_target="tpu_custom_call" | custom-call | tf_op jit(solution)/shard_map/field_kernel/pallas_call | solution.py:115
  3.7 3.8 %collective-permute-start = (s32[1,256]{1,0:T(1,128)S(1)}, s32[1,256]{1,0:T(1,128)S(1)}, u32[]{:S(2)}, u32[]{:S(2)}) collective-permute-start(s32[1,256]{1,0:T(1,128)S(1)} %bitcast.19), channel_id=1, source_target_pairs={{0,2},{1,3},{2,0},{3,1},{4,6},{5,7},{6,4},{7,5},{8,10},{9,11},{10,... | collective-permute-start | bytes 3080 | tf_op jit(solution)/shard_map/ppermute | solution.py:292
  7.5 2.2 %collective-permute-start.5 = (bf16[128,128]{1,0:T(8,128)(2,1)S(1)}, bf16[128,128]{1,0:T(8,128)(2,1)S(1)}, u32[]{:S(2)}, u32[]{:S(2)}) collective-permute-start(bf16[128,128]{1,0:T(8,128)(2,1)S(1)} %get-tuple-element.23), channel_id=1, source_target_pairs={{0,8},{16,24},{8,0},{24,16},{1,9},{17,25},{9,1},{25,17},{2,10},{18... | collective-permute-start | bytes 98312 | tf_op jit(solution)/shard_map/ppermute | solution.py:386
  10.3 2.5 %velocity_kernel.1 = (bf16[192,1024]{1,0:T(8,128)(2,1)S(1)}, bf16[384,256]{1,0:T(8,128)(2,1)S(1)}) custom-call(s32[2]{0:T(128)S(1)} %pad_add_fusion.1.flags_ref, bf16[64,3,8,128]{3,2,1,0:T(8,128)(2,1)} %bitcast.18, s32[384,256]{1,0:T(8,128)} %test_ref.1, s32[8,128]{1,0:T(8,128)} %bitcast.14), custom_call_target="tpu_custom_call" | custom-call | tf_op jit(solution)/shard_map/velocity_kernel/pallas_call | solution.py:115
  14.4 0.9 %curl_kernel.1.current_ref = bf16[192,1024]{1,0:T(8,128)(2,1)S(1)} custom-call(s32[2]{0:T(128)S(1)} %pad_add_fusion.1.flags_ref, bf16[192,1024]{1,0:T(8,128)(2,1)S(1)} %get-tuple-element.21.field_ref, bf16[128,1024]{1,0:T(8,128)(2,1)S(1)} %collective-permute-done.3.plane_a_ref, bf16[128,1024]{1,0:T(8,128)(2,1)S(1)} %collective-permute-done.4.plane_b_ref, ...), custom_call_target="tpu_custom_call" | custom-call | tf_op jit(solution)/shard_map/curl_kernel/pallas_call | solution.py:28
  15.4 1.6 %collective-permute-start.1 = (s32[2,256]{1,0:T(2,128)S(1)}, s32[2,256]{1,0:T(2,128)S(1)}, u32[]{:S(2)}, u32[]{:S(2)}) collective-permute-start(s32[2,256]{1,0:T(2,128)S(1)} %pad_add_fusion), channel_id=1, source_target_pairs={{0,4},{1,5},{2,6},{3,7},{4,0},{5,1},{6,2},{7,3},{8,12},{9,13},{10,... | collective-permute-start | bytes 6152 | tf_op jit(solution)/shard_map/ppermute | solution.py:292
  17.1 2.0 %collective-permute-done.1 = s32[2,256]{1,0:T(2,128)S(1)} collective-permute-done((s32[2,256]{1,0:T(2,128)S(1)}, s32[2,256]{1,0:T(2,128)S(1)}, u32[]{:S(2)}, u32[]{:S(2)}) %collective-permute-start.1) | collective-permute-done | bytes 2080 | tf_op jit(solution)/shard_map/ppermute | solution.py:292
  19.1 1.9 %parts_kernel.1 = (f32[512,128]{1,0:T(8,128)S(1)}, f32[512,128]{1,0:T(8,128)S(1)}, f32[512,128]{1,0:T(8,128)S(1)}, f32[512,128]{1,0:T(8,128)S(1)}) custom-call(s32[2]{0:T(128)S(1)} %pad_add_fusion.1.flags_ref, s32[1024]{0:T(1024)S(1)} %bitcast.16, bf16[192,1024]{1,0:T(8,128)(2,1)S(1)} %get-tuple-element.20.pair_ref, ...), custom_call_target="tpu_custom_call" | custom-call | tf_op jit(solution)/shard_map/parts_kernel/pallas_call | solution.py:28
  21.0 3.1 %collective-permute-start.10 = (f32[512,128]{1,0:T(8,128)S(1)}, f32[512,128]{1,0:T(8,128)S(1)}, u32[]{:S(2)}, u32[]{:S(2)}) collective-permute-start(f32[512,128]{1,0:T(8,128)S(1)} %get-tuple-element.29), channel_id=1, source_target_pairs={{0,6},{1,7},{2,4},{3,5},{4,2},{5,3},{6,0},{7,1},{8,14},{9,15},{10,... | collective-permute-start | bytes 786440 | tf_op jit(solution)/shard_map/ppermute | solution.py:306
  24.9 6.5 %collective-permute-done.10.refs_3_ = f32[512,128]{1,0:T(8,128)S(1)} collective-permute-done((f32[512,128]{1,0:T(8,128)S(1)}, f32[512,128]{1,0:T(8,128)S(1)}, u32[]{:S(2)}, u32[]{:S(2)}) %collective-permute-start.10) | collective-permute-done | bytes 262176 | tf_op jit(solution)/shard_map/ppermute | solution.py:306
  31.4 3.9 %collective-permute-done.8.refs_1_ = f32[512,128]{1,0:T(8,128)S(1)} collective-permute-done((f32[512,128]{1,0:T(8,128)S(1)}, f32[512,128]{1,0:T(8,128)S(1)}, u32[]{:S(2)}, u32[]{:S(2)}) %collective-permute-start.8) | collective-permute-done | bytes 262176 | tf_op jit(solution)/shard_map/ppermute | solution.py:306
  35.3 1.0 %gram_kernel.1 = (f32[256,256]{1,0:T(8,128)S(1)}, f32[160,256]{1,0:T(8,128)S(1)}) custom-call(f32[5]{0:T(128)S(1)} %stack.26.signs_ref, f32[512,128]{1,0:T(8,128)S(1)} %get-tuple-element.26.refs_0_, f32[512,128]{1,0:T(8,128)S(1)} %collective-permute-done.8.refs_1_, f32[512,128]{1,0:T(8,128)S(1)} %collective-permute-done.9.refs_2_, ...), custom_call_target="tpu_custom_call" | custom-call | tf_op jit(solution)/shard_map/gram_kernel/pallas_call | solution.py:28
  36.4 1.3 %collective-permute-done.11 = f32[80,256]{1,0:T(8,128)S(1)} collective-permute-done((f32[80,256]{1,0:T(8,128)S(1)}, f32[80,256]{1,0:T(8,128)S(1)}, u32[]{:S(2)}, u32[]{:S(2)}) %collective-permute-start.11) | collective-permute-done | bytes 81952 | tf_op jit(solution)/shard_map/ppermute | solution.py:331
  37.7 1.8 %collective-permute-start.12 = (f32[80,256]{1,0:T(8,128)S(1)}, f32[80,256]{1,0:T(8,128)S(1)}, u32[]{:S(2)}, u32[]{:S(2)}) collective-permute-start(f32[80,256]{1,0:T(8,128)S(1)} %select_add_fusion), channel_id=1, source_target_pairs={{0,2},{1,3},{2,0},{3,1},{4,6},{5,7},{6,4},{7,5},{8,10},{9,11},{10,... | collective-permute-start | bytes 245768 | tf_op jit(solution)/shard_map/ppermute | solution.py:332
  39.5 1.3 %collective-permute-start.13 = (f32[80,256]{1,0:T(8,128)S(1)}, f32[80,256]{1,0:T(8,128)S(1)}, u32[]{:S(2)}, u32[]{:S(2)}) collective-permute-start(f32[80,256]{1,0:T(8,128)S(1)} %select_add_fusion), channel_id=1, source_target_pairs={{0,4},{1,5},{2,6},{3,7},{4,0},{5,1},{6,2},{7,3},{8,12},{9,13},{10,... | collective-permute-start | bytes 245768 | tf_op jit(solution)/shard_map/ppermute | solution.py:332
  41.3 1.0 %collective-permute-done.12 = f32[80,256]{1,0:T(8,128)S(1)} collective-permute-done((f32[80,256]{1,0:T(8,128)S(1)}, f32[80,256]{1,0:T(8,128)S(1)}, u32[]{:S(2)}, u32[]{:S(2)}) %collective-permute-start.12) | collective-permute-done | bytes 81952 | tf_op jit(solution)/shard_map/ppermute | solution.py:332
  42.3 1.7 %collective-permute-done.13 = f32[80,256]{1,0:T(8,128)S(1)} collective-permute-done((f32[80,256]{1,0:T(8,128)S(1)}, f32[80,256]{1,0:T(8,128)S(1)}, u32[]{:S(2)}, u32[]{:S(2)}) %collective-permute-start.13) | collective-permute-done | bytes 81952 | tf_op jit(solution)/shard_map/ppermute | solution.py:332
  44.0 2.2 %collective-permute-done.14 = f32[80,256]{1,0:T(8,128)S(1)} collective-permute-done((f32[80,256]{1,0:T(8,128)S(1)}, f32[80,256]{1,0:T(8,128)S(1)}, u32[]{:S(2)}, u32[]{:S(2)}) %collective-permute-start.14) | collective-permute-done | bytes 81952 | tf_op jit(solution)/shard_map/ppermute | solution.py:332
  46.2 3.3 %collective-permute-start.15 = (f32[80,256]{1,0:T(8,128)S(1)}, f32[80,256]{1,0:T(8,128)S(1)}, u32[]{:S(2)}, u32[]{:S(2)}) collective-permute-start(f32[80,256]{1,0:T(8,128)S(1)} %add_add_fusion.1), channel_id=1, source_target_pairs={{0,8},{8,0},{16,24},{24,16},{1,9},{9,1},{17,25},{25,17},{2,10},{10... | collective-permute-start | bytes 245768 | tf_op jit(solution)/shard_map/ppermute | solution.py:333
  49.5 0.9 %collective-permute-start.16 = (f32[80,256]{1,0:T(8,128)S(1)}, f32[80,256]{1,0:T(8,128)S(1)}, u32[]{:S(2)}, u32[]{:S(2)}) collective-permute-start(f32[80,256]{1,0:T(8,128)S(1)} %add_add_fusion.1), channel_id=1, source_target_pairs={{0,16},{8,24},{16,0},{24,8},{1,17},{9,25},{17,1},{25,9},{2,18},{10... | collective-permute-start | bytes 245768 | tf_op jit(solution)/shard_map/ppermute | solution.py:333
  50.4 1.5 %collective-permute-start.17 = (f32[80,256]{1,0:T(8,128)S(1)}, f32[80,256]{1,0:T(8,128)S(1)}, u32[]{:S(2)}, u32[]{:S(2)}) collective-permute-start(f32[80,256]{1,0:T(8,128)S(1)} %add_add_fusion.1), channel_id=1, source_target_pairs={{0,24},{8,16},{16,8},{24,0},{1,25},{9,17},{17,9},{25,1},{2,26},{10... | collective-permute-start | bytes 245768 | tf_op jit(solution)/shard_map/ppermute | solution.py:333
  52.0 5.1 %collective-permute-done.16 = f32[80,256]{1,0:T(8,128)S(1)} collective-permute-done((f32[80,256]{1,0:T(8,128)S(1)}, f32[80,256]{1,0:T(8,128)S(1)}, u32[]{:S(2)}, u32[]{:S(2)}) %collective-permute-start.16) | collective-permute-done | bytes 81952 | tf_op jit(solution)/shard_map/ppermute | solution.py:333
  57.2 1.3 %collective-permute-done.18.other_ref = f32[80,256]{1,0:T(8,128)S(1)} collective-permute-done((f32[80,256]{1,0:T(8,128)S(1)}, f32[80,256]{1,0:T(8,128)S(1)}, u32[]{:S(2)}, u32[]{:S(2)}) %collective-permute-start.18) | collective-permute-done | bytes 81952 | tf_op jit(solution)/shard_map/ppermute | solution.py:334
  58.5 10.3 %finish_kernel.1 = (f32[256,256]{1,0:T(8,128)}, f32[256,256]{1,0:T(8,128)}) custom-call(s32[1]{0:T(128)} %bitcast.core_ref, f32[80,256]{1,0:T(8,128)S(1)} %add_add_fusion.half_ref, f32[80,256]{1,0:T(8,128)S(1)} %collective-permute-done.18.other_ref, f32[256,256]{1,0:T(8,128)S(1)} %get-tuple-element.31.picked_ref), custom_call_target="tpu_custom_call" | custom-call | tf_op jit(solution)/shard_map/finish_kernel/pallas_call | solution.py:28
  (33 shorter events, 5.1 us)
Async XLA Ops:
  2.4 1.2 %copy-start.1 = (s32[1,1,256]{2,1,0:T(1,128)S(1)}, s32[1,1,256]{2,1,0:T(1,128)}, u32[]{:S(2)}) copy-start(s32[1,1,256]{2,1,0:T(1,128)} %param.9) | copy-start | bytes 3076
  2.5 11.9 %collective-permute-start.3 = (bf16[128,1024]{1,0:T(8,128)(2,1)S(1)}, bf16[128,1024]{1,0:T(8,128)(2,1)S(1)}, u32[]{:S(2)}, u32[]{:S(2)}) collective-permute-start(bf16[128,1024]{1,0:T(8,128)(2,1)S(1)} %get-tuple-element.22), channel_id=1, source_target_pairs={{0,1},{2,3},{4,5},{6,7},{1,0},{3,2},{5,4},{7,6},{8,9},{10,11},{12,... | collective-permute-start | bytes 786440 | tf_op jit(solution)/shard_map/ppermute | solution.py:393
  3.0 11.4 %collective-permute-start.4 = (bf16[128,1024]{1,0:T(8,128)(2,1)S(1)}, bf16[128,1024]{1,0:T(8,128)(2,1)S(1)}, u32[]{:S(2)}, u32[]{:S(2)}) collective-permute-start(bf16[128,1024]{1,0:T(8,128)(2,1)S(1)} %get-tuple-element.22), channel_id=1, source_target_pairs={{1,2},{3,4},{5,6},{2,1},{4,3},{6,5},{9,10},{11,12},{13,14},{10,9},... | collective-permute-start | bytes 786440 | tf_op jit(solution)/shard_map/ppermute | solution.py:385
  3.7 10.0 %collective-permute-start = (s32[1,256]{1,0:T(1,128)S(1)}, s32[1,256]{1,0:T(1,128)S(1)}, u32[]{:S(2)}, u32[]{:S(2)}) collective-permute-start(s32[1,256]{1,0:T(1,128)S(1)} %bitcast.19), channel_id=1, source_target_pairs={{0,2},{1,3},{2,0},{3,1},{4,6},{5,7},{6,4},{7,5},{8,10},{9,11},{10,... | collective-permute-start | bytes 3080 | tf_op jit(solution)/shard_map/ppermute | solution.py:292
  7.5 6.9 %collective-permute-start.5 = (bf16[128,128]{1,0:T(8,128)(2,1)S(1)}, bf16[128,128]{1,0:T(8,128)(2,1)S(1)}, u32[]{:S(2)}, u32[]{:S(2)}) collective-permute-start(bf16[128,128]{1,0:T(8,128)(2,1)S(1)} %get-tuple-element.23), channel_id=1, source_target_pairs={{0,8},{16,24},{8,0},{24,16},{1,9},{17,25},{9,1},{25,17},{2,10},{18... | collective-permute-start | bytes 98312 | tf_op jit(solution)/shard_map/ppermute | solution.py:386
  9.7 4.7 %collective-permute-start.6 = (bf16[128,128]{1,0:T(8,128)(2,1)S(1)}, bf16[128,128]{1,0:T(8,128)(2,1)S(1)}, u32[]{:S(2)}, u32[]{:S(2)}) collective-permute-start(bf16[128,128]{1,0:T(8,128)(2,1)S(1)} %get-tuple-element.24), channel_id=1, source_target_pairs={{8,16},{16,8},{9,17},{17,9},{10,18},{18,10},{11,19},{19,11},{12,20... | collective-permute-start | bytes 98312 | tf_op jit(solution)/shard_map/ppermute | solution.py:387
  12.8 1.6 %copy-start = (s32[1,8,128]{2,1,0:T(8,128)S(1)}, s32[1,8,128]{2,1,0:T(8,128)}, u32[]{:S(2)}) copy-start(s32[1,8,128]{2,1,0:T(8,128)} %param.8) | copy-start | bytes 12292
  13.7 5.4 %collective-permute-start.2 = (bf16[192,1024]{1,0:T(8,128)(2,1)S(1)}, bf16[192,1024]{1,0:T(8,128)(2,1)S(1)}, u32[]{:S(2)}, u32[]{:S(2)}) collective-permute-start(bf16[192,1024]{1,0:T(8,128)(2,1)S(1)} %get-tuple-element.20.pair_ref), channel_id=1, source_target_pairs={{0,1},{2,3},{4,5},{6,7},{1,0},{3,2},{5,4},{7,6},{8,9},{10,11},{12,... | collective-permute-start | bytes 1179656 | tf_op jit(solution)/shard_map/ppermute | solution.py:395
  15.3 3.8 %collective-permute-start.7 = (bf16[192,1024]{1,0:T(8,128)(2,1)S(1)}, bf16[192,1024]{1,0:T(8,128)(2,1)S(1)}, u32[]{:S(2)}, u32[]{:S(2)}) collective-permute-start(bf16[192,1024]{1,0:T(8,128)(2,1)S(1)} %curl_kernel.1.current_ref), channel_id=1, source_target_pairs={{0,1},{1,0},{2,3},{3,2},{4,5},{5,4},{6,7},{7,6},{8,9},{9,8},{10,11... | collective-permute-start | bytes 1179656 | tf_op jit(solution)/shard_map/ppermute | solution.py:301
  15.4 3.6 %collective-permute-start.1 = (s32[2,256]{1,0:T(2,128)S(1)}, s32[2,256]{1,0:T(2,128)S(1)}, u32[]{:S(2)}, u32[]{:S(2)}) collective-permute-start(s32[2,256]{1,0:T(2,128)S(1)} %pad_add_fusion), channel_id=1, source_target_pairs={{0,4},{1,5},{2,6},{3,7},{4,0},{5,1},{6,2},{7,3},{8,12},{9,13},{10,... | collective-permute-start | bytes 6152 | tf_op jit(solution)/shard_map/ppermute | solution.py:292
  21.0 10.3 %collective-permute-start.10 = (f32[512,128]{1,0:T(8,128)S(1)}, f32[512,128]{1,0:T(8,128)S(1)}, u32[]{:S(2)}, u32[]{:S(2)}) collective-permute-start(f32[512,128]{1,0:T(8,128)S(1)} %get-tuple-element.29), channel_id=1, source_target_pairs={{0,6},{1,7},{2,4},{3,5},{4,2},{5,3},{6,0},{7,1},{8,14},{9,15},{10,... | collective-permute-start | bytes 786440 | tf_op jit(solution)/shard_map/ppermute | solution.py:306
  24.1 11.2 %collective-permute-start.8 = (f32[512,128]{1,0:T(8,128)S(1)}, f32[512,128]{1,0:T(8,128)S(1)}, u32[]{:S(2)}, u32[]{:S(2)}) collective-permute-start(f32[512,128]{1,0:T(8,128)S(1)} %get-tuple-element.27), channel_id=1, source_target_pairs={{0,2},{1,3},{2,0},{3,1},{4,6},{5,7},{6,4},{7,5},{8,10},{9,11},{10,... | collective-permute-start | bytes 786440 | tf_op jit(solution)/shard_map/ppermute | solution.py:306
  24.2 11.1 %collective-permute-start.9 = (f32[512,128]{1,0:T(8,128)S(1)}, f32[512,128]{1,0:T(8,128)S(1)}, u32[]{:S(2)}, u32[]{:S(2)}) collective-permute-start(f32[512,128]{1,0:T(8,128)S(1)} %get-tuple-element.28), channel_id=1, source_target_pairs={{0,4},{1,5},{2,6},{3,7},{4,0},{5,1},{6,2},{7,3},{8,12},{9,13},{10,... | collective-permute-start | bytes 786440 | tf_op jit(solution)/shard_map/ppermute | solution.py:306
  36.3 1.3 %collective-permute-start.11 = (f32[80,256]{1,0:T(8,128)S(1)}, f32[80,256]{1,0:T(8,128)S(1)}, u32[]{:S(2)}, u32[]{:S(2)}) collective-permute-start(f32[80,256]{1,0:T(8,128)S(1)} %slice_select_fusion), channel_id=1, source_target_pairs={{0,1},{1,0},{2,3},{3,2},{4,5},{5,4},{6,7},{7,6},{8,9},{9,8},{10,11... | collective-permute-start | bytes 245768 | tf_op jit(solution)/shard_map/ppermute | solution.py:331
  37.7 4.6 %collective-permute-start.12 = (f32[80,256]{1,0:T(8,128)S(1)}, f32[80,256]{1,0:T(8,128)S(1)}, u32[]{:S(2)}, u32[]{:S(2)}) collective-permute-start(f32[80,256]{1,0:T(8,128)S(1)} %select_add_fusion), channel_id=1, source_target_pairs={{0,2},{1,3},{2,0},{3,1},{4,6},{5,7},{6,4},{7,5},{8,10},{9,11},{10,... | collective-permute-start | bytes 245768 | tf_op jit(solution)/shard_map/ppermute | solution.py:332
  39.5 4.5 %collective-permute-start.13 = (f32[80,256]{1,0:T(8,128)S(1)}, f32[80,256]{1,0:T(8,128)S(1)}, u32[]{:S(2)}, u32[]{:S(2)}) collective-permute-start(f32[80,256]{1,0:T(8,128)S(1)} %select_add_fusion), channel_id=1, source_target_pairs={{0,4},{1,5},{2,6},{3,7},{4,0},{5,1},{6,2},{7,3},{8,12},{9,13},{10,... | collective-permute-start | bytes 245768 | tf_op jit(solution)/shard_map/ppermute | solution.py:332
  40.8 5.3 %collective-permute-start.14 = (f32[80,256]{1,0:T(8,128)S(1)}, f32[80,256]{1,0:T(8,128)S(1)}, u32[]{:S(2)}, u32[]{:S(2)}) collective-permute-start(f32[80,256]{1,0:T(8,128)S(1)} %select_add_fusion), channel_id=1, source_target_pairs={{0,6},{1,7},{2,4},{3,5},{4,2},{5,3},{6,0},{7,1},{8,14},{9,15},{10,... | collective-permute-start | bytes 245768 | tf_op jit(solution)/shard_map/ppermute | solution.py:332
  46.2 5.8 %collective-permute-start.15 = (f32[80,256]{1,0:T(8,128)S(1)}, f32[80,256]{1,0:T(8,128)S(1)}, u32[]{:S(2)}, u32[]{:S(2)}) collective-permute-start(f32[80,256]{1,0:T(8,128)S(1)} %add_add_fusion.1), channel_id=1, source_target_pairs={{0,8},{8,0},{16,24},{24,16},{1,9},{9,1},{17,25},{25,17},{2,10},{10... | collective-permute-start | bytes 245768 | tf_op jit(solution)/shard_map/ppermute | solution.py:333
  49.5 7.7 %collective-permute-start.16 = (f32[80,256]{1,0:T(8,128)S(1)}, f32[80,256]{1,0:T(8,128)S(1)}, u32[]{:S(2)}, u32[]{:S(2)}) collective-permute-start(f32[80,256]{1,0:T(8,128)S(1)} %add_add_fusion.1), channel_id=1, source_target_pairs={{0,16},{8,24},{16,0},{24,8},{1,17},{9,25},{17,1},{25,9},{2,18},{10... | collective-permute-start | bytes 245768 | tf_op jit(solution)/shard_map/ppermute | solution.py:333
  50.4 6.8 %collective-permute-start.17 = (f32[80,256]{1,0:T(8,128)S(1)}, f32[80,256]{1,0:T(8,128)S(1)}, u32[]{:S(2)}, u32[]{:S(2)}) collective-permute-start(f32[80,256]{1,0:T(8,128)S(1)} %add_add_fusion.1), channel_id=1, source_target_pairs={{0,24},{8,16},{16,8},{24,0},{1,25},{9,17},{17,9},{25,1},{2,26},{10... | collective-permute-start | bytes 245768 | tf_op jit(solution)/shard_map/ppermute | solution.py:333
  57.2 1.3 %collective-permute-start.18 = (f32[80,256]{1,0:T(8,128)S(1)}, f32[80,256]{1,0:T(8,128)S(1)}, u32[]{:S(2)}, u32[]{:S(2)}) collective-permute-start(f32[80,256]{1,0:T(8,128)S(1)} %add_add_fusion.half_ref), channel_id=1, source_target_pairs={{0,1},{1,0},{2,3},{3,2},{4,5},{5,4},{6,7},{7,6},{8,9},{9,8},{10,11... | collective-permute-start | bytes 245768 | tf_op jit(solution)/shard_map/ppermute | solution.py:334

commit v4 on v3

--- a/solution.py
+++ b/solution.py
@@ -214,23 +214,31 @@
 
 def eliminate(a_ref, z_ref):
     n = a_ref.shape[0]
+    blocks = n // ROWS
     row = lax.broadcasted_iota(jnp.int32, (ROWS, n), 0)
     lane = lax.broadcasted_iota(jnp.int32, (ROWS, n), 1)
 
     def spread(x):
         return jnp.broadcast_to(x, (ROWS, n))
 
-    def rows_of(ref, start):
-        return ref[start : start + ROWS, :]
-
-    for start in range(0, n, ROWS):
-        z_ref[start : start + ROWS, :] = jnp.where(lane == row + start, 1.0, 0.0)
-    for start in range(0, n, ROWS):
-        block, block_z = rows_of(a_ref, start), rows_of(z_ref, start)
-        columns = [spread(block[:, start + c : start + c + 1]) for c in range(ROWS)]
-        pivots = {(k, c): spread(columns[c][k : k + 1, :]) for c in range(ROWS) for k in range(c + 1)}
-        top = [spread(block[k : k + 1, :]) for k in range(ROWS)]
-        top_z = [spread(block_z[k : k + 1, :]) for k in range(ROWS)]
+    def column(block, c):
+        return spread(block[:, c : c + 1])
+
+    def line(block, k):
+        return spread(block[k : k + 1, :])
+
+    rest = [a_ref[b * ROWS : (b + 1) * ROWS, :] for b in range(blocks)]
+    rest_z = [jnp.where(lane == row + b * ROWS, 1.0, 0.0) for b in range(blocks)]
+    columns = [column(rest[0], c) for c in range(ROWS)]
+    for b in range(blocks):
+        start = b * ROWS
+        pivots = {(k, c): line(columns[c], k) for c in range(ROWS) for k in range(c + 1)}
+        top = [line(rest[b], k) for k in range(ROWS)]
+        top_z = [line(rest_z[b], k) for k in range(ROWS)]
+        following = range(b + 1, min(b + 2, blocks))
+        for g in following:
+            next_old = [column(rest[g], start + c) for c in range(ROWS)]
+            columns = [column(rest[g], start + ROWS + c) for c in range(ROWS)]
         inverse = []
         for k in range(ROWS):
             inverse.append(1.0 / pivots[k, k])
@@ -240,18 +248,22 @@
                     pivots[i, c] = pivots[i, c] - times * pivots[k, c]
                 top[i] = top[i] - times * top[k]
                 top_z[i] = top_z[i] - times * top_z[k]
-        for below in range(start + ROWS, n, ROWS):
-            rest, rest_z = rows_of(a_ref, below), rows_of(z_ref, below)
-            columns = [spread(rest[:, start + c : start + c + 1]) for c in range(ROWS)]
+            for g in following:
+                times = next_old[k] * inverse[k]
+                columns = [values - times * line(next_old[k], c) for c, values in enumerate(columns)]
+                for c in range(k + 1, ROWS):
+                    next_old[c] = next_old[c] - times * pivots[k, c]
+                rest[g] = rest[g] - times * top[k]
+                rest_z[g] = rest_z[g] - times * top_z[k]
+        for g in range(b + 2, blocks):
+            old = [column(rest[g], start + c) for c in range(ROWS)]
             for k in range(ROWS):
-                times = columns[k] * inverse[k]
+                times = old[k] * inverse[k]
                 for c in range(k + 1, ROWS):
-                    columns[c] = columns[c] - times * pivots[k, c]
-                rest = rest - times * top[k]
-                rest_z = rest_z - times * top_z[k]
-            a_ref[below : below + ROWS, :] = rest
-            z_ref[below : below + ROWS, :] = rest_z
-        done, done_z = jnp.zeros_like(block), jnp.zeros_like(block)
+                    old[c] = old[c] - times * pivots[k, c]
+                rest[g] = rest[g] - times * top[k]
+                rest_z[g] = rest_z[g] - times * top_z[k]
+        done, done_z = jnp.zeros((ROWS, n), jnp.float32), jnp.zeros((ROWS, n), jnp.float32)
         for k in range(ROWS):
             scale = lax.rsqrt(pivots[k, k])
             done = jnp.where(row == k, top[k] * scale, done)

time: 69 us -> 67.5 us (0.978)
  Pallas kernels: 18.4 us -> 16.9 us
    pallas_call x4, Pallas kernels: 14.1 us -> 12.6 us  [local(): pl.pallas_call(kernel, out_shape=[jax.ShapeDtypeStruct(shape, dtype) for...]
where the time goes in v4:
time: 67.5 us; the launch traced here: 67.3 us
  waiting for transfers between devices  25.8 us (38%)
  starting transfers between devices  23.5 us (35%)
  Pallas kernels  16.9 us (25%)
  between operations  0.81 us (1%)
    pallas_call x4, Pallas kernels, local(): pl.pallas_call(kernel, out_shape=[jax.ShapeDtypeStruct(shape, dtype) for...  12.6 us
    ppermute x3, waiting for transfers between devices, sampled_mixing(): lax.ppermute(part, 'mix', xor_route(planes, k))  10.4 us
    ppermute x3, starting transfers between devices, sum_over_mesh(): lax.ppermute(half, 'row', xor_route(blocks, k))  5.77 us
    ppermute x2, starting transfers between devices, doubled(): lax.ppermute(rows, 'mix', xor_route(lax.axis_size('mix'), bit))  5.47 us
    ppermute x3, waiting for transfers between devices, sum_over_mesh(): lax.ppermute(half, 'row', xor_route(blocks, k))  5.21 us
    ppermute x3, waiting for transfers between devices, sum_over_mesh(): lax.ppermute(half, 'mix', xor_route(planes, k))  4.87 us
    pallas_call x2, Pallas kernels, relay(): pl.pallas_call(kernel, out_shape=[jax.ShapeDtypeStruct(shape, dtype) for...  4.23 us
    ppermute x3, starting transfers between devices, sampled_mixing(): lax.ppermute(part, 'mix', xor_route(planes, k))  3.8 us
  transfers between devices with their start and end apart: 19, of which 11 were waited for; matrix products, arithmetic and copies ran while one was open for 0% of the time, Pallas kernels for 5%

profile of v4, /device:TPU:0, one launch (start us, length us, event | category | flops | bytes accessed | tf_op | source)
XLA Modules:
  0.0 67.3 jit_solution(7977824588456497419)
XLA Ops:
  0.7 1.7 %field_kernel.1 = (bf16[192,1024]{1,0:T(8,128)(2,1)S(1)}, bf16[128,1024]{1,0:T(8,128)(2,1)S(1)}, bf16[128,128]{1,0:T(8,128)(2,1)S(1)}, bf16[128,128]{1,0:T(8,128)(2,1)S(1)}) custom-call(s32[2]{0:T(128)S(1)} %pad_add_fusion.1.flags_ref, bf16[64,3,8,128]{3,2,1,0:T(8,128)(2,1)} %bitcast.17), custom_call_target="tpu_custom_call" | custom-call | tf_op jit(solution)/shard_map/field_kernel/pallas_call | solution.py:115
  3.7 3.8 %collective-permute-start = (s32[1,256]{1,0:T(1,128)S(1)}, s32[1,256]{1,0:T(1,128)S(1)}, u32[]{:S(2)}, u32[]{:S(2)}) collective-permute-start(s32[1,256]{1,0:T(1,128)S(1)} %bitcast.19), channel_id=1, source_target_pairs={{0,2},{1,3},{2,0},{3,1},{4,6},{5,7},{6,4},{7,5},{8,10},{9,11},{10,... | collective-permute-start | bytes 3080 | tf_op jit(solution)/shard_map/ppermute | solution.py:304
  7.5 2.2 %collective-permute-start.5 = (bf16[128,128]{1,0:T(8,128)(2,1)S(1)}, bf16[128,128]{1,0:T(8,128)(2,1)S(1)}, u32[]{:S(2)}, u32[]{:S(2)}) collective-permute-start(bf16[128,128]{1,0:T(8,128)(2,1)S(1)} %get-tuple-element.23), channel_id=1, source_target_pairs={{0,8},{16,24},{8,0},{24,16},{1,9},{17,25},{9,1},{25,17},{2,10},{18... | collective-permute-start | bytes 98312 | tf_op jit(solution)/shard_map/ppermute | solution.py:398
  10.3 2.5 %velocity_kernel.1 = (bf16[192,1024]{1,0:T(8,128)(2,1)S(1)}, bf16[384,256]{1,0:T(8,128)(2,1)S(1)}) custom-call(s32[2]{0:T(128)S(1)} %pad_add_fusion.1.flags_ref, bf16[64,3,8,128]{3,2,1,0:T(8,128)(2,1)} %bitcast.18, s32[384,256]{1,0:T(8,128)} %test_ref.1, s32[8,128]{1,0:T(8,128)} %bitcast.14), custom_call_target="tpu_custom_call" | custom-call | tf_op jit(solution)/shard_map/velocity_kernel/pallas_call | solution.py:115
  14.4 0.9 %curl_kernel.1.current_ref = bf16[192,1024]{1,0:T(8,128)(2,1)S(1)} custom-call(s32[2]{0:T(128)S(1)} %pad_add_fusion.1.flags_ref, bf16[192,1024]{1,0:T(8,128)(2,1)S(1)} %get-tuple-element.21.field_ref, bf16[128,1024]{1,0:T(8,128)(2,1)S(1)} %collective-permute-done.3.plane_a_ref, bf16[128,1024]{1,0:T(8,128)(2,1)S(1)} %collective-permute-done.4.plane_b_ref, ...), custom_call_target="tpu_custom_call" | custom-call | tf_op jit(solution)/shard_map/curl_kernel/pallas_call | solution.py:28
  15.4 1.6 %collective-permute-start.1 = (s32[2,256]{1,0:T(2,128)S(1)}, s32[2,256]{1,0:T(2,128)S(1)}, u32[]{:S(2)}, u32[]{:S(2)}) collective-permute-start(s32[2,256]{1,0:T(2,128)S(1)} %pad_add_fusion), channel_id=1, source_target_pairs={{0,4},{1,5},{2,6},{3,7},{4,0},{5,1},{6,2},{7,3},{8,12},{9,13},{10,... | collective-permute-start | bytes 6152 | tf_op jit(solution)/shard_map/ppermute | solution.py:304
  17.1 2.0 %collective-permute-done.1 = s32[2,256]{1,0:T(2,128)S(1)} collective-permute-done((s32[2,256]{1,0:T(2,128)S(1)}, s32[2,256]{1,0:T(2,128)S(1)}, u32[]{:S(2)}, u32[]{:S(2)}) %collective-permute-start.1) | collective-permute-done | bytes 2080 | tf_op jit(solution)/shard_map/ppermute | solution.py:304
  19.1 1.9 %parts_kernel.1 = (f32[512,128]{1,0:T(8,128)S(1)}, f32[512,128]{1,0:T(8,128)S(1)}, f32[512,128]{1,0:T(8,128)S(1)}, f32[512,128]{1,0:T(8,128)S(1)}) custom-call(s32[2]{0:T(128)S(1)} %pad_add_fusion.1.flags_ref, s32[1024]{0:T(1024)S(1)} %bitcast.16, bf16[192,1024]{1,0:T(8,128)(2,1)S(1)} %get-tuple-element.20.pair_ref, ...), custom_call_target="tpu_custom_call" | custom-call | tf_op jit(solution)/shard_map/parts_kernel/pallas_call | solution.py:28
  21.0 3.1 %collective-permute-start.10 = (f32[512,128]{1,0:T(8,128)S(1)}, f32[512,128]{1,0:T(8,128)S(1)}, u32[]{:S(2)}, u32[]{:S(2)}) collective-permute-start(f32[512,128]{1,0:T(8,128)S(1)} %get-tuple-element.29), channel_id=1, source_target_pairs={{0,6},{1,7},{2,4},{3,5},{4,2},{5,3},{6,0},{7,1},{8,14},{9,15},{10,... | collective-permute-start | bytes 786440 | tf_op jit(solution)/shard_map/ppermute | solution.py:318
  24.9 6.5 %collective-permute-done.10.refs_3_ = f32[512,128]{1,0:T(8,128)S(1)} collective-permute-done((f32[512,128]{1,0:T(8,128)S(1)}, f32[512,128]{1,0:T(8,128)S(1)}, u32[]{:S(2)}, u32[]{:S(2)}) %collective-permute-start.10) | collective-permute-done | bytes 262176 | tf_op jit(solution)/shard_map/ppermute | solution.py:318
  31.4 3.9 %collective-permute-done.8.refs_1_ = f32[512,128]{1,0:T(8,128)S(1)} collective-permute-done((f32[512,128]{1,0:T(8,128)S(1)}, f32[512,128]{1,0:T(8,128)S(1)}, u32[]{:S(2)}, u32[]{:S(2)}) %collective-permute-start.8) | collective-permute-done | bytes 262176 | tf_op jit(solution)/shard_map/ppermute | solution.py:318
  35.3 1.0 %gram_kernel.1 = (f32[256,256]{1,0:T(8,128)S(1)}, f32[160,256]{1,0:T(8,128)S(1)}) custom-call(f32[5]{0:T(128)S(1)} %stack.26.signs_ref, f32[512,128]{1,0:T(8,128)S(1)} %get-tuple-element.26.refs_0_, f32[512,128]{1,0:T(8,128)S(1)} %collective-permute-done.8.refs_1_, f32[512,128]{1,0:T(8,128)S(1)} %collective-permute-done.9.refs_2_, ...), custom_call_target="tpu_custom_call" | custom-call | tf_op jit(solution)/shard_map/gram_kernel/pallas_call | solution.py:28
  36.4 1.3 %collective-permute-done.11 = f32[80,256]{1,0:T(8,128)S(1)} collective-permute-done((f32[80,256]{1,0:T(8,128)S(1)}, f32[80,256]{1,0:T(8,128)S(1)}, u32[]{:S(2)}, u32[]{:S(2)}) %collective-permute-start.11) | collective-permute-done | bytes 81952 | tf_op jit(solution)/shard_map/ppermute | solution.py:343
  37.7 1.8 %collective-permute-start.12 = (f32[80,256]{1,0:T(8,128)S(1)}, f32[80,256]{1,0:T(8,128)S(1)}, u32[]{:S(2)}, u32[]{:S(2)}) collective-permute-start(f32[80,256]{1,0:T(8,128)S(1)} %select_add_fusion), channel_id=1, source_target_pairs={{0,2},{1,3},{2,0},{3,1},{4,6},{5,7},{6,4},{7,5},{8,10},{9,11},{10,... | collective-permute-start | bytes 245768 | tf_op jit(solution)/shard_map/ppermute | solution.py:344
  39.5 1.3 %collective-permute-start.13 = (f32[80,256]{1,0:T(8,128)S(1)}, f32[80,256]{1,0:T(8,128)S(1)}, u32[]{:S(2)}, u32[]{:S(2)}) collective-permute-start(f32[80,256]{1,0:T(8,128)S(1)} %select_add_fusion), channel_id=1, source_target_pairs={{0,4},{1,5},{2,6},{3,7},{4,0},{5,1},{6,2},{7,3},{8,12},{9,13},{10,... | collective-permute-start | bytes 245768 | tf_op jit(solution)/shard_map/ppermute | solution.py:344
  41.3 1.0 %collective-permute-done.12 = f32[80,256]{1,0:T(8,128)S(1)} collective-permute-done((f32[80,256]{1,0:T(8,128)S(1)}, f32[80,256]{1,0:T(8,128)S(1)}, u32[]{:S(2)}, u32[]{:S(2)}) %collective-permute-start.12) | collective-permute-done | bytes 81952 | tf_op jit(solution)/shard_map/ppermute | solution.py:344
  42.3 1.7 %collective-permute-done.13 = f32[80,256]{1,0:T(8,128)S(1)} collective-permute-done((f32[80,256]{1,0:T(8,128)S(1)}, f32[80,256]{1,0:T(8,128)S(1)}, u32[]{:S(2)}, u32[]{:S(2)}) %collective-permute-start.13) | collective-permute-done | bytes 81952 | tf_op jit(solution)/shard_map/ppermute | solution.py:344
  44.0 2.2 %collective-permute-done.14 = f32[80,256]{1,0:T(8,128)S(1)} collective-permute-done((f32[80,256]{1,0:T(8,128)S(1)}, f32[80,256]{1,0:T(8,128)S(1)}, u32[]{:S(2)}, u32[]{:S(2)}) %collective-permute-start.14) | collective-permute-done | bytes 81952 | tf_op jit(solution)/shard_map/ppermute | solution.py:344
  46.2 3.3 %collective-permute-start.15 = (f32[80,256]{1,0:T(8,128)S(1)}, f32[80,256]{1,0:T(8,128)S(1)}, u32[]{:S(2)}, u32[]{:S(2)}) collective-permute-start(f32[80,256]{1,0:T(8,128)S(1)} %add_add_fusion.1), channel_id=1, source_target_pairs={{0,8},{8,0},{16,24},{24,16},{1,9},{9,1},{17,25},{25,17},{2,10},{10... | collective-permute-start | bytes 245768 | tf_op jit(solution)/shard_map/ppermute | solution.py:345
  49.5 0.9 %collective-permute-start.16 = (f32[80,256]{1,0:T(8,128)S(1)}, f32[80,256]{1,0:T(8,128)S(1)}, u32[]{:S(2)}, u32[]{:S(2)}) collective-permute-start(f32[80,256]{1,0:T(8,128)S(1)} %add_add_fusion.1), channel_id=1, source_target_pairs={{0,16},{8,24},{16,0},{24,8},{1,17},{9,25},{17,1},{25,9},{2,18},{10... | collective-permute-start | bytes 245768 | tf_op jit(solution)/shard_map/ppermute | solution.py:345
  50.4 1.5 %collective-permute-start.17 = (f32[80,256]{1,0:T(8,128)S(1)}, f32[80,256]{1,0:T(8,128)S(1)}, u32[]{:S(2)}, u32[]{:S(2)}) collective-permute-start(f32[80,256]{1,0:T(8,128)S(1)} %add_add_fusion.1), channel_id=1, source_target_pairs={{0,24},{8,16},{16,8},{24,0},{1,25},{9,17},{17,9},{25,1},{2,26},{10... | collective-permute-start | bytes 245768 | tf_op jit(solution)/shard_map/ppermute | solution.py:345
  52.0 5.1 %collective-permute-done.16 = f32[80,256]{1,0:T(8,128)S(1)} collective-permute-done((f32[80,256]{1,0:T(8,128)S(1)}, f32[80,256]{1,0:T(8,128)S(1)}, u32[]{:S(2)}, u32[]{:S(2)}) %collective-permute-start.16) | collective-permute-done | bytes 81952 | tf_op jit(solution)/shard_map/ppermute | solution.py:345
  57.2 1.3 %collective-permute-done.18.other_ref = f32[80,256]{1,0:T(8,128)S(1)} collective-permute-done((f32[80,256]{1,0:T(8,128)S(1)}, f32[80,256]{1,0:T(8,128)S(1)}, u32[]{:S(2)}, u32[]{:S(2)}) %collective-permute-start.18) | collective-permute-done | bytes 81952 | tf_op jit(solution)/shard_map/ppermute | solution.py:346
  58.5 8.8 %finish_kernel.1 = (f32[256,256]{1,0:T(8,128)}, f32[256,256]{1,0:T(8,128)}) custom-call(s32[1]{0:T(128)} %bitcast.core_ref, f32[80,256]{1,0:T(8,128)S(1)} %add_add_fusion.half_ref, f32[80,256]{1,0:T(8,128)S(1)} %collective-permute-done.18.other_ref, f32[256,256]{1,0:T(8,128)S(1)} %get-tuple-element.31.picked_ref), custom_call_target="tpu_custom_call" | custom-call | tf_op jit(solution)/shard_map/finish_kernel/pallas_call | solution.py:28
  (33 shorter events, 5.1 us)
Async XLA Ops:
  2.4 1.2 %copy-start.1 = (s32[1,1,256]{2,1,0:T(1,128)S(1)}, s32[1,1,256]{2,1,0:T(1,128)}, u32[]{:S(2)}) copy-start(s32[1,1,256]{2,1,0:T(1,128)} %param.9) | copy-start | bytes 3076
  2.5 11.9 %collective-permute-start.3 = (bf16[128,1024]{1,0:T(8,128)(2,1)S(1)}, bf16[128,1024]{1,0:T(8,128)(2,1)S(1)}, u32[]{:S(2)}, u32[]{:S(2)}) collective-permute-start(bf16[128,1024]{1,0:T(8,128)(2,1)S(1)} %get-tuple-element.22), channel_id=1, source_target_pairs={{0,1},{2,3},{4,5},{6,7},{1,0},{3,2},{5,4},{7,6},{8,9},{10,11},{12,... | collective-permute-start | bytes 786440 | tf_op jit(solution)/shard_map/ppermute | solution.py:405
  3.0 11.4 %collective-permute-start.4 = (bf16[128,1024]{1,0:T(8,128)(2,1)S(1)}, bf16[128,1024]{1,0:T(8,128)(2,1)S(1)}, u32[]{:S(2)}, u32[]{:S(2)}) collective-permute-start(bf16[128,1024]{1,0:T(8,128)(2,1)S(1)} %get-tuple-element.22), channel_id=1, source_target_pairs={{1,2},{3,4},{5,6},{2,1},{4,3},{6,5},{9,10},{11,12},{13,14},{10,9},... | collective-permute-start | bytes 786440 | tf_op jit(solution)/shard_map/ppermute | solution.py:397
  3.7 10.0 %collective-permute-start = (s32[1,256]{1,0:T(1,128)S(1)}, s32[1,256]{1,0:T(1,128)S(1)}, u32[]{:S(2)}, u32[]{:S(2)}) collective-permute-start(s32[1,256]{1,0:T(1,128)S(1)} %bitcast.19), channel_id=1, source_target_pairs={{0,2},{1,3},{2,0},{3,1},{4,6},{5,7},{6,4},{7,5},{8,10},{9,11},{10,... | collective-permute-start | bytes 3080 | tf_op jit(solution)/shard_map/ppermute | solution.py:304
  7.5 6.9 %collective-permute-start.5 = (bf16[128,128]{1,0:T(8,128)(2,1)S(1)}, bf16[128,128]{1,0:T(8,128)(2,1)S(1)}, u32[]{:S(2)}, u32[]{:S(2)}) collective-permute-start(bf16[128,128]{1,0:T(8,128)(2,1)S(1)} %get-tuple-element.23), channel_id=1, source_target_pairs={{0,8},{16,24},{8,0},{24,16},{1,9},{17,25},{9,1},{25,17},{2,10},{18... | collective-permute-start | bytes 98312 | tf_op jit(solution)/shard_map/ppermute | solution.py:398
  9.7 4.7 %collective-permute-start.6 = (bf16[128,128]{1,0:T(8,128)(2,1)S(1)}, bf16[128,128]{1,0:T(8,128)(2,1)S(1)}, u32[]{:S(2)}, u32[]{:S(2)}) collective-permute-start(bf16[128,128]{1,0:T(8,128)(2,1)S(1)} %get-tuple-element.24), channel_id=1, source_target_pairs={{8,16},{16,8},{9,17},{17,9},{10,18},{18,10},{11,19},{19,11},{12,20... | collective-permute-start | bytes 98312 | tf_op jit(solution)/shard_map/ppermute | solution.py:399
  12.8 1.6 %copy-start = (s32[1,8,128]{2,1,0:T(8,128)S(1)}, s32[1,8,128]{2,1,0:T(8,128)}, u32[]{:S(2)}) copy-start(s32[1,8,128]{2,1,0:T(8,128)} %param.8) | copy-start | bytes 12292
  13.7 5.4 %collective-permute-start.2 = (bf16[192,1024]{1,0:T(8,128)(2,1)S(1)}, bf16[192,1024]{1,0:T(8,128)(2,1)S(1)}, u32[]{:S(2)}, u32[]{:S(2)}) collective-permute-start(bf16[192,1024]{1,0:T(8,128)(2,1)S(1)} %get-tuple-element.20.pair_ref), channel_id=1, source_target_pairs={{0,1},{2,3},{4,5},{6,7},{1,0},{3,2},{5,4},{7,6},{8,9},{10,11},{12,... | collective-permute-start | bytes 1179656 | tf_op jit(solution)/shard_map/ppermute | solution.py:407
  15.3 3.8 %collective-permute-start.7 = (bf16[192,1024]{1,0:T(8,128)(2,1)S(1)}, bf16[192,1024]{1,0:T(8,128)(2,1)S(1)}, u32[]{:S(2)}, u32[]{:S(2)}) collective-permute-start(bf16[192,1024]{1,0:T(8,128)(2,1)S(1)} %curl_kernel.1.current_ref), channel_id=1, source_target_pairs={{0,1},{1,0},{2,3},{3,2},{4,5},{5,4},{6,7},{7,6},{8,9},{9,8},{10,11... | collective-permute-start | bytes 1179656 | tf_op jit(solution)/shard_map/ppermute | solution.py:313
  15.4 3.6 %collective-permute-start.1 = (s32[2,256]{1,0:T(2,128)S(1)}, s32[2,256]{1,0:T(2,128)S(1)}, u32[]{:S(2)}, u32[]{:S(2)}) collective-permute-start(s32[2,256]{1,0:T(2,128)S(1)} %pad_add_fusion), channel_id=1, source_target_pairs={{0,4},{1,5},{2,6},{3,7},{4,0},{5,1},{6,2},{7,3},{8,12},{9,13},{10,... | collective-permute-start | bytes 6152 | tf_op jit(solution)/shard_map/ppermute | solution.py:304
  21.0 10.3 %collective-permute-start.10 = (f32[512,128]{1,0:T(8,128)S(1)}, f32[512,128]{1,0:T(8,128)S(1)}, u32[]{:S(2)}, u32[]{:S(2)}) collective-permute-start(f32[512,128]{1,0:T(8,128)S(1)} %get-tuple-element.29), channel_id=1, source_target_pairs={{0,6},{1,7},{2,4},{3,5},{4,2},{5,3},{6,0},{7,1},{8,14},{9,15},{10,... | collective-permute-start | bytes 786440 | tf_op jit(solution)/shard_map/ppermute | solution.py:318
  24.1 11.2 %collective-permute-start.8 = (f32[512,128]{1,0:T(8,128)S(1)}, f32[512,128]{1,0:T(8,128)S(1)}, u32[]{:S(2)}, u32[]{:S(2)}) collective-permute-start(f32[512,128]{1,0:T(8,128)S(1)} %get-tuple-element.27), channel_id=1, source_target_pairs={{0,2},{1,3},{2,0},{3,1},{4,6},{5,7},{6,4},{7,5},{8,10},{9,11},{10,... | collective-permute-start | bytes 786440 | tf_op jit(solution)/shard_map/ppermute | solution.py:318
  24.2 11.1 %collective-permute-start.9 = (f32[512,128]{1,0:T(8,128)S(1)}, f32[512,128]{1,0:T(8,128)S(1)}, u32[]{:S(2)}, u32[]{:S(2)}) collective-permute-start(f32[512,128]{1,0:T(8,128)S(1)} %get-tuple-element.28), channel_id=1, source_target_pairs={{0,4},{1,5},{2,6},{3,7},{4,0},{5,1},{6,2},{7,3},{8,12},{9,13},{10,... | collective-permute-start | bytes 786440 | tf_op jit(solution)/shard_map/ppermute | solution.py:318
  36.3 1.3 %collective-permute-start.11 = (f32[80,256]{1,0:T(8,128)S(1)}, f32[80,256]{1,0:T(8,128)S(1)}, u32[]{:S(2)}, u32[]{:S(2)}) collective-permute-start(f32[80,256]{1,0:T(8,128)S(1)} %slice_select_fusion), channel_id=1, source_target_pairs={{0,1},{1,0},{2,3},{3,2},{4,5},{5,4},{6,7},{7,6},{8,9},{9,8},{10,11... | collective-permute-start | bytes 245768 | tf_op jit(solution)/shard_map/ppermute | solution.py:343
  37.7 4.6 %collective-permute-start.12 = (f32[80,256]{1,0:T(8,128)S(1)}, f32[80,256]{1,0:T(8,128)S(1)}, u32[]{:S(2)}, u32[]{:S(2)}) collective-permute-start(f32[80,256]{1,0:T(8,128)S(1)} %select_add_fusion), channel_id=1, source_target_pairs={{0,2},{1,3},{2,0},{3,1},{4,6},{5,7},{6,4},{7,5},{8,10},{9,11},{10,... | collective-permute-start | bytes 245768 | tf_op jit(solution)/shard_map/ppermute | solution.py:344
  39.5 4.5 %collective-permute-start.13 = (f32[80,256]{1,0:T(8,128)S(1)}, f32[80,256]{1,0:T(8,128)S(1)}, u32[]{:S(2)}, u32[]{:S(2)}) collective-permute-start(f32[80,256]{1,0:T(8,128)S(1)} %select_add_fusion), channel_id=1, source_target_pairs={{0,4},{1,5},{2,6},{3,7},{4,0},{5,1},{6,2},{7,3},{8,12},{9,13},{10,... | collective-permute-start | bytes 245768 | tf_op jit(solution)/shard_map/ppermute | solution.py:344
  40.8 5.3 %collective-permute-start.14 = (f32[80,256]{1,0:T(8,128)S(1)}, f32[80,256]{1,0:T(8,128)S(1)}, u32[]{:S(2)}, u32[]{:S(2)}) collective-permute-start(f32[80,256]{1,0:T(8,128)S(1)} %select_add_fusion), channel_id=1, source_target_pairs={{0,6},{1,7},{2,4},{3,5},{4,2},{5,3},{6,0},{7,1},{8,14},{9,15},{10,... | collective-permute-start | bytes 245768 | tf_op jit(solution)/shard_map/ppermute | solution.py:344
  46.2 5.8 %collective-permute-start.15 = (f32[80,256]{1,0:T(8,128)S(1)}, f32[80,256]{1,0:T(8,128)S(1)}, u32[]{:S(2)}, u32[]{:S(2)}) collective-permute-start(f32[80,256]{1,0:T(8,128)S(1)} %add_add_fusion.1), channel_id=1, source_target_pairs={{0,8},{8,0},{16,24},{24,16},{1,9},{9,1},{17,25},{25,17},{2,10},{10... | collective-permute-start | bytes 245768 | tf_op jit(solution)/shard_map/ppermute | solution.py:345
  49.5 7.7 %collective-permute-start.16 = (f32[80,256]{1,0:T(8,128)S(1)}, f32[80,256]{1,0:T(8,128)S(1)}, u32[]{:S(2)}, u32[]{:S(2)}) collective-permute-start(f32[80,256]{1,0:T(8,128)S(1)} %add_add_fusion.1), channel_id=1, source_target_pairs={{0,16},{8,24},{16,0},{24,8},{1,17},{9,25},{17,1},{25,9},{2,18},{10... | collective-permute-start | bytes 245768 | tf_op jit(solution)/shard_map/ppermute | solution.py:345
  50.4 6.8 %collective-permute-start.17 = (f32[80,256]{1,0:T(8,128)S(1)}, f32[80,256]{1,0:T(8,128)S(1)}, u32[]{:S(2)}, u32[]{:S(2)}) collective-permute-start(f32[80,256]{1,0:T(8,128)S(1)} %add_add_fusion.1), channel_id=1, source_target_pairs={{0,24},{8,16},{16,8},{24,0},{1,25},{9,17},{17,9},{25,1},{2,26},{10... | collective-permute-start | bytes 245768 | tf_op jit(solution)/shard_map/ppermute | solution.py:345
  57.2 1.3 %collective-permute-start.18 = (f32[80,256]{1,0:T(8,128)S(1)}, f32[80,256]{1,0:T(8,128)S(1)}, u32[]{:S(2)}, u32[]{:S(2)}) collective-permute-start(f32[80,256]{1,0:T(8,128)S(1)} %add_add_fusion.half_ref), channel_id=1, source_target_pairs={{0,1},{1,0},{2,3},{3,2},{4,5},{5,4},{6,7},{7,6},{8,9},{9,8},{10,11... | collective-permute-start | bytes 245768 | tf_op jit(solution)/shard_map/ppermute | solution.py:346

commit v5 on v4

--- a/solution.py
+++ b/solution.py
@@ -10,6 +10,7 @@
 MESH_AXES = ("row", "mix")
 ROWS = 8
 LANES = 128
+NEAR = 4
 NN, NT, TN = ((1,), (0,)), ((1,), (1,)), ((0,), (0,))
 SMEM = pl.BlockSpec(memory_space=pltpu.SMEM)
 VMEM = pl.BlockSpec(memory_space=pltpu.VMEM)
@@ -212,6 +213,20 @@
     )
 
 
+def in_three(x):
+    high = x.astype(jnp.bfloat16)
+    left = x - high.astype(jnp.float32)
+    middle = left.astype(jnp.bfloat16)
+    return high, middle, (left - middle.astype(jnp.float32)).astype(jnp.bfloat16)
+
+
+def outer(a, b):
+    (a0, a1, a2), (b0, b1, b2) = in_three(a), in_three(b)
+    left = jnp.concatenate([a0, a0, a1, a0, a2, a1])
+    right = jnp.concatenate([b0, b1, b0, b2, b0, b1])
+    return lax.dot_general(left, right, (TN, ((), ())), preferred_element_type=jnp.float32)
+
+
 def eliminate(a_ref, z_ref):
     n = a_ref.shape[0]
     blocks = n // ROWS
@@ -255,7 +270,7 @@
                     next_old[c] = next_old[c] - times * pivots[k, c]
                 rest[g] = rest[g] - times * top[k]
                 rest_z[g] = rest_z[g] - times * top_z[k]
-        for g in range(b + 2, blocks):
+        for g in range(b + 2, min(b + NEAR, blocks)):
             old = [column(rest[g], start + c) for c in range(ROWS)]
             for k in range(ROWS):
                 times = old[k] * inverse[k]
@@ -268,8 +283,16 @@
             scale = lax.rsqrt(pivots[k, k])
             done = jnp.where(row == k, top[k] * scale, done)
             done_z = jnp.where(row == k, top_z[k] * scale, done_z)
-        a_ref[start : start + ROWS, :] = jnp.where(lane >= row + start, done, 0.0)
+        done = jnp.where(lane >= row + start, done, 0.0)
+        a_ref[start : start + ROWS, :] = done
         z_ref[start : start + ROWS, :] = done_z
+        far = (b + NEAR) * ROWS
+        if far < n:
+            update = outer(done[:, far:], jnp.concatenate([done, done_z], axis=1))
+            for g in range(b + NEAR, blocks):
+                low = g * ROWS - far
+                rest[g] = rest[g] - update[low : low + ROWS, :n]
+                rest_z[g] = rest_z[g] - update[low : low + ROWS, n:]
 
 
 def pack(gram, packed_ref):
@@ -342,7 +365,7 @@
     half = jnp.where(core == 0, low, high)
     half = half + lax.ppermute(jnp.where(core == 0, high, low), "mix", xor_route(planes, 1))
     half = half + sum(lax.ppermute(half, "mix", xor_route(planes, k)) for k in range(2, planes, 2))
-    half = half + sum(lax.ppermute(half, "row", xor_route(blocks, k)) for k in range(1, blocks))
+    half = half + sum(lax.ppermute(half, "row", xor_route(blocks, k)) for k in range(blocks - 1, 0, -1))
     return half, lax.ppermute(half, "mix", xor_route(planes, 1)), core
 
 

time: 67.5 us -> 65.6 us (0.972)
  Pallas kernels: 16.9 us -> 15.5 us
  starting transfers between devices: 23.5 us -> 22.6 us
    pallas_call x4, Pallas kernels: 12.6 us -> 11.3 us  [local(): pl.pallas_call(kernel, out_shape=[jax.ShapeDtypeStruct(shape, dtype) for...]
    ppermute x3, starting transfers between devices: 5.77 us -> 4.79 us  [sum_over_mesh(): lax.ppermute(half, 'row', xor_route(blocks, k))]
where the time goes in v5:
time: 65.6 us; the launch traced here: 65.4 us
  waiting for transfers between devices  26.2 us (40%)
  starting transfers between devices  22.6 us (34%)
  Pallas kernels  15.5 us (24%)
  between operations  0.81 us (1%)
    pallas_call x4, Pallas kernels, local(): pl.pallas_call(kernel, out_shape=[jax.ShapeDtypeStruct(shape, dtype) for...  11.3 us
    ppermute x3, waiting for transfers between devices, sampled_mixing(): lax.ppermute(part, 'mix', xor_route(planes, k))  10.4 us
    ppermute x3, waiting for transfers between devices, sum_over_mesh(): lax.ppermute(half, 'row', xor_route(blocks, k))  5.61 us
    ppermute x2, starting transfers between devices, doubled(): lax.ppermute(rows, 'mix', xor_route(lax.axis_size('mix'), bit))  5.47 us
    ppermute x3, waiting for transfers between devices, sum_over_mesh(): lax.ppermute(half, 'mix', xor_route(planes, k))  4.87 us
    ppermute x3, starting transfers between devices, sum_over_mesh(): lax.ppermute(half, 'row', xor_route(blocks, k))  4.79 us
    pallas_call x2, Pallas kernels, relay(): pl.pallas_call(kernel, out_shape=[jax.ShapeDtypeStruct(shape, dtype) for...  4.23 us
    ppermute x3, starting transfers between devices, sampled_mixing(): lax.ppermute(part, 'mix', xor_route(planes, k))  3.8 us
  transfers between devices with their start and end apart: 19, of which 11 were waited for; matrix products, arithmetic and copies ran while one was open for 0% of the time, Pallas kernels for 5%

profile of v5, /device:TPU:0, one launch (start us, length us, event | category | flops | bytes accessed | tf_op | source)
XLA Modules:
  0.0 65.4 jit_solution(10692162331223750561)
XLA Ops:
  0.7 1.7 %field_kernel.1 = (bf16[192,1024]{1,0:T(8,128)(2,1)S(1)}, bf16[128,1024]{1,0:T(8,128)(2,1)S(1)}, bf16[128,128]{1,0:T(8,128)(2,1)S(1)}, bf16[128,128]{1,0:T(8,128)(2,1)S(1)}) custom-call(s32[2]{0:T(128)S(1)} %pad_add_fusion.1.flags_ref, bf16[64,3,8,128]{3,2,1,0:T(8,128)(2,1)} %bitcast.17), custom_call_target="tpu_custom_call" | custom-call | tf_op jit(solution)/shard_map/field_kernel/pallas_call | solution.py:116
  3.7 3.8 %collective-permute-start = (s32[1,256]{1,0:T(1,128)S(1)}, s32[1,256]{1,0:T(1,128)S(1)}, u32[]{:S(2)}, u32[]{:S(2)}) collective-permute-start(s32[1,256]{1,0:T(1,128)S(1)} %bitcast.19), channel_id=1, source_target_pairs={{0,2},{1,3},{2,0},{3,1},{4,6},{5,7},{6,4},{7,5},{8,10},{9,11},{10,... | collective-permute-start | bytes 3080 | tf_op jit(solution)/shard_map/ppermute | solution.py:327
  7.5 2.2 %collective-permute-start.5 = (bf16[128,128]{1,0:T(8,128)(2,1)S(1)}, bf16[128,128]{1,0:T(8,128)(2,1)S(1)}, u32[]{:S(2)}, u32[]{:S(2)}) collective-permute-start(bf16[128,128]{1,0:T(8,128)(2,1)S(1)} %get-tuple-element.23), channel_id=1, source_target_pairs={{0,8},{16,24},{8,0},{24,16},{1,9},{17,25},{9,1},{25,17},{2,10},{18... | collective-permute-start | bytes 98312 | tf_op jit(solution)/shard_map/ppermute | solution.py:421
  10.3 2.5 %velocity_kernel.1 = (bf16[192,1024]{1,0:T(8,128)(2,1)S(1)}, bf16[384,256]{1,0:T(8,128)(2,1)S(1)}) custom-call(s32[2]{0:T(128)S(1)} %pad_add_fusion.1.flags_ref, bf16[64,3,8,128]{3,2,1,0:T(8,128)(2,1)} %bitcast.18, s32[384,256]{1,0:T(8,128)} %test_ref.1, s32[8,128]{1,0:T(8,128)} %bitcast.14), custom_call_target="tpu_custom_call" | custom-call | tf_op jit(solution)/shard_map/velocity_kernel/pallas_call | solution.py:116
  14.4 0.9 %curl_kernel.1.current_ref = bf16[192,1024]{1,0:T(8,128)(2,1)S(1)} custom-call(s32[2]{0:T(128)S(1)} %pad_add_fusion.1.flags_ref, bf16[192,1024]{1,0:T(8,128)(2,1)S(1)} %get-tuple-element.21.field_ref, bf16[128,1024]{1,0:T(8,128)(2,1)S(1)} %collective-permute-done.3.plane_a_ref, bf16[128,1024]{1,0:T(8,128)(2,1)S(1)} %collective-permute-done.4.plane_b_ref, ...), custom_call_target="tpu_custom_call" | custom-call | tf_op jit(solution)/shard_map/curl_kernel/pallas_call | solution.py:29
  15.4 1.6 %collective-permute-start.1 = (s32[2,256]{1,0:T(2,128)S(1)}, s32[2,256]{1,0:T(2,128)S(1)}, u32[]{:S(2)}, u32[]{:S(2)}) collective-permute-start(s32[2,256]{1,0:T(2,128)S(1)} %pad_add_fusion), channel_id=1, source_target_pairs={{0,4},{1,5},{2,6},{3,7},{4,0},{5,1},{6,2},{7,3},{8,12},{9,13},{10,... | collective-permute-start | bytes 6152 | tf_op jit(solution)/shard_map/ppermute | solution.py:327
  17.1 2.0 %collective-permute-done.1 = s32[2,256]{1,0:T(2,128)S(1)} collective-permute-done((s32[2,256]{1,0:T(2,128)S(1)}, s32[2,256]{1,0:T(2,128)S(1)}, u32[]{:S(2)}, u32[]{:S(2)}) %collective-permute-start.1) | collective-permute-done | bytes 2080 | tf_op jit(solution)/shard_map/ppermute | solution.py:327
  19.1 1.9 %parts_kernel.1 = (f32[512,128]{1,0:T(8,128)S(1)}, f32[512,128]{1,0:T(8,128)S(1)}, f32[512,128]{1,0:T(8,128)S(1)}, f32[512,128]{1,0:T(8,128)S(1)}) custom-call(s32[2]{0:T(128)S(1)} %pad_add_fusion.1.flags_ref, s32[1024]{0:T(1024)S(1)} %bitcast.16, bf16[192,1024]{1,0:T(8,128)(2,1)S(1)} %get-tuple-element.20.pair_ref, ...), custom_call_target="tpu_custom_call" | custom-call | tf_op jit(solution)/shard_map/parts_kernel/pallas_call | solution.py:29
  21.0 3.1 %collective-permute-start.10 = (f32[512,128]{1,0:T(8,128)S(1)}, f32[512,128]{1,0:T(8,128)S(1)}, u32[]{:S(2)}, u32[]{:S(2)}) collective-permute-start(f32[512,128]{1,0:T(8,128)S(1)} %get-tuple-element.29), channel_id=1, source_target_pairs={{0,6},{1,7},{2,4},{3,5},{4,2},{5,3},{6,0},{7,1},{8,14},{9,15},{10,... | collective-permute-start | bytes 786440 | tf_op jit(solution)/shard_map/ppermute | solution.py:341
  24.9 6.5 %collective-permute-done.10.refs_3_ = f32[512,128]{1,0:T(8,128)S(1)} collective-permute-done((f32[512,128]{1,0:T(8,128)S(1)}, f32[512,128]{1,0:T(8,128)S(1)}, u32[]{:S(2)}, u32[]{:S(2)}) %collective-permute-start.10) | collective-permute-done | bytes 262176 | tf_op jit(solution)/shard_map/ppermute | solution.py:341
  31.4 3.9 %collective-permute-done.8.refs_1_ = f32[512,128]{1,0:T(8,128)S(1)} collective-permute-done((f32[512,128]{1,0:T(8,128)S(1)}, f32[512,128]{1,0:T(8,128)S(1)}, u32[]{:S(2)}, u32[]{:S(2)}) %collective-permute-start.8) | collective-permute-done | bytes 262176 | tf_op jit(solution)/shard_map/ppermute | solution.py:341
  35.3 1.0 %gram_kernel.1 = (f32[256,256]{1,0:T(8,128)S(1)}, f32[160,256]{1,0:T(8,128)S(1)}) custom-call(f32[5]{0:T(128)S(1)} %stack.26.signs_ref, f32[512,128]{1,0:T(8,128)S(1)} %get-tuple-element.26.refs_0_, f32[512,128]{1,0:T(8,128)S(1)} %collective-permute-done.8.refs_1_, f32[512,128]{1,0:T(8,128)S(1)} %collective-permute-done.9.refs_2_, ...), custom_call_target="tpu_custom_call" | custom-call | tf_op jit(solution)/shard_map/gram_kernel/pallas_call | solution.py:29
  36.4 1.3 %collective-permute-done.11 = f32[80,256]{1,0:T(8,128)S(1)} collective-permute-done((f32[80,256]{1,0:T(8,128)S(1)}, f32[80,256]{1,0:T(8,128)S(1)}, u32[]{:S(2)}, u32[]{:S(2)}) %collective-permute-start.11) | collective-permute-done | bytes 81952 | tf_op jit(solution)/shard_map/ppermute | solution.py:366
  37.7 1.8 %collective-permute-start.12 = (f32[80,256]{1,0:T(8,128)S(1)}, f32[80,256]{1,0:T(8,128)S(1)}, u32[]{:S(2)}, u32[]{:S(2)}) collective-permute-start(f32[80,256]{1,0:T(8,128)S(1)} %select_add_fusion), channel_id=1, source_target_pairs={{0,2},{1,3},{2,0},{3,1},{4,6},{5,7},{6,4},{7,5},{8,10},{9,11},{10,... | collective-permute-start | bytes 245768 | tf_op jit(solution)/shard_map/ppermute | solution.py:367
  39.5 1.3 %collective-permute-start.13 = (f32[80,256]{1,0:T(8,128)S(1)}, f32[80,256]{1,0:T(8,128)S(1)}, u32[]{:S(2)}, u32[]{:S(2)}) collective-permute-start(f32[80,256]{1,0:T(8,128)S(1)} %select_add_fusion), channel_id=1, source_target_pairs={{0,4},{1,5},{2,6},{3,7},{4,0},{5,1},{6,2},{7,3},{8,12},{9,13},{10,... | collective-permute-start | bytes 245768 | tf_op jit(solution)/shard_map/ppermute | solution.py:367
  41.3 1.0 %collective-permute-done.12 = f32[80,256]{1,0:T(8,128)S(1)} collective-permute-done((f32[80,256]{1,0:T(8,128)S(1)}, f32[80,256]{1,0:T(8,128)S(1)}, u32[]{:S(2)}, u32[]{:S(2)}) %collective-permute-start.12) | collective-permute-done | bytes 81952 | tf_op jit(solution)/shard_map/ppermute | solution.py:367
  42.3 1.7 %collective-permute-done.13 = f32[80,256]{1,0:T(8,128)S(1)} collective-permute-done((f32[80,256]{1,0:T(8,128)S(1)}, f32[80,256]{1,0:T(8,128)S(1)}, u32[]{:S(2)}, u32[]{:S(2)}) %collective-permute-start.13) | collective-permute-done | bytes 81952 | tf_op jit(solution)/shard_map/ppermute | solution.py:367
  44.0 2.2 %collective-permute-done.14 = f32[80,256]{1,0:T(8,128)S(1)} collective-permute-done((f32[80,256]{1,0:T(8,128)S(1)}, f32[80,256]{1,0:T(8,128)S(1)}, u32[]{:S(2)}, u32[]{:S(2)}) %collective-permute-start.14) | collective-permute-done | bytes 81952 | tf_op jit(solution)/shard_map/ppermute | solution.py:367
  46.2 3.7 %collective-permute-start.15 = (f32[80,256]{1,0:T(8,128)S(1)}, f32[80,256]{1,0:T(8,128)S(1)}, u32[]{:S(2)}, u32[]{:S(2)}) collective-permute-start(f32[80,256]{1,0:T(8,128)S(1)} %add_add_fusion.1), channel_id=1, source_target_pairs={{0,24},{8,16},{16,8},{24,0},{1,25},{9,17},{17,9},{25,1},{2,26},{10... | collective-permute-start | bytes 245768 | tf_op jit(solution)/shard_map/ppermute | solution.py:368
  49.8 1.1 %collective-permute-start.16 = (f32[80,256]{1,0:T(8,128)S(1)}, f32[80,256]{1,0:T(8,128)S(1)}, u32[]{:S(2)}, u32[]{:S(2)}) collective-permute-start(f32[80,256]{1,0:T(8,128)S(1)} %add_add_fusion.1), channel_id=1, source_target_pairs={{0,16},{8,24},{16,0},{24,8},{1,17},{9,25},{17,1},{25,9},{2,18},{10... | collective-permute-start | bytes 245768 | tf_op jit(solution)/shard_map/ppermute | solution.py:368
  51.0 2.4 %collective-permute-done.15 = f32[80,256]{1,0:T(8,128)S(1)} collective-permute-done((f32[80,256]{1,0:T(8,128)S(1)}, f32[80,256]{1,0:T(8,128)S(1)}, u32[]{:S(2)}, u32[]{:S(2)}) %collective-permute-start.15) | collective-permute-done | bytes 81952 | tf_op jit(solution)/shard_map/ppermute | solution.py:368
  53.3 3.2 %collective-permute-done.16 = f32[80,256]{1,0:T(8,128)S(1)} collective-permute-done((f32[80,256]{1,0:T(8,128)S(1)}, f32[80,256]{1,0:T(8,128)S(1)}, u32[]{:S(2)}, u32[]{:S(2)}) %collective-permute-start.16) | collective-permute-done | bytes 81952 | tf_op jit(solution)/shard_map/ppermute | solution.py:368
  56.7 1.3 %collective-permute-done.18.other_ref = f32[80,256]{1,0:T(8,128)S(1)} collective-permute-done((f32[80,256]{1,0:T(8,128)S(1)}, f32[80,256]{1,0:T(8,128)S(1)}, u32[]{:S(2)}, u32[]{:S(2)}) %collective-permute-start.18) | collective-permute-done | bytes 81952 | tf_op jit(solution)/shard_map/ppermute | solution.py:369
  57.9 7.4 %finish_kernel.1 = (f32[256,256]{1,0:T(8,128)}, f32[256,256]{1,0:T(8,128)}) custom-call(s32[1]{0:T(128)} %bitcast.core_ref, f32[80,256]{1,0:T(8,128)S(1)} %add_add_fusion.half_ref, f32[80,256]{1,0:T(8,128)S(1)} %collective-permute-done.18.other_ref, f32[256,256]{1,0:T(8,128)S(1)} %get-tuple-element.31.picked_ref), custom_call_target="tpu_custom_call" | custom-call | tf_op jit(solution)/shard_map/finish_kernel/pallas_call | solution.py:29
  (33 shorter events, 5.1 us)
Async XLA Ops:
  2.4 1.2 %copy-start.1 = (s32[1,1,256]{2,1,0:T(1,128)S(1)}, s32[1,1,256]{2,1,0:T(1,128)}, u32[]{:S(2)}) copy-start(s32[1,1,256]{2,1,0:T(1,128)} %param.9) | copy-start | bytes 3076
  2.5 11.9 %collective-permute-start.3 = (bf16[128,1024]{1,0:T(8,128)(2,1)S(1)}, bf16[128,1024]{1,0:T(8,128)(2,1)S(1)}, u32[]{:S(2)}, u32[]{:S(2)}) collective-permute-start(bf16[128,1024]{1,0:T(8,128)(2,1)S(1)} %get-tuple-element.22), channel_id=1, source_target_pairs={{0,1},{2,3},{4,5},{6,7},{1,0},{3,2},{5,4},{7,6},{8,9},{10,11},{12,... | collective-permute-start | bytes 786440 | tf_op jit(solution)/shard_map/ppermute | solution.py:428
  3.0 11.4 %collective-permute-start.4 = (bf16[128,1024]{1,0:T(8,128)(2,1)S(1)}, bf16[128,1024]{1,0:T(8,128)(2,1)S(1)}, u32[]{:S(2)}, u32[]{:S(2)}) collective-permute-start(bf16[128,1024]{1,0:T(8,128)(2,1)S(1)} %get-tuple-element.22), channel_id=1, source_target_pairs={{1,2},{3,4},{5,6},{2,1},{4,3},{6,5},{9,10},{11,12},{13,14},{10,9},... | collective-permute-start | bytes 786440 | tf_op jit(solution)/shard_map/ppermute | solution.py:420
  3.7 10.0 %collective-permute-start = (s32[1,256]{1,0:T(1,128)S(1)}, s32[1,256]{1,0:T(1,128)S(1)}, u32[]{:S(2)}, u32[]{:S(2)}) collective-permute-start(s32[1,256]{1,0:T(1,128)S(1)} %bitcast.19), channel_id=1, source_target_pairs={{0,2},{1,3},{2,0},{3,1},{4,6},{5,7},{6,4},{7,5},{8,10},{9,11},{10,... | collective-permute-start | bytes 3080 | tf_op jit(solution)/shard_map/ppermute | solution.py:327
  7.5 6.9 %collective-permute-start.5 = (bf16[128,128]{1,0:T(8,128)(2,1)S(1)}, bf16[128,128]{1,0:T(8,128)(2,1)S(1)}, u32[]{:S(2)}, u32[]{:S(2)}) collective-permute-start(bf16[128,128]{1,0:T(8,128)(2,1)S(1)} %get-tuple-element.23), channel_id=1, source_target_pairs={{0,8},{16,24},{8,0},{24,16},{1,9},{17,25},{9,1},{25,17},{2,10},{18... | collective-permute-start | bytes 98312 | tf_op jit(solution)/shard_map/ppermute | solution.py:421
  9.7 4.7 %collective-permute-start.6 = (bf16[128,128]{1,0:T(8,128)(2,1)S(1)}, bf16[128,128]{1,0:T(8,128)(2,1)S(1)}, u32[]{:S(2)}, u32[]{:S(2)}) collective-permute-start(bf16[128,128]{1,0:T(8,128)(2,1)S(1)} %get-tuple-element.24), channel_id=1, source_target_pairs={{8,16},{16,8},{9,17},{17,9},{10,18},{18,10},{11,19},{19,11},{12,20... | collective-permute-start | bytes 98312 | tf_op jit(solution)/shard_map/ppermute | solution.py:422
  12.8 1.6 %copy-start = (s32[1,8,128]{2,1,0:T(8,128)S(1)}, s32[1,8,128]{2,1,0:T(8,128)}, u32[]{:S(2)}) copy-start(s32[1,8,128]{2,1,0:T(8,128)} %param.8) | copy-start | bytes 12292
  13.7 5.4 %collective-permute-start.2 = (bf16[192,1024]{1,0:T(8,128)(2,1)S(1)}, bf16[192,1024]{1,0:T(8,128)(2,1)S(1)}, u32[]{:S(2)}, u32[]{:S(2)}) collective-permute-start(bf16[192,1024]{1,0:T(8,128)(2,1)S(1)} %get-tuple-element.20.pair_ref), channel_id=1, source_target_pairs={{0,1},{2,3},{4,5},{6,7},{1,0},{3,2},{5,4},{7,6},{8,9},{10,11},{12,... | collective-permute-start | bytes 1179656 | tf_op jit(solution)/shard_map/ppermute | solution.py:430
  15.3 3.8 %collective-permute-start.7 = (bf16[192,1024]{1,0:T(8,128)(2,1)S(1)}, bf16[192,1024]{1,0:T(8,128)(2,1)S(1)}, u32[]{:S(2)}, u32[]{:S(2)}) collective-permute-start(bf16[192,1024]{1,0:T(8,128)(2,1)S(1)} %curl_kernel.1.current_ref), channel_id=1, source_target_pairs={{0,1},{1,0},{2,3},{3,2},{4,5},{5,4},{6,7},{7,6},{8,9},{9,8},{10,11... | collective-permute-start | bytes 1179656 | tf_op jit(solution)/shard_map/ppermute | solution.py:336
  15.4 3.6 %collective-permute-start.1 = (s32[2,256]{1,0:T(2,128)S(1)}, s32[2,256]{1,0:T(2,128)S(1)}, u32[]{:S(2)}, u32[]{:S(2)}) collective-permute-start(s32[2,256]{1,0:T(2,128)S(1)} %pad_add_fusion), channel_id=1, source_target_pairs={{0,4},{1,5},{2,6},{3,7},{4,0},{5,1},{6,2},{7,3},{8,12},{9,13},{10,... | collective-permute-start | bytes 6152 | tf_op jit(solution)/shard_map/ppermute | solution.py:327
  21.0 10.3 %collective-permute-start.10 = (f32[512,128]{1,0:T(8,128)S(1)}, f32[512,128]{1,0:T(8,128)S(1)}, u32[]{:S(2)}, u32[]{:S(2)}) collective-permute-start(f32[512,128]{1,0:T(8,128)S(1)} %get-tuple-element.29), channel_id=1, source_target_pairs={{0,6},{1,7},{2,4},{3,5},{4,2},{5,3},{6,0},{7,1},{8,14},{9,15},{10,... | collective-permute-start | bytes 786440 | tf_op jit(solution)/shard_map/ppermute | solution.py:341
  24.1 11.2 %collective-permute-start.8 = (f32[512,128]{1,0:T(8,128)S(1)}, f32[512,128]{1,0:T(8,128)S(1)}, u32[]{:S(2)}, u32[]{:S(2)}) collective-permute-start(f32[512,128]{1,0:T(8,128)S(1)} %get-tuple-element.27), channel_id=1, source_target_pairs={{0,2},{1,3},{2,0},{3,1},{4,6},{5,7},{6,4},{7,5},{8,10},{9,11},{10,... | collective-permute-start | bytes 786440 | tf_op jit(solution)/shard_map/ppermute | solution.py:341
  24.2 11.1 %collective-permute-start.9 = (f32[512,128]{1,0:T(8,128)S(1)}, f32[512,128]{1,0:T(8,128)S(1)}, u32[]{:S(2)}, u32[]{:S(2)}) collective-permute-start(f32[512,128]{1,0:T(8,128)S(1)} %get-tuple-element.28), channel_id=1, source_target_pairs={{0,4},{1,5},{2,6},{3,7},{4,0},{5,1},{6,2},{7,3},{8,12},{9,13},{10,... | collective-permute-start | bytes 786440 | tf_op jit(solution)/shard_map/ppermute | solution.py:341
  36.3 1.3 %collective-permute-start.11 = (f32[80,256]{1,0:T(8,128)S(1)}, f32[80,256]{1,0:T(8,128)S(1)}, u32[]{:S(2)}, u32[]{:S(2)}) collective-permute-start(f32[80,256]{1,0:T(8,128)S(1)} %slice_select_fusion), channel_id=1, source_target_pairs={{0,1},{1,0},{2,3},{3,2},{4,5},{5,4},{6,7},{7,6},{8,9},{9,8},{10,11... | collective-permute-start | bytes 245768 | tf_op jit(solution)/shard_map/ppermute | solution.py:366
  37.7 4.6 %collective-permute-start.12 = (f32[80,256]{1,0:T(8,128)S(1)}, f32[80,256]{1,0:T(8,128)S(1)}, u32[]{:S(2)}, u32[]{:S(2)}) collective-permute-start(f32[80,256]{1,0:T(8,128)S(1)} %select_add_fusion), channel_id=1, source_target_pairs={{0,2},{1,3},{2,0},{3,1},{4,6},{5,7},{6,4},{7,5},{8,10},{9,11},{10,... | collective-permute-start | bytes 245768 | tf_op jit(solution)/shard_map/ppermute | solution.py:367
  39.5 4.5 %collective-permute-start.13 = (f32[80,256]{1,0:T(8,128)S(1)}, f32[80,256]{1,0:T(8,128)S(1)}, u32[]{:S(2)}, u32[]{:S(2)}) collective-permute-start(f32[80,256]{1,0:T(8,128)S(1)} %select_add_fusion), channel_id=1, source_target_pairs={{0,4},{1,5},{2,6},{3,7},{4,0},{5,1},{6,2},{7,3},{8,12},{9,13},{10,... | collective-permute-start | bytes 245768 | tf_op jit(solution)/shard_map/ppermute | solution.py:367
  40.8 5.3 %collective-permute-start.14 = (f32[80,256]{1,0:T(8,128)S(1)}, f32[80,256]{1,0:T(8,128)S(1)}, u32[]{:S(2)}, u32[]{:S(2)}) collective-permute-start(f32[80,256]{1,0:T(8,128)S(1)} %select_add_fusion), channel_id=1, source_target_pairs={{0,6},{1,7},{2,4},{3,5},{4,2},{5,3},{6,0},{7,1},{8,14},{9,15},{10,... | collective-permute-start | bytes 245768 | tf_op jit(solution)/shard_map/ppermute | solution.py:367
  46.2 7.2 %collective-permute-start.15 = (f32[80,256]{1,0:T(8,128)S(1)}, f32[80,256]{1,0:T(8,128)S(1)}, u32[]{:S(2)}, u32[]{:S(2)}) collective-permute-start(f32[80,256]{1,0:T(8,128)S(1)} %add_add_fusion.1), channel_id=1, source_target_pairs={{0,24},{8,16},{16,8},{24,0},{1,25},{9,17},{17,9},{25,1},{2,26},{10... | collective-permute-start | bytes 245768 | tf_op jit(solution)/shard_map/ppermute | solution.py:368
  49.8 6.7 %collective-permute-start.16 = (f32[80,256]{1,0:T(8,128)S(1)}, f32[80,256]{1,0:T(8,128)S(1)}, u32[]{:S(2)}, u32[]{:S(2)}) collective-permute-start(f32[80,256]{1,0:T(8,128)S(1)} %add_add_fusion.1), channel_id=1, source_target_pairs={{0,16},{8,24},{16,0},{24,8},{1,17},{9,25},{17,1},{25,9},{2,18},{10... | collective-permute-start | bytes 245768 | tf_op jit(solution)/shard_map/ppermute | solution.py:368
  51.0 5.6 %collective-permute-start.17 = (f32[80,256]{1,0:T(8,128)S(1)}, f32[80,256]{1,0:T(8,128)S(1)}, u32[]{:S(2)}, u32[]{:S(2)}) collective-permute-start(f32[80,256]{1,0:T(8,128)S(1)} %add_add_fusion.1), channel_id=1, source_target_pairs={{0,8},{8,0},{16,24},{24,16},{1,9},{9,1},{17,25},{25,17},{2,10},{10... | collective-permute-start | bytes 245768 | tf_op jit(solution)/shard_map/ppermute | solution.py:368
  56.6 1.3 %collective-permute-start.18 = (f32[80,256]{1,0:T(8,128)S(1)}, f32[80,256]{1,0:T(8,128)S(1)}, u32[]{:S(2)}, u32[]{:S(2)}) collective-permute-start(f32[80,256]{1,0:T(8,128)S(1)} %add_add_fusion.half_ref), channel_id=1, source_target_pairs={{0,1},{1,0},{2,3},{3,2},{4,5},{5,4},{6,7},{7,6},{8,9},{9,8},{10,11... | collective-permute-start | bytes 245768 | tf_op jit(solution)/shard_map/ppermute | solution.py:369

commit v6 on v5

--- a/solution.py
+++ b/solution.py
@@ -41,7 +41,7 @@
     return ref[:, x * width : (x + 1) * width]
 
 
-def to_lanes(source_ref, held_ref, sems, wide_ref, out_ref, signs_ref=None):
+def to_lanes(source_ref, held_ref, sems, wide_ref, out_ref, signs_ref=None, first=()):
     snaps, parts, depth, width = source_ref.shape
     pieces = sems.shape[0]
     step = snaps // pieces
@@ -51,8 +51,10 @@
         )
         for i in range(pieces)
     ]
-    for copy in copies:
+    for copy in [*first, *copies]:
         copy.start()
+    for copy in first:
+        copy.wait()
     tall = step * parts * depth
     for i, copy in enumerate(copies):
         copy.wait()
@@ -95,11 +97,9 @@
 ):
     snaps, parts = velocity_ref.shape[:2]
     copy_signs = pltpu.make_async_copy(signs_ref, held_signs_ref, signs_sem)
-    copy_signs.start()
     copy = pltpu.make_async_copy(test_ref, bits_ref, bits_sem)
     copy.start()
-    copy_signs.wait()
-    to_lanes(velocity_ref, held_ref, sems, wide_ref, pair_ref, held_signs_ref)
+    to_lanes(velocity_ref, held_ref, sems, wide_ref, pair_ref, held_signs_ref, [copy_signs])
     copy.wait()
     columns = bits_ref.shape[0]
     width = wide_ref.shape[1]
@@ -337,9 +337,11 @@
     inputs = (flags, wanted.reshape(-1) * halves, pair, other, current, other_current, matrix)
     scratch = ((current.shape[1] * halves, LANES),)
     parts = local(parts_kernel, inputs, [part] * targets, scratch, megabytes=12, scalars=2)
-    hops = range(2, planes, 2)
-    arrived = [parts[0]] + [lax.ppermute(part, "mix", xor_route(planes, k)) for part, k in zip(parts[1:], hops)]
-    return arrived, [parity_sign(mine, (mine ^ k) - mine % 2) for k in range(0, planes, 2)]
+    hops = [0]
+    for level in range(planes.bit_length() - 2, 0, -1):
+        hops += [hop ^ 1 << level for hop in hops]
+    arrived = [parts[0]] + [lax.ppermute(part, "mix", xor_route(planes, k)) for part, k in zip(parts[1:], hops[1:])]
+    return arrived, [parity_sign(mine, (mine ^ k) - mine % 2) for k in hops]
 
 
 def whole_mixing(pair, current, matrix, wanted):
@@ -415,7 +417,7 @@
     sampled = sampled_bytes < whole_bytes
     wanted = sample_index.reshape(1, -1)
     if sampled:
-        wanted = doubled(wanted, 2)
+        wanted = doubled(wanted, planes // 2)
     field, flat, rim_a, rim_b = relay(field_kernel, flags, [field_b[:, :, 0]], [], [lanes, flat, rim, rim])
     plane_b = lax.ppermute(flat, "mix", pair_route(planes, 1))
     rim_a = lax.ppermute(rim_a, "row", pair_route(blocks, 0))
@@ -429,7 +431,7 @@
     pair, wanted = lax.optimization_barrier((pair, wanted))
     other = lax.ppermute(pair, "mix", pair_route(planes, 0))
     if sampled:
-        for level in range(2, planes.bit_length() - 1):
+        for level in range(planes.bit_length() - 3, 0, -1):
             wanted = doubled(wanted, 1 << level)
     (current,) = local(curl_kernel, (flags, field, plane_a, plane_b, rim_a, rim_b, signs), [lanes])
     if sampled:

time: 65.6 us -> 65.1 us (level)
  waiting for transfers between devices: 26.2 us -> 24.8 us
  starting transfers between devices: 22.6 us -> 23.5 us
    ppermute x2, starting transfers between devices: 5.47 us -> 8.24 us  [doubled(): lax.ppermute(rows, 'mix', xor_route(lax.axis_size('mix'), bit))]
    ppermute x2, waiting for transfers between devices: 2.79 us -> 1.56 us  [doubled(): lax.ppermute(rows, 'mix', xor_route(lax.axis_size('mix'), bit))]
  transfers between devices with their start and end apart: 19 -> 19, of which waited for: 11 -> 9; matrix products, arithmetic and copies ran while one was open for 0% -> 0% of each run, Pallas kernels for 5% -> 4%
where the time goes in v6:
time: 65.1 us; the launch traced here: 64.8 us
  waiting for transfers between devices  24.8 us (38%)
  starting transfers between devices  23.5 us (36%)
  Pallas kernels  14.9 us (23%)
  between operations  0.85 us (1%)
    pallas_call x4, Pallas kernels, local(): pl.pallas_call(kernel, out_shape=[jax.ShapeDtypeStruct(shape, dtype) for...  11.3 us
    ppermute x3, waiting for transfers between devices, sampled_mixing(): lax.ppermute(part, 'mix', xor_route(planes, k))  10.4 us
    ppermute x2, starting transfers between devices, doubled(): lax.ppermute(rows, 'mix', xor_route(lax.axis_size('mix'), bit))  8.24 us
    ppermute x3, waiting for transfers between devices, sum_over_mesh(): lax.ppermute(half, 'row', xor_route(blocks, k))  5.9 us
    ppermute x3, starting transfers between devices, sum_over_mesh(): lax.ppermute(half, 'row', xor_route(blocks, k))  4.45 us
    ppermute x3, waiting for transfers between devices, sum_over_mesh(): lax.ppermute(half, 'mix', xor_route(planes, k))  4.42 us
    pallas_call x2, Pallas kernels, relay(): pl.pallas_call(kernel, out_shape=[jax.ShapeDtypeStruct(shape, dtype) for...  3.62 us
    ppermute x3, starting transfers between devices, sampled_mixing(): lax.ppermute(part, 'mix', xor_route(planes, k))  3.55 us
  transfers between devices with their start and end apart: 19, of which 9 were waited for; matrix products, arithmetic and copies ran while one was open for 0% of the time, Pallas kernels for 4%

profile of v6, /device:TPU:0, one launch (start us, length us, event | category | flops | bytes accessed | tf_op | source)
XLA Modules:
  0.0 64.8 jit_solution(11843929883505798805)
XLA Ops:
  0.7 1.7 %field_kernel.1 = (bf16[192,1024]{1,0:T(8,128)(2,1)S(1)}, bf16[128,1024]{1,0:T(8,128)(2,1)S(1)}, bf16[128,128]{1,0:T(8,128)(2,1)S(1)}, bf16[128,128]{1,0:T(8,128)(2,1)S(1)}) custom-call(s32[2]{0:T(128)S(1)} %pad_add_fusion.1.flags_ref, bf16[64,3,8,128]{3,2,1,0:T(8,128)(2,1)} %bitcast.17), custom_call_target="tpu_custom_call" | custom-call | tf_op jit(solution)/shard_map/field_kernel/pallas_call | solution.py:116
  3.0 0.7 %collective-permute-start.4 = (bf16[128,1024]{1,0:T(8,128)(2,1)S(1)}, bf16[128,1024]{1,0:T(8,128)(2,1)S(1)}, u32[]{:S(2)}, u32[]{:S(2)}) collective-permute-start(bf16[128,1024]{1,0:T(8,128)(2,1)S(1)} %get-tuple-element.22), channel_id=1, source_target_pairs={{1,2},{3,4},{5,6},{2,1},{4,3},{6,5},{9,10},{11,12},{13,14},{10,9},... | collective-permute-start | bytes 786440 | tf_op jit(solution)/shard_map/ppermute | solution.py:422
  3.7 5.4 %collective-permute-start = (s32[1,256]{1,0:T(1,128)S(1)}, s32[1,256]{1,0:T(1,128)S(1)}, u32[]{:S(2)}, u32[]{:S(2)}) collective-permute-start(s32[1,256]{1,0:T(1,128)S(1)} %bitcast.19), channel_id=1, source_target_pairs={{0,4},{1,5},{2,6},{3,7},{4,0},{5,1},{6,2},{7,3},{8,12},{9,13},{10,... | collective-permute-start | bytes 3080 | tf_op jit(solution)/shard_map/ppermute | solution.py:327
  9.0 1.6 %collective-permute-start.5 = (bf16[128,128]{1,0:T(8,128)(2,1)S(1)}, bf16[128,128]{1,0:T(8,128)(2,1)S(1)}, u32[]{:S(2)}, u32[]{:S(2)}) collective-permute-start(bf16[128,128]{1,0:T(8,128)(2,1)S(1)} %get-tuple-element.23), channel_id=1, source_target_pairs={{0,8},{16,24},{8,0},{24,16},{1,9},{17,25},{9,1},{25,17},{2,10},{18... | collective-permute-start | bytes 98312 | tf_op jit(solution)/shard_map/ppermute | solution.py:423
  11.3 1.9 %velocity_kernel.1 = (bf16[192,1024]{1,0:T(8,128)(2,1)S(1)}, bf16[384,256]{1,0:T(8,128)(2,1)S(1)}) custom-call(s32[2]{0:T(128)S(1)} %pad_add_fusion.1.flags_ref, bf16[64,3,8,128]{3,2,1,0:T(8,128)(2,1)} %bitcast.18, s32[384,256]{1,0:T(8,128)} %test_ref.1, s32[8,128]{1,0:T(8,128)} %bitcast.14), custom_call_target="tpu_custom_call" | custom-call | tf_op jit(solution)/shard_map/velocity_kernel/pallas_call | solution.py:116
  13.9 0.9 %curl_kernel.1.current_ref = bf16[192,1024]{1,0:T(8,128)(2,1)S(1)} custom-call(s32[2]{0:T(128)S(1)} %pad_add_fusion.1.flags_ref, bf16[192,1024]{1,0:T(8,128)(2,1)S(1)} %get-tuple-element.21.field_ref, bf16[128,1024]{1,0:T(8,128)(2,1)S(1)} %collective-permute-done.3.plane_a_ref, bf16[128,1024]{1,0:T(8,128)(2,1)S(1)} %collective-permute-done.4.plane_b_ref, ...), custom_call_target="tpu_custom_call" | custom-call | tf_op jit(solution)/shard_map/curl_kernel/pallas_call | solution.py:29
  14.8 2.9 %collective-permute-start.1 = (s32[2,256]{1,0:T(2,128)S(1)}, s32[2,256]{1,0:T(2,128)S(1)}, u32[]{:S(2)}, u32[]{:S(2)}) collective-permute-start(s32[2,256]{1,0:T(2,128)S(1)} %pad_add_fusion), channel_id=1, source_target_pairs={{0,2},{1,3},{2,0},{3,1},{4,6},{5,7},{6,4},{7,5},{8,10},{9,11},{10,... | collective-permute-start | bytes 6152 | tf_op jit(solution)/shard_map/ppermute | solution.py:327
  17.7 1.6 %collective-permute-done.1 = s32[2,256]{1,0:T(2,128)S(1)} collective-permute-done((s32[2,256]{1,0:T(2,128)S(1)}, s32[2,256]{1,0:T(2,128)S(1)}, u32[]{:S(2)}, u32[]{:S(2)}) %collective-permute-start.1) | collective-permute-done | bytes 2080 | tf_op jit(solution)/shard_map/ppermute | solution.py:327
  19.3 1.9 %parts_kernel.1 = (f32[512,128]{1,0:T(8,128)S(1)}, f32[512,128]{1,0:T(8,128)S(1)}, f32[512,128]{1,0:T(8,128)S(1)}, f32[512,128]{1,0:T(8,128)S(1)}) custom-call(s32[2]{0:T(128)S(1)} %pad_add_fusion.1.flags_ref, s32[1024]{0:T(1024)S(1)} %bitcast.16, bf16[192,1024]{1,0:T(8,128)(2,1)S(1)} %get-tuple-element.20.pair_ref, ...), custom_call_target="tpu_custom_call" | custom-call | tf_op jit(solution)/shard_map/parts_kernel/pallas_call | solution.py:29
  21.3 1.8 %collective-permute-start.10 = (f32[512,128]{1,0:T(8,128)S(1)}, f32[512,128]{1,0:T(8,128)S(1)}, u32[]{:S(2)}, u32[]{:S(2)}) collective-permute-start(f32[512,128]{1,0:T(8,128)S(1)} %get-tuple-element.29), channel_id=1, source_target_pairs={{0,6},{1,7},{2,4},{3,5},{4,2},{5,3},{6,0},{7,1},{8,14},{9,15},{10,... | collective-permute-start | bytes 786440 | tf_op jit(solution)/shard_map/ppermute | solution.py:343
  23.1 1.8 %collective-permute-start.8 = (f32[512,128]{1,0:T(8,128)S(1)}, f32[512,128]{1,0:T(8,128)S(1)}, u32[]{:S(2)}, u32[]{:S(2)}) collective-permute-start(f32[512,128]{1,0:T(8,128)S(1)} %get-tuple-element.27), channel_id=1, source_target_pairs={{0,4},{1,5},{2,6},{3,7},{4,0},{5,1},{6,2},{7,3},{8,12},{9,13},{10,... | collective-permute-start | bytes 786440 | tf_op jit(solution)/shard_map/ppermute | solution.py:343
  24.9 6.6 %collective-permute-done.10.refs_3_ = f32[512,128]{1,0:T(8,128)S(1)} collective-permute-done((f32[512,128]{1,0:T(8,128)S(1)}, f32[512,128]{1,0:T(8,128)S(1)}, u32[]{:S(2)}, u32[]{:S(2)}) %collective-permute-start.10) | collective-permute-done | bytes 262176 | tf_op jit(solution)/shard_map/ppermute | solution.py:343
  31.5 3.8 %collective-permute-done.8.refs_1_ = f32[512,128]{1,0:T(8,128)S(1)} collective-permute-done((f32[512,128]{1,0:T(8,128)S(1)}, f32[512,128]{1,0:T(8,128)S(1)}, u32[]{:S(2)}, u32[]{:S(2)}) %collective-permute-start.8) | collective-permute-done | bytes 262176 | tf_op jit(solution)/shard_map/ppermute | solution.py:343
  35.3 1.0 %gram_kernel.1 = (f32[256,256]{1,0:T(8,128)S(1)}, f32[160,256]{1,0:T(8,128)S(1)}) custom-call(f32[5]{0:T(128)S(1)} %stack.26.signs_ref, f32[512,128]{1,0:T(8,128)S(1)} %get-tuple-element.26.refs_0_, f32[512,128]{1,0:T(8,128)S(1)} %collective-permute-done.8.refs_1_, f32[512,128]{1,0:T(8,128)S(1)} %collective-permute-done.9.refs_2_, ...), custom_call_target="tpu_custom_call" | custom-call | tf_op jit(solution)/shard_map/gram_kernel/pallas_call | solution.py:29
  36.4 1.3 %collective-permute-done.11 = f32[80,256]{1,0:T(8,128)S(1)} collective-permute-done((f32[80,256]{1,0:T(8,128)S(1)}, f32[80,256]{1,0:T(8,128)S(1)}, u32[]{:S(2)}, u32[]{:S(2)}) %collective-permute-start.11) | collective-permute-done | bytes 81952 | tf_op jit(solution)/shard_map/ppermute | solution.py:368
  37.7 1.8 %collective-permute-start.12 = (f32[80,256]{1,0:T(8,128)S(1)}, f32[80,256]{1,0:T(8,128)S(1)}, u32[]{:S(2)}, u32[]{:S(2)}) collective-permute-start(f32[80,256]{1,0:T(8,128)S(1)} %select_add_fusion), channel_id=1, source_target_pairs={{0,2},{1,3},{2,0},{3,1},{4,6},{5,7},{6,4},{7,5},{8,10},{9,11},{10,... | collective-permute-start | bytes 245768 | tf_op jit(solution)/shard_map/ppermute | solution.py:369
  40.1 1.1 %collective-permute-start.14 = (f32[80,256]{1,0:T(8,128)S(1)}, f32[80,256]{1,0:T(8,128)S(1)}, u32[]{:S(2)}, u32[]{:S(2)}) collective-permute-start(f32[80,256]{1,0:T(8,128)S(1)} %select_add_fusion), channel_id=1, source_target_pairs={{0,6},{1,7},{2,4},{3,5},{4,2},{5,3},{6,0},{7,1},{8,14},{9,15},{10,... | collective-permute-start | bytes 245768 | tf_op jit(solution)/shard_map/ppermute | solution.py:369
  41.2 1.0 %collective-permute-done.12 = f32[80,256]{1,0:T(8,128)S(1)} collective-permute-done((f32[80,256]{1,0:T(8,128)S(1)}, f32[80,256]{1,0:T(8,128)S(1)}, u32[]{:S(2)}, u32[]{:S(2)}) %collective-permute-start.12) | collective-permute-done | bytes 81952 | tf_op jit(solution)/shard_map/ppermute | solution.py:369
  42.3 3.4 %collective-permute-done.13 = f32[80,256]{1,0:T(8,128)S(1)} collective-permute-done((f32[80,256]{1,0:T(8,128)S(1)}, f32[80,256]{1,0:T(8,128)S(1)}, u32[]{:S(2)}, u32[]{:S(2)}) %collective-permute-start.13) | collective-permute-done | bytes 81952 | tf_op jit(solution)/shard_map/ppermute | solution.py:369
  45.7 3.7 %collective-permute-start.15 = (f32[80,256]{1,0:T(8,128)S(1)}, f32[80,256]{1,0:T(8,128)S(1)}, u32[]{:S(2)}, u32[]{:S(2)}) collective-permute-start(f32[80,256]{1,0:T(8,128)S(1)} %add_add_fusion.1), channel_id=1, source_target_pairs={{0,24},{8,16},{16,8},{24,0},{1,25},{9,17},{17,9},{25,1},{2,26},{10... | collective-permute-start | bytes 245768 | tf_op jit(solution)/shard_map/ppermute | solution.py:370
  50.1 2.5 %collective-permute-done.15 = f32[80,256]{1,0:T(8,128)S(1)} collective-permute-done((f32[80,256]{1,0:T(8,128)S(1)}, f32[80,256]{1,0:T(8,128)S(1)}, u32[]{:S(2)}, u32[]{:S(2)}) %collective-permute-start.15) | collective-permute-done | bytes 81952 | tf_op jit(solution)/shard_map/ppermute | solution.py:370
  52.6 3.4 %collective-permute-done.16 = f32[80,256]{1,0:T(8,128)S(1)} collective-permute-done((f32[80,256]{1,0:T(8,128)S(1)}, f32[80,256]{1,0:T(8,128)S(1)}, u32[]{:S(2)}, u32[]{:S(2)}) %collective-permute-start.16) | collective-permute-done | bytes 81952 | tf_op jit(solution)/shard_map/ppermute | solution.py:370
  56.1 1.3 %collective-permute-done.18.other_ref = f32[80,256]{1,0:T(8,128)S(1)} collective-permute-done((f32[80,256]{1,0:T(8,128)S(1)}, f32[80,256]{1,0:T(8,128)S(1)}, u32[]{:S(2)}, u32[]{:S(2)}) %collective-permute-start.18) | collective-permute-done | bytes 81952 | tf_op jit(solution)/shard_map/ppermute | solution.py:371
  57.4 7.4 %finish_kernel.1 = (f32[256,256]{1,0:T(8,128)}, f32[256,256]{1,0:T(8,128)}) custom-call(s32[1]{0:T(128)} %bitcast.core_ref, f32[80,256]{1,0:T(8,128)S(1)} %add_add_fusion.half_ref, f32[80,256]{1,0:T(8,128)S(1)} %collective-permute-done.18.other_ref, f32[256,256]{1,0:T(8,128)S(1)} %get-tuple-element.31.picked_ref), custom_call_target="tpu_custom_call" | custom-call | tf_op jit(solution)/shard_map/finish_kernel/pallas_call | solution.py:29
  (33 shorter events, 3.7 us)
Async XLA Ops:
  2.4 1.2 %copy-start.1 = (s32[1,1,256]{2,1,0:T(1,128)S(1)}, s32[1,1,256]{2,1,0:T(1,128)}, u32[]{:S(2)}) copy-start(s32[1,1,256]{2,1,0:T(1,128)} %param.9) | copy-start | bytes 3076
  2.5 10.9 %collective-permute-start.3 = (bf16[128,1024]{1,0:T(8,128)(2,1)S(1)}, bf16[128,1024]{1,0:T(8,128)(2,1)S(1)}, u32[]{:S(2)}, u32[]{:S(2)}) collective-permute-start(bf16[128,1024]{1,0:T(8,128)(2,1)S(1)} %get-tuple-element.22), channel_id=1, source_target_pairs={{0,1},{2,3},{4,5},{6,7},{1,0},{3,2},{5,4},{7,6},{8,9},{10,11},{12,... | collective-permute-start | bytes 786440 | tf_op jit(solution)/shard_map/ppermute | solution.py:430
  3.0 10.3 %collective-permute-start.4 = (bf16[128,1024]{1,0:T(8,128)(2,1)S(1)}, bf16[128,1024]{1,0:T(8,128)(2,1)S(1)}, u32[]{:S(2)}, u32[]{:S(2)}) collective-permute-start(bf16[128,1024]{1,0:T(8,128)(2,1)S(1)} %get-tuple-element.22), channel_id=1, source_target_pairs={{1,2},{3,4},{5,6},{2,1},{4,3},{6,5},{9,10},{11,12},{13,14},{10,9},... | collective-permute-start | bytes 786440 | tf_op jit(solution)/shard_map/ppermute | solution.py:422
  3.7 9.5 %collective-permute-start = (s32[1,256]{1,0:T(1,128)S(1)}, s32[1,256]{1,0:T(1,128)S(1)}, u32[]{:S(2)}, u32[]{:S(2)}) collective-permute-start(s32[1,256]{1,0:T(1,128)S(1)} %bitcast.19), channel_id=1, source_target_pairs={{0,4},{1,5},{2,6},{3,7},{4,0},{5,1},{6,2},{7,3},{8,12},{9,13},{10,... | collective-permute-start | bytes 3080 | tf_op jit(solution)/shard_map/ppermute | solution.py:327
  9.0 4.3 %collective-permute-start.5 = (bf16[128,128]{1,0:T(8,128)(2,1)S(1)}, bf16[128,128]{1,0:T(8,128)(2,1)S(1)}, u32[]{:S(2)}, u32[]{:S(2)}) collective-permute-start(bf16[128,128]{1,0:T(8,128)(2,1)S(1)} %get-tuple-element.23), channel_id=1, source_target_pairs={{0,8},{16,24},{8,0},{24,16},{1,9},{17,25},{9,1},{25,17},{2,10},{18... | collective-permute-start | bytes 98312 | tf_op jit(solution)/shard_map/ppermute | solution.py:423
  10.6 2.7 %collective-permute-start.6 = (bf16[128,128]{1,0:T(8,128)(2,1)S(1)}, bf16[128,128]{1,0:T(8,128)(2,1)S(1)}, u32[]{:S(2)}, u32[]{:S(2)}) collective-permute-start(bf16[128,128]{1,0:T(8,128)(2,1)S(1)} %get-tuple-element.24), channel_id=1, source_target_pairs={{8,16},{16,8},{9,17},{17,9},{10,18},{18,10},{11,19},{19,11},{12,20... | collective-permute-start | bytes 98312 | tf_op jit(solution)/shard_map/ppermute | solution.py:424
  13.2 0.7 %copy-start = (s32[1,8,128]{2,1,0:T(8,128)S(1)}, s32[1,8,128]{2,1,0:T(8,128)}, u32[]{:S(2)}) copy-start(s32[1,8,128]{2,1,0:T(8,128)} %param.8) | copy-start | bytes 12292
  13.2 6.1 %collective-permute-start.2 = (bf16[192,1024]{1,0:T(8,128)(2,1)S(1)}, bf16[192,1024]{1,0:T(8,128)(2,1)S(1)}, u32[]{:S(2)}, u32[]{:S(2)}) collective-permute-start(bf16[192,1024]{1,0:T(8,128)(2,1)S(1)} %get-tuple-element.20.pair_ref), channel_id=1, source_target_pairs={{0,1},{2,3},{4,5},{6,7},{1,0},{3,2},{5,4},{7,6},{8,9},{10,11},{12,... | collective-permute-start | bytes 1179656 | tf_op jit(solution)/shard_map/ppermute | solution.py:432
  14.8 4.6 %collective-permute-start.7 = (bf16[192,1024]{1,0:T(8,128)(2,1)S(1)}, bf16[192,1024]{1,0:T(8,128)(2,1)S(1)}, u32[]{:S(2)}, u32[]{:S(2)}) collective-permute-start(bf16[192,1024]{1,0:T(8,128)(2,1)S(1)} %curl_kernel.1.current_ref), channel_id=1, source_target_pairs={{0,1},{1,0},{2,3},{3,2},{4,5},{5,4},{6,7},{7,6},{8,9},{9,8},{10,11... | collective-permute-start | bytes 1179656 | tf_op jit(solution)/shard_map/ppermute | solution.py:336
  14.8 4.4 %collective-permute-start.1 = (s32[2,256]{1,0:T(2,128)S(1)}, s32[2,256]{1,0:T(2,128)S(1)}, u32[]{:S(2)}, u32[]{:S(2)}) collective-permute-start(s32[2,256]{1,0:T(2,128)S(1)} %pad_add_fusion), channel_id=1, source_target_pairs={{0,2},{1,3},{2,0},{3,1},{4,6},{5,7},{6,4},{7,5},{8,10},{9,11},{10,... | collective-permute-start | bytes 6152 | tf_op jit(solution)/shard_map/ppermute | solution.py:327
  21.3 10.3 %collective-permute-start.10 = (f32[512,128]{1,0:T(8,128)S(1)}, f32[512,128]{1,0:T(8,128)S(1)}, u32[]{:S(2)}, u32[]{:S(2)}) collective-permute-start(f32[512,128]{1,0:T(8,128)S(1)} %get-tuple-element.29), channel_id=1, source_target_pairs={{0,6},{1,7},{2,4},{3,5},{4,2},{5,3},{6,0},{7,1},{8,14},{9,15},{10,... | collective-permute-start | bytes 786440 | tf_op jit(solution)/shard_map/ppermute | solution.py:343
  23.1 12.2 %collective-permute-start.8 = (f32[512,128]{1,0:T(8,128)S(1)}, f32[512,128]{1,0:T(8,128)S(1)}, u32[]{:S(2)}, u32[]{:S(2)}) collective-permute-start(f32[512,128]{1,0:T(8,128)S(1)} %get-tuple-element.27), channel_id=1, source_target_pairs={{0,4},{1,5},{2,6},{3,7},{4,0},{5,1},{6,2},{7,3},{8,12},{9,13},{10,... | collective-permute-start | bytes 786440 | tf_op jit(solution)/shard_map/ppermute | solution.py:343
  24.8 10.5 %collective-permute-start.9 = (f32[512,128]{1,0:T(8,128)S(1)}, f32[512,128]{1,0:T(8,128)S(1)}, u32[]{:S(2)}, u32[]{:S(2)}) collective-permute-start(f32[512,128]{1,0:T(8,128)S(1)} %get-tuple-element.28), channel_id=1, source_target_pairs={{0,2},{1,3},{2,0},{3,1},{4,6},{5,7},{6,4},{7,5},{8,10},{9,11},{10,... | collective-permute-start | bytes 786440 | tf_op jit(solution)/shard_map/ppermute | solution.py:343
  36.3 1.3 %collective-permute-start.11 = (f32[80,256]{1,0:T(8,128)S(1)}, f32[80,256]{1,0:T(8,128)S(1)}, u32[]{:S(2)}, u32[]{:S(2)}) collective-permute-start(f32[80,256]{1,0:T(8,128)S(1)} %slice_select_fusion), channel_id=1, source_target_pairs={{0,1},{1,0},{2,3},{3,2},{4,5},{5,4},{6,7},{7,6},{8,9},{9,8},{10,11... | collective-permute-start | bytes 245768 | tf_op jit(solution)/shard_map/ppermute | solution.py:368
  37.7 4.6 %collective-permute-start.12 = (f32[80,256]{1,0:T(8,128)S(1)}, f32[80,256]{1,0:T(8,128)S(1)}, u32[]{:S(2)}, u32[]{:S(2)}) collective-permute-start(f32[80,256]{1,0:T(8,128)S(1)} %select_add_fusion), channel_id=1, source_target_pairs={{0,2},{1,3},{2,0},{3,1},{4,6},{5,7},{6,4},{7,5},{8,10},{9,11},{10,... | collective-permute-start | bytes 245768 | tf_op jit(solution)/shard_map/ppermute | solution.py:369
  39.5 6.2 %collective-permute-start.13 = (f32[80,256]{1,0:T(8,128)S(1)}, f32[80,256]{1,0:T(8,128)S(1)}, u32[]{:S(2)}, u32[]{:S(2)}) collective-permute-start(f32[80,256]{1,0:T(8,128)S(1)} %select_add_fusion), channel_id=1, source_target_pairs={{0,4},{1,5},{2,6},{3,7},{4,0},{5,1},{6,2},{7,3},{8,12},{9,13},{10,... | collective-permute-start | bytes 245768 | tf_op jit(solution)/shard_map/ppermute | solution.py:369
  40.1 5.6 %collective-permute-start.14 = (f32[80,256]{1,0:T(8,128)S(1)}, f32[80,256]{1,0:T(8,128)S(1)}, u32[]{:S(2)}, u32[]{:S(2)}) collective-permute-start(f32[80,256]{1,0:T(8,128)S(1)} %select_add_fusion), channel_id=1, source_target_pairs={{0,6},{1,7},{2,4},{3,5},{4,2},{5,3},{6,0},{7,1},{8,14},{9,15},{10,... | collective-permute-start | bytes 245768 | tf_op jit(solution)/shard_map/ppermute | solution.py:369
  45.7 6.9 %collective-permute-start.15 = (f32[80,256]{1,0:T(8,128)S(1)}, f32[80,256]{1,0:T(8,128)S(1)}, u32[]{:S(2)}, u32[]{:S(2)}) collective-permute-start(f32[80,256]{1,0:T(8,128)S(1)} %add_add_fusion.1), channel_id=1, source_target_pairs={{0,24},{8,16},{16,8},{24,0},{1,25},{9,17},{17,9},{25,1},{2,26},{10... | collective-permute-start | bytes 245768 | tf_op jit(solution)/shard_map/ppermute | solution.py:370
  49.4 6.6 %collective-permute-start.16 = (f32[80,256]{1,0:T(8,128)S(1)}, f32[80,256]{1,0:T(8,128)S(1)}, u32[]{:S(2)}, u32[]{:S(2)}) collective-permute-start(f32[80,256]{1,0:T(8,128)S(1)} %add_add_fusion.1), channel_id=1, source_target_pairs={{0,16},{8,24},{16,0},{24,8},{1,17},{9,25},{17,1},{25,9},{2,18},{10... | collective-permute-start | bytes 245768 | tf_op jit(solution)/shard_map/ppermute | solution.py:370
  49.8 6.3 %collective-permute-start.17 = (f32[80,256]{1,0:T(8,128)S(1)}, f32[80,256]{1,0:T(8,128)S(1)}, u32[]{:S(2)}, u32[]{:S(2)}) collective-permute-start(f32[80,256]{1,0:T(8,128)S(1)} %add_add_fusion.1), channel_id=1, source_target_pairs={{0,8},{8,0},{16,24},{24,16},{1,9},{9,1},{17,25},{25,17},{2,10},{10... | collective-permute-start | bytes 245768 | tf_op jit(solution)/shard_map/ppermute | solution.py:370
  56.1 1.3 %collective-permute-start.18 = (f32[80,256]{1,0:T(8,128)S(1)}, f32[80,256]{1,0:T(8,128)S(1)}, u32[]{:S(2)}, u32[]{:S(2)}) collective-permute-start(f32[80,256]{1,0:T(8,128)S(1)} %add_add_fusion.half_ref), channel_id=1, source_target_pairs={{0,1},{1,0},{2,3},{3,2},{4,5},{5,4},{6,7},{7,6},{8,9},{9,8},{10,11... | collective-permute-start | bytes 245768 | tf_op jit(solution)/shard_map/ppermute | solution.py:371

commit v7 on v6

--- a/solution.py
+++ b/solution.py
@@ -10,7 +10,7 @@
 MESH_AXES = ("row", "mix")
 ROWS = 8
 LANES = 128
-NEAR = 4
+NEAR = 5
 NN, NT, TN = ((1,), (0,)), ((1,), (1,)), ((0,), (0,))
 SMEM = pl.BlockSpec(memory_space=pltpu.SMEM)
 VMEM = pl.BlockSpec(memory_space=pltpu.VMEM)

time: 65.1 us -> 65.2 us (level)
  no operation moved by 1% of the time
where the time goes in v7:
time: 65.2 us; the launch traced here: 65 us
  waiting for transfers between devices  24.8 us (38%)
  starting transfers between devices  23.5 us (36%)
  Pallas kernels  15 us (23%)
  between operations  0.85 us (1%)
    pallas_call x4, Pallas kernels, local(): pl.pallas_call(kernel, out_shape=[jax.ShapeDtypeStruct(shape, dtype) for...  11.4 us
    ppermute x3, waiting for transfers between devices, sampled_mixing(): lax.ppermute(part, 'mix', xor_route(planes, k))  10.4 us
    ppermute x2, starting transfers between devices, doubled(): lax.ppermute(rows, 'mix', xor_route(lax.axis_size('mix'), bit))  8.24 us
    ppermute x3, waiting for transfers between devices, sum_over_mesh(): lax.ppermute(half, 'row', xor_route(blocks, k))  5.88 us
    ppermute x3, starting transfers between devices, sum_over_mesh(): lax.ppermute(half, 'row', xor_route(blocks, k))  4.45 us
    ppermute x3, waiting for transfers between devices, sum_over_mesh(): lax.ppermute(half, 'mix', xor_route(planes, k))  4.43 us
    pallas_call x2, Pallas kernels, relay(): pl.pallas_call(kernel, out_shape=[jax.ShapeDtypeStruct(shape, dtype) for...  3.62 us
    ppermute x3, starting transfers between devices, sampled_mixing(): lax.ppermute(part, 'mix', xor_route(planes, k))  3.56 us
  transfers between devices with their start and end apart: 19, of which 9 were waited for; matrix products, arithmetic and copies ran while one was open for 0% of the time, Pallas kernels for 4%

profile of v7, /device:TPU:0, one launch (start us, length us, event | category | flops | bytes accessed | tf_op | source)
XLA Modules:
  0.0 65.0 jit_solution(552253518666429643)
XLA Ops:
  0.7 1.7 %field_kernel.1 = (bf16[192,1024]{1,0:T(8,128)(2,1)S(1)}, bf16[128,1024]{1,0:T(8,128)(2,1)S(1)}, bf16[128,128]{1,0:T(8,128)(2,1)S(1)}, bf16[128,128]{1,0:T(8,128)(2,1)S(1)}) custom-call(s32[2]{0:T(128)S(1)} %pad_add_fusion.1.flags_ref, bf16[64,3,8,128]{3,2,1,0:T(8,128)(2,1)} %bitcast.17), custom_call_target="tpu_custom_call" | custom-call | tf_op jit(solution)/shard_map/field_kernel/pallas_call | solution.py:116
  3.0 0.7 %collective-permute-start.4 = (bf16[128,1024]{1,0:T(8,128)(2,1)S(1)}, bf16[128,1024]{1,0:T(8,128)(2,1)S(1)}, u32[]{:S(2)}, u32[]{:S(2)}) collective-permute-start(bf16[128,1024]{1,0:T(8,128)(2,1)S(1)} %get-tuple-element.22), channel_id=1, source_target_pairs={{1,2},{3,4},{5,6},{2,1},{4,3},{6,5},{9,10},{11,12},{13,14},{10,9},... | collective-permute-start | bytes 786440 | tf_op jit(solution)/shard_map/ppermute | solution.py:422
  3.7 5.4 %collective-permute-start = (s32[1,256]{1,0:T(1,128)S(1)}, s32[1,256]{1,0:T(1,128)S(1)}, u32[]{:S(2)}, u32[]{:S(2)}) collective-permute-start(s32[1,256]{1,0:T(1,128)S(1)} %bitcast.19), channel_id=1, source_target_pairs={{0,4},{1,5},{2,6},{3,7},{4,0},{5,1},{6,2},{7,3},{8,12},{9,13},{10,... | collective-permute-start | bytes 3080 | tf_op jit(solution)/shard_map/ppermute | solution.py:327
  9.0 1.6 %collective-permute-start.5 = (bf16[128,128]{1,0:T(8,128)(2,1)S(1)}, bf16[128,128]{1,0:T(8,128)(2,1)S(1)}, u32[]{:S(2)}, u32[]{:S(2)}) collective-permute-start(bf16[128,128]{1,0:T(8,128)(2,1)S(1)} %get-tuple-element.23), channel_id=1, source_target_pairs={{0,8},{16,24},{8,0},{24,16},{1,9},{17,25},{9,1},{25,17},{2,10},{18... | collective-permute-start | bytes 98312 | tf_op jit(solution)/shard_map/ppermute | solution.py:423
  11.3 1.9 %velocity_kernel.1 = (bf16[192,1024]{1,0:T(8,128)(2,1)S(1)}, bf16[384,256]{1,0:T(8,128)(2,1)S(1)}) custom-call(s32[2]{0:T(128)S(1)} %pad_add_fusion.1.flags_ref, bf16[64,3,8,128]{3,2,1,0:T(8,128)(2,1)} %bitcast.18, s32[384,256]{1,0:T(8,128)} %test_ref.1, s32[8,128]{1,0:T(8,128)} %bitcast.14), custom_call_target="tpu_custom_call" | custom-call | tf_op jit(solution)/shard_map/velocity_kernel/pallas_call | solution.py:116
  13.9 0.9 %curl_kernel.1.current_ref = bf16[192,1024]{1,0:T(8,128)(2,1)S(1)} custom-call(s32[2]{0:T(128)S(1)} %pad_add_fusion.1.flags_ref, bf16[192,1024]{1,0:T(8,128)(2,1)S(1)} %get-tuple-element.21.field_ref, bf16[128,1024]{1,0:T(8,128)(2,1)S(1)} %collective-permute-done.3.plane_a_ref, bf16[128,1024]{1,0:T(8,128)(2,1)S(1)} %collective-permute-done.4.plane_b_ref, ...), custom_call_target="tpu_custom_call" | custom-call | tf_op jit(solution)/shard_map/curl_kernel/pallas_call | solution.py:29
  14.8 2.9 %collective-permute-start.1 = (s32[2,256]{1,0:T(2,128)S(1)}, s32[2,256]{1,0:T(2,128)S(1)}, u32[]{:S(2)}, u32[]{:S(2)}) collective-permute-start(s32[2,256]{1,0:T(2,128)S(1)} %pad_add_fusion), channel_id=1, source_target_pairs={{0,2},{1,3},{2,0},{3,1},{4,6},{5,7},{6,4},{7,5},{8,10},{9,11},{10,... | collective-permute-start | bytes 6152 | tf_op jit(solution)/shard_map/ppermute | solution.py:327
  17.7 1.6 %collective-permute-done.1 = s32[2,256]{1,0:T(2,128)S(1)} collective-permute-done((s32[2,256]{1,0:T(2,128)S(1)}, s32[2,256]{1,0:T(2,128)S(1)}, u32[]{:S(2)}, u32[]{:S(2)}) %collective-permute-start.1) | collective-permute-done | bytes 2080 | tf_op jit(solution)/shard_map/ppermute | solution.py:327
  19.3 1.9 %parts_kernel.1 = (f32[512,128]{1,0:T(8,128)S(1)}, f32[512,128]{1,0:T(8,128)S(1)}, f32[512,128]{1,0:T(8,128)S(1)}, f32[512,128]{1,0:T(8,128)S(1)}) custom-call(s32[2]{0:T(128)S(1)} %pad_add_fusion.1.flags_ref, s32[1024]{0:T(1024)S(1)} %bitcast.16, bf16[192,1024]{1,0:T(8,128)(2,1)S(1)} %get-tuple-element.20.pair_ref, ...), custom_call_target="tpu_custom_call" | custom-call | tf_op jit(solution)/shard_map/parts_kernel/pallas_call | solution.py:29
  21.3 1.8 %collective-permute-start.10 = (f32[512,128]{1,0:T(8,128)S(1)}, f32[512,128]{1,0:T(8,128)S(1)}, u32[]{:S(2)}, u32[]{:S(2)}) collective-permute-start(f32[512,128]{1,0:T(8,128)S(1)} %get-tuple-element.29), channel_id=1, source_target_pairs={{0,6},{1,7},{2,4},{3,5},{4,2},{5,3},{6,0},{7,1},{8,14},{9,15},{10,... | collective-permute-start | bytes 786440 | tf_op jit(solution)/shard_map/ppermute | solution.py:343
  23.1 1.8 %collective-permute-start.8 = (f32[512,128]{1,0:T(8,128)S(1)}, f32[512,128]{1,0:T(8,128)S(1)}, u32[]{:S(2)}, u32[]{:S(2)}) collective-permute-start(f32[512,128]{1,0:T(8,128)S(1)} %get-tuple-element.27), channel_id=1, source_target_pairs={{0,4},{1,5},{2,6},{3,7},{4,0},{5,1},{6,2},{7,3},{8,12},{9,13},{10,... | collective-permute-start | bytes 786440 | tf_op jit(solution)/shard_map/ppermute | solution.py:343
  24.9 6.6 %collective-permute-done.10.refs_3_ = f32[512,128]{1,0:T(8,128)S(1)} collective-permute-done((f32[512,128]{1,0:T(8,128)S(1)}, f32[512,128]{1,0:T(8,128)S(1)}, u32[]{:S(2)}, u32[]{:S(2)}) %collective-permute-start.10) | collective-permute-done | bytes 262176 | tf_op jit(solution)/shard_map/ppermute | solution.py:343
  31.5 3.8 %collective-permute-done.8.refs_1_ = f32[512,128]{1,0:T(8,128)S(1)} collective-permute-done((f32[512,128]{1,0:T(8,128)S(1)}, f32[512,128]{1,0:T(8,128)S(1)}, u32[]{:S(2)}, u32[]{:S(2)}) %collective-permute-start.8) | collective-permute-done | bytes 262176 | tf_op jit(solution)/shard_map/ppermute | solution.py:343
  35.3 1.0 %gram_kernel.1 = (f32[256,256]{1,0:T(8,128)S(1)}, f32[160,256]{1,0:T(8,128)S(1)}) custom-call(f32[5]{0:T(128)S(1)} %stack.26.signs_ref, f32[512,128]{1,0:T(8,128)S(1)} %get-tuple-element.26.refs_0_, f32[512,128]{1,0:T(8,128)S(1)} %collective-permute-done.8.refs_1_, f32[512,128]{1,0:T(8,128)S(1)} %collective-permute-done.9.refs_2_, ...), custom_call_target="tpu_custom_call" | custom-call | tf_op jit(solution)/shard_map/gram_kernel/pallas_call | solution.py:29
  36.4 1.3 %collective-permute-done.11 = f32[80,256]{1,0:T(8,128)S(1)} collective-permute-done((f32[80,256]{1,0:T(8,128)S(1)}, f32[80,256]{1,0:T(8,128)S(1)}, u32[]{:S(2)}, u32[]{:S(2)}) %collective-permute-start.11) | collective-permute-done | bytes 81952 | tf_op jit(solution)/shard_map/ppermute | solution.py:368
  37.7 1.8 %collective-permute-start.12 = (f32[80,256]{1,0:T(8,128)S(1)}, f32[80,256]{1,0:T(8,128)S(1)}, u32[]{:S(2)}, u32[]{:S(2)}) collective-permute-start(f32[80,256]{1,0:T(8,128)S(1)} %select_add_fusion), channel_id=1, source_target_pairs={{0,2},{1,3},{2,0},{3,1},{4,6},{5,7},{6,4},{7,5},{8,10},{9,11},{10,... | collective-permute-start | bytes 245768 | tf_op jit(solution)/shard_map/ppermute | solution.py:369
  40.1 1.1 %collective-permute-start.14 = (f32[80,256]{1,0:T(8,128)S(1)}, f32[80,256]{1,0:T(8,128)S(1)}, u32[]{:S(2)}, u32[]{:S(2)}) collective-permute-start(f32[80,256]{1,0:T(8,128)S(1)} %select_add_fusion), channel_id=1, source_target_pairs={{0,6},{1,7},{2,4},{3,5},{4,2},{5,3},{6,0},{7,1},{8,14},{9,15},{10,... | collective-permute-start | bytes 245768 | tf_op jit(solution)/shard_map/ppermute | solution.py:369
  41.2 1.0 %collective-permute-done.12 = f32[80,256]{1,0:T(8,128)S(1)} collective-permute-done((f32[80,256]{1,0:T(8,128)S(1)}, f32[80,256]{1,0:T(8,128)S(1)}, u32[]{:S(2)}, u32[]{:S(2)}) %collective-permute-start.12) | collective-permute-done | bytes 81952 | tf_op jit(solution)/shard_map/ppermute | solution.py:369
  42.3 3.4 %collective-permute-done.13 = f32[80,256]{1,0:T(8,128)S(1)} collective-permute-done((f32[80,256]{1,0:T(8,128)S(1)}, f32[80,256]{1,0:T(8,128)S(1)}, u32[]{:S(2)}, u32[]{:S(2)}) %collective-permute-start.13) | collective-permute-done | bytes 81952 | tf_op jit(solution)/shard_map/ppermute | solution.py:369
  45.7 3.7 %collective-permute-start.15 = (f32[80,256]{1,0:T(8,128)S(1)}, f32[80,256]{1,0:T(8,128)S(1)}, u32[]{:S(2)}, u32[]{:S(2)}) collective-permute-start(f32[80,256]{1,0:T(8,128)S(1)} %add_add_fusion.1), channel_id=1, source_target_pairs={{0,24},{8,16},{16,8},{24,0},{1,25},{9,17},{17,9},{25,1},{2,26},{10... | collective-permute-start | bytes 245768 | tf_op jit(solution)/shard_map/ppermute | solution.py:370
  50.2 2.5 %collective-permute-done.15 = f32[80,256]{1,0:T(8,128)S(1)} collective-permute-done((f32[80,256]{1,0:T(8,128)S(1)}, f32[80,256]{1,0:T(8,128)S(1)}, u32[]{:S(2)}, u32[]{:S(2)}) %collective-permute-start.15) | collective-permute-done | bytes 81952 | tf_op jit(solution)/shard_map/ppermute | solution.py:370
  52.6 3.4 %collective-permute-done.16 = f32[80,256]{1,0:T(8,128)S(1)} collective-permute-done((f32[80,256]{1,0:T(8,128)S(1)}, f32[80,256]{1,0:T(8,128)S(1)}, u32[]{:S(2)}, u32[]{:S(2)}) %collective-permute-start.16) | collective-permute-done | bytes 81952 | tf_op jit(solution)/shard_map/ppermute | solution.py:370
  56.1 1.3 %collective-permute-done.18.other_ref = f32[80,256]{1,0:T(8,128)S(1)} collective-permute-done((f32[80,256]{1,0:T(8,128)S(1)}, f32[80,256]{1,0:T(8,128)S(1)}, u32[]{:S(2)}, u32[]{:S(2)}) %collective-permute-start.18) | collective-permute-done | bytes 81952 | tf_op jit(solution)/shard_map/ppermute | solution.py:371
  57.4 7.6 %finish_kernel.1 = (f32[256,256]{1,0:T(8,128)}, f32[256,256]{1,0:T(8,128)}) custom-call(s32[1]{0:T(128)} %bitcast.core_ref, f32[80,256]{1,0:T(8,128)S(1)} %add_add_fusion.half_ref, f32[80,256]{1,0:T(8,128)S(1)} %collective-permute-done.18.other_ref, f32[256,256]{1,0:T(8,128)S(1)} %get-tuple-element.31.picked_ref), custom_call_target="tpu_custom_call" | custom-call | tf_op jit(solution)/shard_map/finish_kernel/pallas_call | solution.py:29
  (33 shorter events, 3.7 us)
Async XLA Ops:
  2.4 1.2 %copy-start.1 = (s32[1,1,256]{2,1,0:T(1,128)S(1)}, s32[1,1,256]{2,1,0:T(1,128)}, u32[]{:S(2)}) copy-start(s32[1,1,256]{2,1,0:T(1,128)} %param.9) | copy-start | bytes 3076
  2.5 10.9 %collective-permute-start.3 = (bf16[128,1024]{1,0:T(8,128)(2,1)S(1)}, bf16[128,1024]{1,0:T(8,128)(2,1)S(1)}, u32[]{:S(2)}, u32[]{:S(2)}) collective-permute-start(bf16[128,1024]{1,0:T(8,128)(2,1)S(1)} %get-tuple-element.22), channel_id=1, source_target_pairs={{0,1},{2,3},{4,5},{6,7},{1,0},{3,2},{5,4},{7,6},{8,9},{10,11},{12,... | collective-permute-start | bytes 786440 | tf_op jit(solution)/shard_map/ppermute | solution.py:430
  3.0 10.3 %collective-permute-start.4 = (bf16[128,1024]{1,0:T(8,128)(2,1)S(1)}, bf16[128,1024]{1,0:T(8,128)(2,1)S(1)}, u32[]{:S(2)}, u32[]{:S(2)}) collective-permute-start(bf16[128,1024]{1,0:T(8,128)(2,1)S(1)} %get-tuple-element.22), channel_id=1, source_target_pairs={{1,2},{3,4},{5,6},{2,1},{4,3},{6,5},{9,10},{11,12},{13,14},{10,9},... | collective-permute-start | bytes 786440 | tf_op jit(solution)/shard_map/ppermute | solution.py:422
  3.7 9.5 %collective-permute-start = (s32[1,256]{1,0:T(1,128)S(1)}, s32[1,256]{1,0:T(1,128)S(1)}, u32[]{:S(2)}, u32[]{:S(2)}) collective-permute-start(s32[1,256]{1,0:T(1,128)S(1)} %bitcast.19), channel_id=1, source_target_pairs={{0,4},{1,5},{2,6},{3,7},{4,0},{5,1},{6,2},{7,3},{8,12},{9,13},{10,... | collective-permute-start | bytes 3080 | tf_op jit(solution)/shard_map/ppermute | solution.py:327
  9.0 4.3 %collective-permute-start.5 = (bf16[128,128]{1,0:T(8,128)(2,1)S(1)}, bf16[128,128]{1,0:T(8,128)(2,1)S(1)}, u32[]{:S(2)}, u32[]{:S(2)}) collective-permute-start(bf16[128,128]{1,0:T(8,128)(2,1)S(1)} %get-tuple-element.23), channel_id=1, source_target_pairs={{0,8},{16,24},{8,0},{24,16},{1,9},{17,25},{9,1},{25,17},{2,10},{18... | collective-permute-start | bytes 98312 | tf_op jit(solution)/shard_map/ppermute | solution.py:423
  10.6 2.7 %collective-permute-start.6 = (bf16[128,128]{1,0:T(8,128)(2,1)S(1)}, bf16[128,128]{1,0:T(8,128)(2,1)S(1)}, u32[]{:S(2)}, u32[]{:S(2)}) collective-permute-start(bf16[128,128]{1,0:T(8,128)(2,1)S(1)} %get-tuple-element.24), channel_id=1, source_target_pairs={{8,16},{16,8},{9,17},{17,9},{10,18},{18,10},{11,19},{19,11},{12,20... | collective-permute-start | bytes 98312 | tf_op jit(solution)/shard_map/ppermute | solution.py:424
  13.2 0.7 %copy-start = (s32[1,8,128]{2,1,0:T(8,128)S(1)}, s32[1,8,128]{2,1,0:T(8,128)}, u32[]{:S(2)}) copy-start(s32[1,8,128]{2,1,0:T(8,128)} %param.8) | copy-start | bytes 12292
  13.2 6.1 %collective-permute-start.2 = (bf16[192,1024]{1,0:T(8,128)(2,1)S(1)}, bf16[192,1024]{1,0:T(8,128)(2,1)S(1)}, u32[]{:S(2)}, u32[]{:S(2)}) collective-permute-start(bf16[192,1024]{1,0:T(8,128)(2,1)S(1)} %get-tuple-element.20.pair_ref), channel_id=1, source_target_pairs={{0,1},{2,3},{4,5},{6,7},{1,0},{3,2},{5,4},{7,6},{8,9},{10,11},{12,... | collective-permute-start | bytes 1179656 | tf_op jit(solution)/shard_map/ppermute | solution.py:432
  14.8 4.6 %collective-permute-start.7 = (bf16[192,1024]{1,0:T(8,128)(2,1)S(1)}, bf16[192,1024]{1,0:T(8,128)(2,1)S(1)}, u32[]{:S(2)}, u32[]{:S(2)}) collective-permute-start(bf16[192,1024]{1,0:T(8,128)(2,1)S(1)} %curl_kernel.1.current_ref), channel_id=1, source_target_pairs={{0,1},{1,0},{2,3},{3,2},{4,5},{5,4},{6,7},{7,6},{8,9},{9,8},{10,11... | collective-permute-start | bytes 1179656 | tf_op jit(solution)/shard_map/ppermute | solution.py:336
  14.8 4.4 %collective-permute-start.1 = (s32[2,256]{1,0:T(2,128)S(1)}, s32[2,256]{1,0:T(2,128)S(1)}, u32[]{:S(2)}, u32[]{:S(2)}) collective-permute-start(s32[2,256]{1,0:T(2,128)S(1)} %pad_add_fusion), channel_id=1, source_target_pairs={{0,2},{1,3},{2,0},{3,1},{4,6},{5,7},{6,4},{7,5},{8,10},{9,11},{10,... | collective-permute-start | bytes 6152 | tf_op jit(solution)/shard_map/ppermute | solution.py:327
  21.3 10.3 %collective-permute-start.10 = (f32[512,128]{1,0:T(8,128)S(1)}, f32[512,128]{1,0:T(8,128)S(1)}, u32[]{:S(2)}, u32[]{:S(2)}) collective-permute-start(f32[512,128]{1,0:T(8,128)S(1)} %get-tuple-element.29), channel_id=1, source_target_pairs={{0,6},{1,7},{2,4},{3,5},{4,2},{5,3},{6,0},{7,1},{8,14},{9,15},{10,... | collective-permute-start | bytes 786440 | tf_op jit(solution)/shard_map/ppermute | solution.py:343
  23.1 12.2 %collective-permute-start.8 = (f32[512,128]{1,0:T(8,128)S(1)}, f32[512,128]{1,0:T(8,128)S(1)}, u32[]{:S(2)}, u32[]{:S(2)}) collective-permute-start(f32[512,128]{1,0:T(8,128)S(1)} %get-tuple-element.27), channel_id=1, source_target_pairs={{0,4},{1,5},{2,6},{3,7},{4,0},{5,1},{6,2},{7,3},{8,12},{9,13},{10,... | collective-permute-start | bytes 786440 | tf_op jit(solution)/shard_map/ppermute | solution.py:343
  24.8 10.5 %collective-permute-start.9 = (f32[512,128]{1,0:T(8,128)S(1)}, f32[512,128]{1,0:T(8,128)S(1)}, u32[]{:S(2)}, u32[]{:S(2)}) collective-permute-start(f32[512,128]{1,0:T(8,128)S(1)} %get-tuple-element.28), channel_id=1, source_target_pairs={{0,2},{1,3},{2,0},{3,1},{4,6},{5,7},{6,4},{7,5},{8,10},{9,11},{10,... | collective-permute-start | bytes 786440 | tf_op jit(solution)/shard_map/ppermute | solution.py:343
  36.3 1.3 %collective-permute-start.11 = (f32[80,256]{1,0:T(8,128)S(1)}, f32[80,256]{1,0:T(8,128)S(1)}, u32[]{:S(2)}, u32[]{:S(2)}) collective-permute-start(f32[80,256]{1,0:T(8,128)S(1)} %slice_select_fusion), channel_id=1, source_target_pairs={{0,1},{1,0},{2,3},{3,2},{4,5},{5,4},{6,7},{7,6},{8,9},{9,8},{10,11... | collective-permute-start | bytes 245768 | tf_op jit(solution)/shard_map/ppermute | solution.py:368
  37.7 4.6 %collective-permute-start.12 = (f32[80,256]{1,0:T(8,128)S(1)}, f32[80,256]{1,0:T(8,128)S(1)}, u32[]{:S(2)}, u32[]{:S(2)}) collective-permute-start(f32[80,256]{1,0:T(8,128)S(1)} %select_add_fusion), channel_id=1, source_target_pairs={{0,2},{1,3},{2,0},{3,1},{4,6},{5,7},{6,4},{7,5},{8,10},{9,11},{10,... | collective-permute-start | bytes 245768 | tf_op jit(solution)/shard_map/ppermute | solution.py:369
  39.5 6.2 %collective-permute-start.13 = (f32[80,256]{1,0:T(8,128)S(1)}, f32[80,256]{1,0:T(8,128)S(1)}, u32[]{:S(2)}, u32[]{:S(2)}) collective-permute-start(f32[80,256]{1,0:T(8,128)S(1)} %select_add_fusion), channel_id=1, source_target_pairs={{0,4},{1,5},{2,6},{3,7},{4,0},{5,1},{6,2},{7,3},{8,12},{9,13},{10,... | collective-permute-start | bytes 245768 | tf_op jit(solution)/shard_map/ppermute | solution.py:369
  40.1 5.6 %collective-permute-start.14 = (f32[80,256]{1,0:T(8,128)S(1)}, f32[80,256]{1,0:T(8,128)S(1)}, u32[]{:S(2)}, u32[]{:S(2)}) collective-permute-start(f32[80,256]{1,0:T(8,128)S(1)} %select_add_fusion), channel_id=1, source_target_pairs={{0,6},{1,7},{2,4},{3,5},{4,2},{5,3},{6,0},{7,1},{8,14},{9,15},{10,... | collective-permute-start | bytes 245768 | tf_op jit(solution)/shard_map/ppermute | solution.py:369
  45.7 6.9 %collective-permute-start.15 = (f32[80,256]{1,0:T(8,128)S(1)}, f32[80,256]{1,0:T(8,128)S(1)}, u32[]{:S(2)}, u32[]{:S(2)}) collective-permute-start(f32[80,256]{1,0:T(8,128)S(1)} %add_add_fusion.1), channel_id=1, source_target_pairs={{0,24},{8,16},{16,8},{24,0},{1,25},{9,17},{17,9},{25,1},{2,26},{10... | collective-permute-start | bytes 245768 | tf_op jit(solution)/shard_map/ppermute | solution.py:370
  49.4 6.7 %collective-permute-start.16 = (f32[80,256]{1,0:T(8,128)S(1)}, f32[80,256]{1,0:T(8,128)S(1)}, u32[]{:S(2)}, u32[]{:S(2)}) collective-permute-start(f32[80,256]{1,0:T(8,128)S(1)} %add_add_fusion.1), channel_id=1, source_target_pairs={{0,16},{8,24},{16,0},{24,8},{1,17},{9,25},{17,1},{25,9},{2,18},{10... | collective-permute-start | bytes 245768 | tf_op jit(solution)/shard_map/ppermute | solution.py:370
  49.8 6.3 %collective-permute-start.17 = (f32[80,256]{1,0:T(8,128)S(1)}, f32[80,256]{1,0:T(8,128)S(1)}, u32[]{:S(2)}, u32[]{:S(2)}) collective-permute-start(f32[80,256]{1,0:T(8,128)S(1)} %add_add_fusion.1), channel_id=1, source_target_pairs={{0,8},{8,0},{16,24},{24,16},{1,9},{9,1},{17,25},{25,17},{2,10},{10... | collective-permute-start | bytes 245768 | tf_op jit(solution)/shard_map/ppermute | solution.py:370
  56.1 1.3 %collective-permute-start.18 = (f32[80,256]{1,0:T(8,128)S(1)}, f32[80,256]{1,0:T(8,128)S(1)}, u32[]{:S(2)}, u32[]{:S(2)}) collective-permute-start(f32[80,256]{1,0:T(8,128)S(1)} %add_add_fusion.half_ref), channel_id=1, source_target_pairs={{0,1},{1,0},{2,3},{3,2},{4,5},{5,4},{6,7},{7,6},{8,9},{9,8},{10,11... | collective-permute-start | bytes 245768 | tf_op jit(solution)/shard_map/ppermute | solution.py:371
